TPU v7x, 256 devices: a whole 4x4x8 slice. The times are simulated.
256 devices in a mesh: tm: 32 (over y, z_hi, x), head: 8 (over z_lo, core).
Axes of the slice: x: 4, y: 4, z: 8 (z_hi: 2, z_lo: 4; z = z_hi * 4 + z_lo), core: 2. Of those that a mesh axis runs over, the one named last changes fastest.
Arguments:
- clean_qkv: bfloat16 [3, 16384, 5120], P(None, 'tm', 'head'), may hold values from -140 to 140
- noise_qkv: bfloat16 [3, 16384, 5120], P(None, 'tm', 'head'), may hold values from -140 to 140
- timestep: int32 [32], P('tm'), may hold values from 1 to 999
- gain_q: float32 [5120], P('head'), may hold values from 0.1 to 1.9
- gain_k: float32 [5120], P('head'), may hold values from 0.1 to 1.9
- attended_grad: bfloat16 [16384, 5120], P('tm', 'head'), may hold values from -6 to 6
Outputs:
- attended: bfloat16 [16384, 5120], P('tm', 'head')
- clean_grads: float32 [3, 16384, 5120], P(None, 'tm', 'head')
All inputs are finite; a program needn't handle non-finite values.
Results may differ from a plain program's by a relative error of at most 0.012.
The roundings to bfloat16 on the way count: a program that leaves them out, or rounds other values in their place, can miss the bound.
Values may be sent and summed in bfloat16 or wider, within the bound.
No kernel may reach another device: no remote copies, remote signals or barrier semaphores. Data moves between devices by JAX's collectives and lax.ppermute only.
A program may use at most 128 MiB of HBM per device.

v0:
```python
import jax
import jax.numpy as jnp
from jax import lax
from jax.sharding import PartitionSpec as P

D = 5120
HEAD_DIM = 128
CONTEXT = 3


epsilon = 1e-06
masked_score = -1e30


def from_behind(block, axis, distance):
    devices = range(lax.axis_size(axis))
    route = [(i - distance, i) for i in devices if i - distance in devices]
    return lax.ppermute(block, axis, route)


def noise_share_of(timestep):
    level = timestep.astype(jnp.float32) / 1000.0
    return 5.0 * level / (1.0 + 4.0 * level)


def contract(left, right, left_dim, right_dim):
    return lax.dot_general(
        left, right, (((left_dim,), (right_dim,)), ((), ())), preferred_element_type=jnp.float32
    )


def on_device(clean_qkv, noise_qkv, timestep, gain_q, gain_k, attended_grad):
    row_count = clean_qkv.shape[1]
    local_width = clean_qkv.shape[2]
    heads_here = local_width // HEAD_DIM
    span_index = lax.axis_index("tm")
    noise_share = noise_share_of(timestep[0])
    keep_share = 1.0 - noise_share
    clean_field = clean_qkv.astype(jnp.float32)
    noisy_field = keep_share * clean_field + noise_share * noise_qkv.astype(jnp.float32)
    partial_sums = jnp.stack(
        [
            jnp.sum(noisy_field[0] * noisy_field[0], axis=-1),
            jnp.sum(noisy_field[1] * noisy_field[1], axis=-1),
            jnp.sum(clean_field[1] * clean_field[1], axis=-1),
        ]
    )
    totals = lax.psum(partial_sums, "head")
    inverse = lax.rsqrt(totals / D + epsilon)
    query_rows = (noisy_field[0] * inverse[0][:, None] * gain_q).astype(jnp.bfloat16)
    key_own = (noisy_field[1] * inverse[1][:, None] * gain_k).astype(jnp.bfloat16)
    key_clean = (clean_field[1] * inverse[2][:, None] * gain_k).astype(jnp.bfloat16)
    value_own = noisy_field[2].astype(jnp.bfloat16)
    value_clean = clean_qkv[2]
    outgoing = jnp.stack([key_clean, value_clean])
    arrived = []
    for hop_index in range(CONTEXT):
        arrived.append(from_behind(outgoing, "tm", hop_index + 1))
    key_rows = jnp.concatenate([key_own] + [piece[0] for piece in arrived], axis=0)
    value_rows = jnp.concatenate([value_own] + [piece[1] for piece in arrived], axis=0)
    block_ids = jnp.arange(CONTEXT + 1, dtype=jnp.int32)
    block_valid = span_index >= block_ids
    key_valid = jnp.repeat(block_valid, row_count)
    score_scale = HEAD_DIM ** (-0.5)
    key_count = (CONTEXT + 1) * row_count

    def one_head(head_index, carried_state):
        output_acc, query_acc, keys_acc, values_acc, stat_acc = carried_state
        head_start = head_index * HEAD_DIM
        query_head = lax.dynamic_slice_in_dim(query_rows, head_start, HEAD_DIM, 1)
        key_head = lax.dynamic_slice_in_dim(key_rows, head_start, HEAD_DIM, 1)
        value_head = lax.dynamic_slice_in_dim(value_rows, head_start, HEAD_DIM, 1)
        grad_head = lax.dynamic_slice_in_dim(attended_grad, head_start, HEAD_DIM, 1)
        scores = contract(query_head, key_head, 1, 1) * score_scale
        scores = jnp.where(key_valid[None, :], scores, masked_score)
        row_max = jnp.max(scores, axis=-1, keepdims=True)
        exponent = jnp.exp(scores - row_max)
        row_total = jnp.sum(exponent, axis=-1, keepdims=True)
        attention = exponent / row_total
        weights = attention.astype(jnp.bfloat16)
        output_head = jnp.dot(weights, value_head, preferred_element_type=jnp.float32)
        grad_probs = contract(grad_head, value_head, 1, 1)
        row_delta = jnp.sum(attention * grad_probs, axis=-1, keepdims=True)
        grad_scores = (attention * (grad_probs - row_delta) * score_scale).astype(jnp.bfloat16)
        grad_query_head = jnp.dot(grad_scores, key_head, preferred_element_type=jnp.float32)
        grad_key_head = contract(grad_scores, query_head, 0, 0)
        grad_value_head = contract(weights, grad_head, 0, 0)
        head_stats = jnp.stack([row_max[:, 0], row_total[:, 0], row_delta[:, 0]])[:, None, :]
        output_acc = lax.dynamic_update_slice_in_dim(output_acc, output_head, head_start, 1)
        query_acc = lax.dynamic_update_slice_in_dim(query_acc, grad_query_head, head_start, 1)
        keys_acc = lax.dynamic_update_slice_in_dim(keys_acc, grad_key_head, head_start, 1)
        values_acc = lax.dynamic_update_slice_in_dim(values_acc, grad_value_head, head_start, 1)
        stat_acc = lax.dynamic_update_slice_in_dim(stat_acc, head_stats, head_index, 1)
        return (output_acc, query_acc, keys_acc, values_acc, stat_acc)

    start_state = (
        jnp.zeros((row_count, local_width), jnp.float32),
        jnp.zeros((row_count, local_width), jnp.float32),
        jnp.zeros((key_count, local_width), jnp.float32),
        jnp.zeros((key_count, local_width), jnp.float32),
        jnp.zeros((3, heads_here, row_count), jnp.float32),
    )
    output_acc, grad_query, grad_keys, grad_values, row_stats = lax.fori_loop(
        0, heads_here, one_head, start_state
    )
    attended = output_acc.astype(jnp.bfloat16)
    returns_parts = []
    for hop_index in range(1, CONTEXT + 1):
        lower = hop_index * row_count
        returns_parts.append(
            jnp.stack(
                [grad_keys[lower : lower + row_count], grad_values[lower : lower + row_count]]
            )
        )
    context_grads = jnp.zeros_like(returns_parts[0])
    for hop_index in range(CONTEXT):
        context_grads = context_grads + from_behind(
            returns_parts[hop_index], "tm", -(hop_index + 1)
        )
    context_key_grad = context_grads[0]
    context_value_grad = context_grads[1]
    own_key_grad = grad_keys[:row_count]
    inner_sums = jnp.stack(
        [
            jnp.sum(noisy_field[0] * gain_q * grad_query, axis=-1),
            jnp.sum(noisy_field[1] * gain_k * own_key_grad, axis=-1),
            jnp.sum(clean_field[1] * gain_k * context_key_grad, axis=-1),
        ]
    )
    inner_totals = lax.psum(inner_sums, "head")
    cube_term = inverse**3 * inner_totals / D
    grad_query_pre = (
        inverse[0][:, None] * gain_q * grad_query - noisy_field[0] * cube_term[0][:, None]
    )
    grad_own_pre = (
        inverse[1][:, None] * gain_k * own_key_grad - noisy_field[1] * cube_term[1][:, None]
    )
    grad_clean_pre = (
        inverse[2][:, None] * gain_k * context_key_grad - clean_field[1] * cube_term[2][:, None]
    )
    clean_grads = jnp.stack(
        [
            keep_share * grad_query_pre,
            keep_share * grad_own_pre + grad_clean_pre,
            keep_share * grad_values[:row_count] + context_value_grad,
        ]
    )
    return (attended, clean_grads)


def solution(mesh):
    placed = (
        P(None, "tm", "head"),
        P(None, "tm", "head"),
        P("tm"),
        P("head"),
        P("head"),
        P("tm", "head"),
    )
    return jax.shard_map(
        on_device,
        mesh=mesh,
        in_specs=placed,
        out_specs=(P("tm", "head"), P(None, "tm", "head")),
        check_vma=False,
    )
```

profile of v0, /device:TPU:24, one launch (start us, length us, event | category | flops | bytes accessed | tf_op | source)
XLA Modules:
  0.0 739.9 jit_solution(1531797735895335018)
XLA Ops:
  0.6 3.9 convert_element_type.42
  5.3 2.2 multiply_add_fusion
  7.5 1.9 copy-done
  11.1 17.9 %psum.14 = f32[3,512]{1,0:T(4,128)S(1)} all-reduce(f32[3,512]{1,0:T(4,128)S(1)} %pad_maximum_fusion.7), channel_id=1, replica_groups=mesh['tm'=32,'head'=8] {'head'}, use_global_device_ids=true, to_apply=%region_3.0 | all-reduce | flops 1536 | bytes 12288 | tf_op jit(solution)/shard_map/psum | solution.py:48
  31.3 4.7 collective-permute-start.2
  36.0 6.7 collective-permute-start.1
  42.7 2.8 collective-permute-start
  47.8 2.0 multiply_convert_fusion.2
  49.8 45.1 %collective-permute-done.2 = bf16[2,512,640]{2,1,0:T(8,128)(2,1)} collective-permute-done((bf16[2,512,640]{2,1,0:T(8,128)(2,1)S(1)}, bf16[2,512,640]{2,1,0:T(8,128)(2,1)}, u32[]{:S(2)}, u32[]{:S(2)}) %collective-permute-start.2) | collective-permute-done | bytes 1310752 | tf_op jit(solution)/shard_map/ppermute | solution.py:18
  96.3 56.2 %collective-permute-done.1 = bf16[2,512,640]{2,1,0:T(8,128)(2,1)} collective-permute-done((bf16[2,512,640]{2,1,0:T(8,128)(2,1)S(1)}, bf16[2,512,640]{2,1,0:T(8,128)(2,1)}, u32[]{:S(2)}, u32[]{:S(2)}) %collective-permute-start.1) | collective-permute-done | bytes 1310752 | tf_op jit(solution)/shard_map/ppermute | solution.py:18
  153.9 54.8 %collective-permute-done = bf16[2,512,640]{2,1,0:T(8,128)(2,1)} collective-permute-done((bf16[2,512,640]{2,1,0:T(8,128)(2,1)S(1)}, bf16[2,512,640]{2,1,0:T(8,128)(2,1)}, u32[]{:S(2)}, u32[]{:S(2)}) %collective-permute-start) | collective-permute-done | bytes 1310752 | tf_op jit(solution)/shard_map/ppermute | solution.py:18
  210.1 8.9 %pad_maximum_fusion.1 = (bf16[2048,640]{1,0:T(8,128)(2,1)S(1)}, bf16[2048,640]{1,0:T(8,128)(2,1)}) fusion(bf16[512,640]{1,0:T(8,128)(2,1)S(1)} %get-tuple-element.246, bf16[512,640]{1,0:T(8,128)(2,1)S(1)} %get-tuple-element.244, bf16[512,640]{1,0:T(8,128)(2,1)S(1)} %get-tuple-element.242, bf16[512,640]{1,0:T(8,128)(2,1)S(1)} %get-tuple-element.238, ...), kind=kLoop, calls=%fused_computation.33 | loop fusion | flops 20971520 | bytes 10485760 | tf_op jit(solution)/shard_map/concatenate | solution.py:59
  220.2 2.7 broadcast.33.clone
  222.9 2.6 broadcast.33
  225.5 78.2 %while.20 = (s32[]{:T(128)}, bf16[512,640]{1,0:T(8,128)(2,1)}, f32[512,640]{1,0:T(8,128)}, f32[2048,640]{1,0:T(8,128)}, f32[2048,640]{1,0:T(8,128)}, /*index=5*/...) while((s32[]{:T(128)}, bf16[512,640]{1,0:T(8,128)(2,1)}, ...), condition=%wide.region_8.9_spmd.clone, body=%wide.region_4.8_spmd.clone.sunk | while | flops 1643117056 | bytes 45140152 | solution.py:103
  227.4 2.8 convolution_dynamic-update-slice_fusion.8
  230.2 2.5 multiply_reduce_fusion.6
  232.8 1.7 multiply_convert_fusion.5
  234.5 3.3 convolution_dynamic-update-slice_fusion.11
  239.3 1.8 convolution_dynamic-update-slice_fusion.10
  242.9 2.8 convolution_dynamic-update-slice_fusion.8
  245.8 2.6 multiply_reduce_fusion.6
  250.0 3.4 convolution_dynamic-update-slice_fusion.11
  254.9 1.9 convolution_dynamic-update-slice_fusion.10
  258.6 2.8 convolution_dynamic-update-slice_fusion.8
  261.5 2.6 multiply_reduce_fusion.6
  265.7 3.4 convolution_dynamic-update-slice_fusion.11
  270.6 1.9 convolution_dynamic-update-slice_fusion.10
  274.3 2.8 convolution_dynamic-update-slice_fusion.8
  277.2 2.5 multiply_reduce_fusion.6
  279.7 1.7 multiply_convert_fusion.5
  281.4 3.4 convolution_dynamic-update-slice_fusion.11
  286.3 1.8 convolution_dynamic-update-slice_fusion.10
  290.0 2.8 convolution_dynamic-update-slice_fusion.8
  292.8 2.6 multiply_reduce_fusion.6
  297.1 3.4 convolution_dynamic-update-slice_fusion.11
  302.0 1.8 convolution_dynamic-update-slice_fusion.10
  303.7 2.5 slice_bitcast_fusion.6
  307.8 1.9 collective-permute-start.5
  309.9 7.2 collective-permute-start.3
  317.3 2.3 collective-permute-start.4
  319.6 106.1 %collective-permute-done.5 = f32[2,512,640]{2,1,0:T(8,128)S(1)} collective-permute-done((f32[2,512,640]{2,1,0:T(8,128)S(1)}, f32[2,512,640]{2,1,0:T(8,128)S(1)}, u32[]{:S(2)}, u32[]{:S(2)}) %collective-permute-start.5) | collective-permute-done | bytes 2621472 | tf_op jit(solution)/shard_map/ppermute | solution.py:18
  425.7 90.5 %collective-permute-done.3 = f32[2,512,640]{2,1,0:T(8,128)S(1)} collective-permute-done((f32[2,512,640]{2,1,0:T(8,128)S(1)}, f32[2,512,640]{2,1,0:T(8,128)S(1)}, u32[]{:S(2)}, u32[]{:S(2)}) %collective-permute-start.3) | collective-permute-done | bytes 2621472 | tf_op jit(solution)/shard_map/ppermute | solution.py:18
  516.2 201.6 %collective-permute-done.4 = f32[2,512,640]{2,1,0:T(8,128)S(1)} collective-permute-done((f32[2,512,640]{2,1,0:T(8,128)S(1)}, f32[2,512,640]{2,1,0:T(8,128)S(1)}, u32[]{:S(2)}, u32[]{:S(2)}) %collective-permute-start.4) | collective-permute-done | bytes 2621472 | tf_op jit(solution)/shard_map/ppermute | solution.py:18
  718.1 1.8 multiply_reduce_fusion.2
  719.9 13.9 %psum.15 = f32[3,512]{1,0:T(4,128)S(1)} all-reduce(f32[3,512]{1,0:T(4,128)S(1)} %pad_maximum_fusion.8), channel_id=1, replica_groups=mesh['tm'=32,'head'=8] {'head'}, use_global_device_ids=true, to_apply=%region_12.13 | all-reduce | flops 1536 | bytes 12288 | tf_op jit(solution)/shard_map/psum | solution.py:130
  733.9 3.8 multiply_bitcast_fusion
  737.8 2.2 pad_maximum_fusion
  (81 shorter events, 35.7 us)
Async XLA Ops:
  0.6 4.6 copy-start.4
  7.5 1.9 copy-start
  9.4 20.3 %copy-start.7 = (f32[640]{0:T(1024)S(1)}, f32[640]{0:T(1024)}, u32[]{:S(2)}) copy-start(f32[640]{0:T(1024)} %param.12) | copy-start | bytes 7684
  9.4 21.8 %slice-start = ((bf16[3,512,640]{2,1,0:T(8,128)(2,1)}), bf16[1,512,640]{2,1,0:T(8,128)(2,1)S(1)}, s32[]{:S(2)}) async-start(bf16[3,512,640]{2,1,0:T(8,128)(2,1)} %param.8), calls=%async_computation | async-start | bytes 1310720 | tf_op jit(solution)/shard_map/slice | solution.py:54
  29.0 0.6 copy-start.5
  29.1 0.6 copy-start.11
  29.1 18.7 %copy-start.9 = (f32[1,512]{1,0:T(1,128)}, f32[1,512]{1,0:T(1,128)S(1)}, u32[]{:S(2)}) copy-start(f32[1,512]{1,0:T(1,128)S(1)} %get-tuple-element.250) | copy-start | bytes 6148
  29.1 18.7 %copy-start.13 = (f32[1,512]{1,0:T(1,128)}, f32[1,512]{1,0:T(1,128)S(1)}, u32[]{:S(2)}) copy-start(f32[1,512]{1,0:T(1,128)S(1)} %get-tuple-element.252) | copy-start | bytes 6148
  31.2 16.6 %copy-start.8 = (f32[640]{0:T(1024)S(1)}, f32[640]{0:T(1024)}, u32[]{:S(2)}) copy-start(f32[640]{0:T(1024)} %param.11) | copy-start | bytes 7684
  31.3 63.6 %collective-permute-start.2 = (bf16[2,512,640]{2,1,0:T(8,128)(2,1)S(1)}, bf16[2,512,640]{2,1,0:T(8,128)(2,1)}, u32[]{:S(2)}, u32[]{:S(2)}) collective-permute-start(bf16[2,512,640]{2,1,0:T(8,128)(2,1)S(1)} %pad_maximum_fusion.6), channel_id=1, source_target_pairs={{0,24},{8,32},{16,40},{24,48},{32,56},{40,64},{48,72},{56,80},{64,... | collective-permute-start | bytes 3932168 | tf_op jit(solution)/shard_map/ppermute | solution.py:18
  36.0 116.5 %collective-permute-start.1 = (bf16[2,512,640]{2,1,0:T(8,128)(2,1)S(1)}, bf16[2,512,640]{2,1,0:T(8,128)(2,1)}, u32[]{:S(2)}, u32[]{:S(2)}) collective-permute-start(bf16[2,512,640]{2,1,0:T(8,128)(2,1)S(1)} %pad_maximum_fusion.6), channel_id=1, source_target_pairs={{0,16},{8,24},{16,32},{24,40},{32,48},{40,56},{48,64},{56,72},{64,... | collective-permute-start | bytes 3932168 | tf_op jit(solution)/shard_map/ppermute | solution.py:18
  42.7 166.0 %collective-permute-start = (bf16[2,512,640]{2,1,0:T(8,128)(2,1)S(1)}, bf16[2,512,640]{2,1,0:T(8,128)(2,1)}, u32[]{:S(2)}, u32[]{:S(2)}) collective-permute-start(bf16[2,512,640]{2,1,0:T(8,128)(2,1)S(1)} %pad_maximum_fusion.6), channel_id=1, source_target_pairs={{0,8},{8,16},{16,24},{24,32},{32,40},{40,48},{48,56},{56,64},{64,7... | collective-permute-start | bytes 3932168 | tf_op jit(solution)/shard_map/ppermute | solution.py:18
  303.7 3.7 copy-start.2
  307.8 117.9 %collective-permute-start.5 = (f32[2,512,640]{2,1,0:T(8,128)S(1)}, f32[2,512,640]{2,1,0:T(8,128)S(1)}, u32[]{:S(2)}, u32[]{:S(2)}) collective-permute-start(f32[2,512,640]{2,1,0:T(8,128)S(1)} %pad_maximum_fusion.5), channel_id=1, source_target_pairs={{24,0},{32,8},{40,16},{48,24},{56,32},{64,40},{72,48},{80,56},{88,... | collective-permute-start | bytes 7864328 | tf_op jit(solution)/shard_map/ppermute | solution.py:18
  309.9 206.2 %collective-permute-start.3 = (f32[2,512,640]{2,1,0:T(8,128)S(1)}, f32[2,512,640]{2,1,0:T(8,128)S(1)}, u32[]{:S(2)}, u32[]{:S(2)}) collective-permute-start(f32[2,512,640]{2,1,0:T(8,128)S(1)} %pad_maximum_fusion.3), channel_id=1, source_target_pairs={{8,0},{16,8},{24,16},{32,24},{40,32},{48,40},{56,48},{64,56},{72,6... | collective-permute-start | bytes 7864328 | tf_op jit(solution)/shard_map/ppermute | solution.py:18
  317.3 400.8 %copy-start.1 = (f32[3,512,640]{2,1,0:T(8,128)S(1)}, f32[3,512,640]{2,1,0:T(8,128)}, u32[]{:S(2)}) copy-start(f32[3,512,640]{2,1,0:T(8,128)} %copy-done) | copy-start | bytes 11796484
  317.3 400.8 %copy-start.3 = (f32[512,640]{1,0:T(8,128)S(1)}, f32[512,640]{1,0:T(8,128)}, u32[]{:S(2)}) copy-start(f32[512,640]{1,0:T(8,128)} %get-tuple-element.175) | copy-start | bytes 3932164
  317.3 400.4 %collective-permute-start.4 = (f32[2,512,640]{2,1,0:T(8,128)S(1)}, f32[2,512,640]{2,1,0:T(8,128)S(1)}, u32[]{:S(2)}, u32[]{:S(2)}) collective-permute-start(f32[2,512,640]{2,1,0:T(8,128)S(1)} %pad_maximum_fusion.4), channel_id=1, source_target_pairs={{16,0},{24,8},{32,16},{40,24},{48,32},{56,40},{64,48},{72,56},{80,... | collective-permute-start | bytes 7864328 | tf_op jit(solution)/shard_map/ppermute | solution.py:18
  718.1 15.8 %copy-start.6 = (f32[3,512]{1,0:T(4,128)S(1)}, f32[3,512]{1,0:T(4,128)}, u32[]{:S(2)}) copy-start(f32[3,512]{1,0:T(4,128)} %copy-done.5) | copy-start | bytes 18436
  718.1 15.8 %copy-start.10 = (f32[1,512]{1,0:T(1,128)S(1)}, f32[1,512]{1,0:T(1,128)}, u32[]{:S(2)}) copy-start(f32[1,512]{1,0:T(1,128)} %copy-done.9) | copy-start | bytes 6148
  718.1 15.8 %copy-start.12 = (f32[1,512]{1,0:T(1,128)S(1)}, f32[1,512]{1,0:T(1,128)}, u32[]{:S(2)}) copy-start(f32[1,512]{1,0:T(1,128)} %copy-done.11) | copy-start | bytes 6148
  718.1 15.8 %copy-start.14 = (f32[1,512]{1,0:T(1,128)S(1)}, f32[1,512]{1,0:T(1,128)}, u32[]{:S(2)}) copy-start(f32[1,512]{1,0:T(1,128)} %copy-done.13) | copy-start | bytes 6148
where the time goes:
time: 741 us; the launch traced here: 740 us
  waiting for transfers between devices  554 us (75%)
  matrix products  64.6 us (9%)
  other arithmetic  43.2 us (6%)
  blocking collectives  31.8 us (4%)
  starting transfers between devices  25.5 us (3%)
  local copies, waits for them, and re-layouts  18.9 us (3%)
    ppermute x6, waiting for transfers between devices, from_behind(): return lax.ppermute(block, axis, route)  554 us
    dot_general x20, matrix products, contract(): lax.dot_general(left, right, (((left_dim,), (right_dim,)), ((), ())), pre...  43 us
    ppermute x6, starting transfers between devices, from_behind(): return lax.ppermute(block, axis, route)  25.5 us
    psum x1, blocking collectives, on_device(): totals = lax.psum(partial_sums, 'head')  17.9 us
  transfers between devices with their start and end apart: 6, of which 6 were waited for; matrix products, arithmetic and copies ran while one was open for 1% of the time, Pallas kernels for 0%

commit v1 on v0

v1 whole, which is shorter than its diff:
```python
import math

import jax
import jax.numpy as jnp
from jax import lax
from jax.experimental import pallas as pl
from jax.experimental.pallas import tpu as pltpu
from jax.sharding import PartitionSpec as P

D = 5120
HEAD_DIM = 128
CONTEXT = 3
COLUMNS = 4
HEAD_CHUNKS = (2, 2, 1)
KEY_TILE = 256

epsilon = 1e-06
masked_score = -1e30
NT = (((1,), (1,)), ((), ()))
NN = (((1,), (0,)), ((), ()))


def dot(left, right, dims):
    return lax.dot_general(left, right, dims, preferred_element_type=jnp.float32)


def noise_share_of(timestep):
    level = timestep.astype(jnp.float32) / 1000.0
    return 5.0 * level / (1.0 + 4.0 * level)


def shift_spans(block, distance, columns=range(COLUMNS)):
    count = lax.axis_size("tm")
    route = [
        (i, i + distance)
        for i in range(count)
        if 0 <= i + distance < count and i % COLUMNS in columns
    ]
    return lax.ppermute(block, "tm", route)


def shift_columns(block, distance, kind):
    count = lax.axis_size("tm")
    route = []
    for i in range(count):
        row, column = divmod(i, COLUMNS)
        target = column + distance
        inside = 0 <= target < COLUMNS
        if kind == "both" or inside == (kind == "inside"):
            route.append((i, row * COLUMNS + target % COLUMNS))
    return lax.ppermute(block, "tm", route)


def attention_body(
    flags, cols, gain, query, key_own, value_own, grad,
    own_1, own_2, own_3, wrap_1, wrap_2, wrap_3, *refs
):
    (attended, grad_query, grad_key, grad_value, back_1, back_2, back_3, inner,
     exps, probs, keys, values) = refs[-12:]
    rows = query.shape[0]
    scale = HEAD_DIM**-0.5
    exponent_scale = scale * math.log2(math.e)
    gains = gain[...]
    sources = ((own_1, wrap_1), (own_2, wrap_2), (own_3, wrap_3))
    backs = (back_1, back_2, back_3)

    @pl.when(pl.program_id(0) == 0)
    def _():
        inner[...] = jnp.zeros_like(inner)

    keys[0:rows] = key_own[...]
    values[0:rows] = value_own[...]
    for hop, (own, wrap) in enumerate(sources):
        inside = flags[hop] > 0
        block = pl.ds((hop + 1) * rows, rows)
        raw = jnp.where(inside, own[0], wrap[0]).astype(jnp.float32)
        keys[block] = (raw * cols[:, hop : hop + 1] * gains).astype(jnp.bfloat16)
        values[block] = jnp.where(inside, own[1], wrap[1])
    queries = query[...]
    grads = grad[...]
    tiles = rows // KEY_TILE

    row_max = None
    for block in range(CONTEXT + 1):
        block_max = None
        for tile in range(tiles):
            part = pl.ds(block * rows + tile * KEY_TILE, KEY_TILE)
            scores = dot(keys[part], queries, NT)
            exps[part] = scores
            tile_max = jnp.max(scores, axis=0, keepdims=True)
            block_max = tile_max if block_max is None else jnp.maximum(block_max, tile_max)
        if block > 0:
            block_max = jnp.where(flags[2 + block] > 0, block_max, masked_score)
        row_max = block_max if row_max is None else jnp.maximum(row_max, block_max)
    offset = row_max * exponent_scale
    total = jnp.zeros((1, rows), jnp.float32)
    delta = jnp.zeros((1, rows), jnp.float32)
    for block in range(CONTEXT + 1):
        block_offset = offset
        if block > 0:
            block_offset = jnp.where(flags[2 + block] > 0, offset, -masked_score)
        for tile in range(tiles):
            part = pl.ds(block * rows + tile * KEY_TILE, KEY_TILE)
            exponent = jnp.exp2(exps[part] * exponent_scale - block_offset)
            grad_probs = dot(values[part], grads, NT)
            exps[part] = exponent
            probs[part] = grad_probs
            total = total + jnp.sum(exponent, axis=0, keepdims=True)
            delta = delta + jnp.sum(exponent * grad_probs, axis=0, keepdims=True)
    inverse_total = 1.0 / total
    delta = delta * inverse_total
    output = jnp.zeros((HEAD_DIM, rows), jnp.float32)
    query_grad = jnp.zeros((HEAD_DIM, rows), jnp.float32)
    lane = lax.broadcasted_iota(jnp.int32, (KEY_TILE, 8), 1)
    for block in range(CONTEXT + 1):
        for tile in range(tiles):
            part = pl.ds(block * rows + tile * KEY_TILE, KEY_TILE)
            here = pl.ds(tile * KEY_TILE, KEY_TILE)
            attention = exps[part] * inverse_total
            weights = attention.astype(jnp.bfloat16)
            grad_scores = (attention * (probs[part] - delta) * scale).astype(jnp.bfloat16)
            output = output + dot(values[part].T, weights, NN)
            query_grad = query_grad + dot(keys[part].T, grad_scores, NN)
            value_part = dot(weights, grads, NN)
            key_part = dot(grad_scores, queries, NN)
            if block == 0:
                grad_key[here] = key_part
                grad_value[here] = value_part
            else:
                back = backs[block - 1]
                back[0, here] = key_part.astype(jnp.bfloat16)
                back[1, here] = value_part.astype(jnp.bfloat16)
                own, wrap = sources[block - 1]
                raw = jnp.where(flags[block - 1] > 0, own[0, here], wrap[0, here])
                product = raw.astype(jnp.float32) * gains * key_part
                inner[here] += jnp.where(
                    lane == block - 1, jnp.sum(product, axis=1, keepdims=True), 0.0
                )
    attended[...] = output.T.astype(jnp.bfloat16)
    grad_query[...] = query_grad.T


def attention_chunk(first, heads, flags, cols, gain, rows_in, own, wrap, previous):
    rows, width = rows_in[0].shape
    here = lambda h: (0, first + h)
    f32, bf16 = jnp.float32, jnp.bfloat16
    wide = pl.BlockSpec((rows, HEAD_DIM), here)
    wide_pair = pl.BlockSpec((2, rows, HEAD_DIM), lambda h: (0, 0, first + h))
    pair = pl.BlockSpec((2, rows, HEAD_DIM), lambda h: (0, 0, h))
    in_specs = (
        [
            pl.BlockSpec(memory_space=pltpu.SMEM),
            pl.BlockSpec(cols.shape, lambda h: (0, 0)),
            pl.BlockSpec((1, HEAD_DIM), here),
        ]
        + [wide] * 4
        + [wide_pair] * 3
        + [pair] * 3
    )
    operands = [flags, cols, gain, *rows_in, *own, *wrap]
    aliases = {}
    for position, array in enumerate(previous):
        aliases[len(operands)] = position
        operands.append(array)
        in_specs.append(pl.BlockSpec(memory_space=pl.ANY))
    back = jax.ShapeDtypeStruct((2, rows, heads * HEAD_DIM), bf16)
    keys = (CONTEXT + 1) * rows
    flops = 6 * 2 * rows * keys * HEAD_DIM * heads
    return pl.pallas_call(
        attention_body,
        grid=(heads,),
        in_specs=in_specs,
        out_specs=[wide] * 4 + [pair] * 3 + [pl.BlockSpec((rows, 8), lambda h: (0, 0))],
        out_shape=[
            jax.ShapeDtypeStruct((rows, width), bf16),
            jax.ShapeDtypeStruct((rows, width), f32),
            jax.ShapeDtypeStruct((rows, width), f32),
            jax.ShapeDtypeStruct((rows, width), f32),
            back,
            back,
            back,
            jax.ShapeDtypeStruct((rows, 8), f32),
        ],
        scratch_shapes=[
            pltpu.VMEM((keys, rows), f32),
            pltpu.VMEM((keys, rows), f32),
            pltpu.VMEM((keys, HEAD_DIM), bf16),
            pltpu.VMEM((keys, HEAD_DIM), bf16),
        ],
        input_output_aliases=aliases,
        compiler_params=pltpu.CompilerParams(
            dimension_semantics=("arbitrary",), vmem_limit_bytes=40 * 2**20
        ),
        cost_estimate=pl.CostEstimate(
            flops=flops, bytes_accessed=heads * 4 * 2**20, transcendentals=rows * keys * heads
        ),
    )(*operands)


def finish_body(
    flags, keep_ref, cols, gain_q, gain_k, clean, noise, grad_query, grad_key, grad_value,
    in_1, in_2, in_3, crossed, *refs
):
    out = refs[-1]
    keep = keep_ref[0]
    share = keep_ref[1]
    f32 = jnp.float32
    clean_key = clean[1].astype(f32)
    noisy_query = keep * clean[0].astype(f32) + share * noise[0].astype(f32)
    noisy_key = keep * clean_key + share * noise[1].astype(f32)
    key_grad = crossed[0].astype(f32)
    value_grad = crossed[1].astype(f32)
    for hop, received in enumerate((in_1, in_2, in_3)):
        inside = flags[6 + hop] > 0
        key_grad = key_grad + jnp.where(inside, received[0], 0).astype(f32)
        value_grad = value_grad + jnp.where(inside, received[1], 0).astype(f32)
    col = lambda i: cols[:, i : i + 1]
    gk = gain_k[...]
    out[0] = keep * (col(0) * gain_q[...] * grad_query[...] - noisy_query * col(3))
    own = col(1) * gk * grad_key[...] - noisy_key * col(4)
    out[1] = keep * own + (col(2) * gk * key_grad - clean_key * col(5))
    out[2] = keep * grad_value[...] + value_grad


def finish_chunk(first, heads, flags, keep, cols, gains, fields, grads, received, crossed, previous):
    _, rows, width = fields[0].shape
    here = lambda h: (0, first + h)
    wide = pl.BlockSpec((rows, HEAD_DIM), here)
    gain_spec = pl.BlockSpec((1, HEAD_DIM), here)
    two = pl.BlockSpec((2, rows, HEAD_DIM), lambda h: (0, 0, first + h))
    pair = pl.BlockSpec((2, rows, HEAD_DIM), lambda h: (0, 0, h))
    smem = pl.BlockSpec(memory_space=pltpu.SMEM)
    operands = [flags, keep, cols, *gains, *fields, *grads, *received, crossed]
    in_specs = (
        [smem, smem, pl.BlockSpec(cols.shape, lambda h: (0, 0))]
        + [gain_spec] * 2
        + [two] * 2
        + [wide] * 3
        + [pair] * 4
    )
    aliases = {}
    if previous is not None:
        aliases[len(operands)] = 0
        operands.append(previous)
        in_specs.append(pl.BlockSpec(memory_space=pl.ANY))
    return pl.pallas_call(
        finish_body,
        grid=(heads,),
        in_specs=in_specs,
        out_specs=pl.BlockSpec((3, rows, HEAD_DIM), lambda h: (0, 0, first + h)),
        out_shape=jax.ShapeDtypeStruct((3, rows, width), jnp.float32),
        input_output_aliases=aliases,
        compiler_params=pltpu.CompilerParams(dimension_semantics=("arbitrary",)),
        cost_estimate=pl.CostEstimate(
            flops=rows * HEAD_DIM * heads * 30,
            bytes_accessed=heads * rows * HEAD_DIM * 48,
            transcendentals=0,
        ),
    )(*operands)


def on_device(clean_qkv, noise_qkv, timestep, gain_q, gain_k, attended_grad):
    f32, bf16 = jnp.float32, jnp.bfloat16
    span = lax.axis_index("tm")
    column = span % COLUMNS
    chunks = []
    first = 0
    for heads in HEAD_CHUNKS:
        chunks.append((first, heads))
        first += heads

    def lanes(first, heads):
        return slice(first * HEAD_DIM, (first + heads) * HEAD_DIM)

    context = clean_qkv[1:3]
    crossing = []
    own = None
    for first, heads in chunks:
        crossing.append(
            shift_spans(context[:, :, lanes(first, heads)], COLUMNS, range(1, COLUMNS))
        )
        if own is None:
            own = [shift_columns(context, hop, "inside") for hop in range(1, CONTEXT + 1)]

    noise_share = noise_share_of(timestep[0])
    keep_share = 1.0 - noise_share
    clean_field = clean_qkv.astype(f32)
    noisy_field = keep_share * clean_field + noise_share * noise_qkv.astype(f32)
    squares = jnp.stack(
        [
            jnp.sum(noisy_field[0] * noisy_field[0], axis=-1),
            jnp.sum(noisy_field[1] * noisy_field[1], axis=-1),
            jnp.sum(clean_field[1] * clean_field[1], axis=-1),
        ]
    )
    inverse = lax.rsqrt(lax.psum(squares, "head") / D + epsilon)
    context_inverse = [shift_spans(inverse[2], hop) for hop in range(1, CONTEXT + 1)]
    query_rows = (noisy_field[0] * inverse[0][:, None] * gain_q).astype(bf16)
    key_own = (noisy_field[1] * inverse[1][:, None] * gain_k).astype(bf16)
    value_own = noisy_field[2].astype(bf16)
    rows_in = [query_rows, key_own, value_own, attended_grad]
    inverse_cols = jnp.stack(context_inverse + [jnp.zeros_like(inverse[2])] * 5).T

    hops = jnp.arange(1, CONTEXT + 1, dtype=jnp.int32)
    flags = jnp.concatenate([column >= hops, span >= hops, column + hops < COLUMNS]).astype(
        jnp.int32
    )
    gain_rows = (gain_q[None, :], gain_k[None, :])

    results = ()
    inner = 0.0
    received = []
    crossed = []
    for (first, heads), cross in zip(chunks, crossing):
        wrap = [shift_columns(cross, hop, "wrapped") for hop in range(1, CONTEXT + 1)]
        out = attention_chunk(
            first, heads, flags, inverse_cols, gain_rows[1], rows_in, own, wrap, results
        )
        results = out[:4]
        inner = inner + out[7]
        back = [shift_columns(out[4 + hop], -(hop + 1), "both") for hop in range(CONTEXT)]
        forward = jnp.zeros(back[0].shape, f32)
        for hop in range(CONTEXT):
            forward = forward + jnp.where(column + hop + 1 >= COLUMNS, back[hop], 0).astype(f32)
        received.append(back)
        crossed.append(shift_spans(forward.astype(bf16), -COLUMNS, range(1, COLUMNS)))
    attended, grad_query, grad_key, grad_value = results

    sums = jnp.stack(
        [
            jnp.sum(noisy_field[0] * gain_q * grad_query, axis=-1),
            jnp.sum(noisy_field[1] * gain_k * grad_key, axis=-1),
        ]
        + [inner[:, hop] for hop in range(CONTEXT)]
    )
    totals = lax.psum(sums, "head") / D
    clean_inner = sum(shift_spans(totals[2 + hop], -(hop + 1)) for hop in range(CONTEXT))
    cubes = inverse**3 * jnp.stack([totals[0], totals[1], clean_inner])
    finish_cols = jnp.concatenate([inverse, cubes, jnp.zeros_like(inverse[:2])]).T
    keep = jnp.stack([keep_share, noise_share])
    clean_grads = None
    for (first, heads), back, cross in zip(chunks, received, crossed):
        clean_grads = finish_chunk(
            first, heads, flags, keep, finish_cols, gain_rows, (clean_qkv, noise_qkv),
            (grad_query, grad_key, grad_value), back, cross, clean_grads,
        )
    return (attended, clean_grads)


def solution(mesh):
    placed = (
        P(None, "tm", "head"),
        P(None, "tm", "head"),
        P("tm"),
        P("head"),
        P("head"),
        P("tm", "head"),
    )
    return jax.shard_map(
        on_device,
        mesh=mesh,
        in_specs=placed,
        out_specs=(P("tm", "head"), P(None, "tm", "head")),
        check_vma=False,
    )
```

time: 741 us -> 354 us (0.48)
  the two profiles are of different devices: /device:TPU:24 before, /device:TPU:26 now
where the time goes in v1:
time: 354 us; the launch traced here: 353 us
  starting transfers between devices  105 us (30%)
  waiting for transfers between devices  87.6 us (25%)
  blocking collectives  81.4 us (23%)
  Pallas kernels  41.9 us (12%)
  local copies, waits for them, and re-layouts  25.1 us (7%)
  other arithmetic  9.77 us (3%)
    ppermute x12, starting transfers between devices, shift_spans(): return lax.ppermute(block, 'tm', route)  54.8 us
    ppermute x12, waiting for transfers between devices, shift_spans(): return lax.ppermute(block, 'tm', route)  54.8 us
    psum x1, blocking collectives, on_device(): inverse = lax.rsqrt(lax.psum(squares, 'head') / D + epsilon)  54.4 us
    ppermute x21, starting transfers between devices, shift_columns(): return lax.ppermute(block, 'tm', route)  50.2 us
    ppermute x21, waiting for transfers between devices, shift_columns(): return lax.ppermute(block, 'tm', route)  32.8 us
    pallas_call x3, Pallas kernels, attention_chunk(): pl.pallas_call(attention_body, grid=(heads,), in_specs=in_specs, out_spec...  30.1 us
    psum x1, blocking collectives, on_device(): totals = lax.psum(sums, 'head') / D  27 us
    unnamed x92, local copies, waits for them, and re-layouts  16.6 us
  transfers between devices with their start and end apart: 33, of which 9 were waited for; matrix products, arithmetic and copies ran while one was open for 4% of the time, Pallas kernels for 9%

profile of v1, /device:TPU:26, one launch (start us, length us, event | category | flops | bytes accessed | tf_op | source)
XLA Modules:
  0.0 353.0 jit_solution(7937290901100932688)
XLA Ops:
  0.6 2.6 slice.76
  3.3 3.4 collective-permute-start.3
  6.7 9.1 %collective-permute-start.6 = (bf16[2,512,128]{2,1,0:T(8,128)(2,1)S(1)}, bf16[2,512,128]{2,1,0:T(8,128)(2,1)}, u32[]{:S(2)}, u32[]{:S(2)}) collective-permute-start(bf16[2,512,128]{2,1,0:T(8,128)(2,1)S(1)} %slice.77), channel_id=1, source_target_pairs={{8,40},{16,48},{24,56},{40,72},{48,80},{56,88},{72,104},{80,112},{... | collective-permute-start | bytes 786440 | tf_op jit(solution)/shard_map/ppermute | solution.py:39
  16.8 1.9 collective-permute-start.10
  18.8 1.9 collective-permute-start.14
  21.8 2.2 multiply_add_fusion
  24.0 1.9 copy-done.23
  26.2 54.4 %psum.14 = f32[3,512]{1,0:T(4,128)S(1)} all-reduce(f32[3,512]{1,0:T(4,128)S(1)} %pad_maximum_fusion), channel_id=1, replica_groups=mesh['tm'=32,'head'=8] {'head'}, use_global_device_ids=true, to_apply=%region_3.4 | all-reduce | flops 1536 | bytes 12288 | tf_op jit(solution)/shard_map/psum | solution.py:296
  81.3 3.1 collective-permute-start
  84.5 2.4 collective-permute-done
  86.8 2.8 collective-permute-start.1
  89.6 9.8 %collective-permute-done.1 = f32[512]{0:T(512)S(1)} collective-permute-done((f32[512]{0:T(512)S(1)}, f32[512]{0:T(512)S(1)}, u32[]{:S(2)}, u32[]{:S(2)}) %collective-permute-start.1) | collective-permute-done | bytes 2080 | tf_op jit(solution)/shard_map/ppermute | solution.py:39
  99.5 5.9 %collective-permute-start.2 = (f32[512]{0:T(512)S(1)}, f32[512]{0:T(512)S(1)}, u32[]{:S(2)}, u32[]{:S(2)}) collective-permute-start(f32[512]{0:T(512)S(1)} %bitcast.63), channel_id=1, source_target_pairs={{0,24},{8,32},{16,40},{24,48},{32,56},{40,64},{48,72},{56,80},{64,... | collective-permute-start | bytes 6152 | tf_op jit(solution)/shard_map/ppermute | solution.py:39
  105.4 5.3 %collective-permute-done.2 = f32[512]{0:T(512)S(1)} collective-permute-done((f32[512]{0:T(512)S(1)}, f32[512]{0:T(512)S(1)}, u32[]{:S(2)}, u32[]{:S(2)}) %collective-permute-start.2) | collective-permute-done | bytes 2080 | tf_op jit(solution)/shard_map/ppermute | solution.py:39
  110.7 2.3 collective-permute-start.4
  113.0 1.8 collective-permute-start.5
  116.9 7.7 %collective-permute-start.17 = (bf16[2,512,256]{2,1,0:T(8,128)(2,1)}, bf16[2,512,256]{2,1,0:T(8,128)(2,1)S(1)}, u32[]{:S(2)}, u32[]{:S(2)}) collective-permute-start(bf16[2,512,256]{2,1,0:T(8,128)(2,1)} %collective-permute-done.14), channel_id=1, source_target_pairs={{8,0},{16,8},{24,16},{40,32},{48,40},{56,48},{72,64},{80,72},{88,8... | collective-permute-start | bytes 1572872 | tf_op jit(solution)/shard_map/ppermute | solution.py:51
  124.7 3.1 multiply_convert_fusion
  127.8 4.9 %collective-permute-done.16.wrap_2 = bf16[2,512,256]{2,1,0:T(8,128)(2,1)} collective-permute-done((bf16[2,512,256]{2,1,0:T(8,128)(2,1)}, bf16[2,512,256]{2,1,0:T(8,128)(2,1)}, u32[]{:S(2)}, u32[]{:S(2)}) %collective-permute-start.16) | collective-permute-done | bytes 524320 | tf_op jit(solution)/shard_map/ppermute | solution.py:51
  132.7 1.6 collective-permute-start.11
  134.3 12.6 %collective-permute-done.17.wrap_3 = bf16[2,512,256]{2,1,0:T(8,128)(2,1)S(1)} collective-permute-done((bf16[2,512,256]{2,1,0:T(8,128)(2,1)}, bf16[2,512,256]{2,1,0:T(8,128)(2,1)S(1)}, u32[]{:S(2)}, u32[]{:S(2)}) %collective-permute-start.17) | collective-permute-done | bytes 524320 | tf_op jit(solution)/shard_map/ppermute | solution.py:51
  149.0 4.3 %collective-permute-start.13 = (bf16[2,512,256]{2,1,0:T(8,128)(2,1)}, bf16[2,512,256]{2,1,0:T(8,128)(2,1)}, u32[]{:S(2)}, u32[]{:S(2)}) collective-permute-start(bf16[2,512,256]{2,1,0:T(8,128)(2,1)} %collective-permute-done.10), channel_id=1, source_target_pairs={{8,0},{16,8},{24,16},{40,32},{48,40},{56,48},{72,64},{80,72},{88,8... | collective-permute-start | bytes 1572872 | tf_op jit(solution)/shard_map/ppermute | solution.py:51
  153.3 1.4 fusion.1.value_own
  158.0 1.3 collective-permute-start.8
  161.5 1.3 copy-done.6
  162.8 1.3 copy-done.8
  167.3 11.5 %shard_map.77 = (bf16[512,640]{1,0:T(8,128)(2,1)}, f32[512,640]{1,0:T(8,128)S(1)}, f32[512,640]{1,0:T(8,128)S(1)}, f32[512,640]{1,0:T(8,128)S(1)}, bf16[2,512,25...) custom-call(s32[9]{0:T(128)S(1)} %add_convert_fusion.3.flags, ...), custom_call_target="tpu_custom_call" | custom-call | flops 3221225472 | bytes 8388608 | tf_op jit(solution)/shard_map/pallas_call | solution.py:169
  180.3 9.3 %collective-permute-start.9 = (bf16[2,512,128]{2,1,0:T(8,128)(2,1)}, bf16[2,512,128]{2,1,0:T(8,128)(2,1)S(1)}, u32[]{:S(2)}, u32[]{:S(2)}) collective-permute-start(bf16[2,512,128]{2,1,0:T(8,128)(2,1)} %collective-permute-done.6), channel_id=1, source_target_pairs={{8,0},{16,8},{24,16},{40,32},{48,40},{56,48},{72,64},{80,72},{88,8... | collective-permute-start | bytes 786440 | tf_op jit(solution)/shard_map/ppermute | solution.py:51
  189.6 12.0 %shard_map.78 = (bf16[512,640]{1,0:T(8,128)(2,1)}, f32[512,640]{1,0:T(8,128)S(1)}, f32[512,640]{1,0:T(8,128)S(1)}, f32[512,640]{1,0:T(8,128)S(1)}, bf16[2,512,25...) custom-call(s32[9]{0:T(128)S(1)} %add_convert_fusion.3.flags, ...), custom_call_target="tpu_custom_call", output_to_operand_aliasing={{0}: (13, {}), {1}: (14, {}), {2}: (15, {}), {3}: (16, {})} | custom-call | flops 3221225472 | bytes 8388608 | tf_op jit(solution)/shard_map/pallas_call | solution.py:169
  201.7 6.6 %shard_map.79 = (bf16[512,640]{1,0:T(8,128)(2,1)}, f32[512,640]{1,0:T(8,128)S(1)}, f32[512,640]{1,0:T(8,128)S(1)}, f32[512,640]{1,0:T(8,128)S(1)}, bf16[2,512,12...) custom-call(s32[9]{0:T(128)S(1)} %add_convert_fusion.3.flags, ...), custom_call_target="tpu_custom_call", output_to_operand_aliasing={{0}: (13, {}), {1}: (14, {}), {2}: (15, {}), {3}: (16, {})} | custom-call | flops 1610612736 | bytes 4194304 | tf_op jit(solution)/shard_map/pallas_call | solution.py:169
  208.9 3.7 %collective-permute-start.26 = (bf16[2,512,256]{2,1,0:T(8,128)(2,1)}, bf16[2,512,256]{2,1,0:T(8,128)(2,1)}, u32[]{:S(2)}, u32[]{:S(2)}) collective-permute-start(bf16[2,512,256]{2,1,0:T(8,128)(2,1)} %get-tuple-element.45), channel_id=1, source_target_pairs={{0,16},{8,24},{16,0},{24,8},{32,48},{40,56},{48,32},{56,40},{64,80... | collective-permute-start | bytes 1572872 | tf_op jit(solution)/shard_map/ppermute | solution.py:51
  212.6 2.5 collective-permute-start.27
  215.6 27.0 %psum.15 = f32[5,512]{1,0:T(8,128)S(1)} all-reduce(f32[5,512]{1,0:T(8,128)S(1)} %stack.63), channel_id=1, replica_groups=mesh['tm'=32,'head'=8] {'head'}, use_global_device_ids=true, to_apply=%region_6.7 | all-reduce | flops 2560 | bytes 20480 | tf_op jit(solution)/shard_map/psum | solution.py:336
  242.6 5.3 %collective-permute-start.20 = (f32[512]{0:T(512)S(1)}, f32[512]{0:T(512)S(1)}, u32[]{:S(2)}, u32[]{:S(2)}) collective-permute-start(f32[512]{0:T(512)S(1)} %bitcast.65), channel_id=1, source_target_pairs={{24,0},{32,8},{40,16},{48,24},{56,32},{64,40},{72,48},{80,56},{88,... | collective-permute-start | bytes 6152 | tf_op jit(solution)/shard_map/ppermute | solution.py:39
  247.9 3.6 %collective-permute-start.18 = (f32[512]{0:T(512)S(1)}, f32[512]{0:T(512)S(1)}, u32[]{:S(2)}, u32[]{:S(2)}) collective-permute-start(f32[512]{0:T(512)S(1)} %bitcast.64), channel_id=1, source_target_pairs={{8,0},{16,8},{24,16},{32,24},{40,32},{48,40},{56,48},{64,56},{72,6... | collective-permute-start | bytes 6152 | tf_op jit(solution)/shard_map/ppermute | solution.py:39
  251.5 1.4 collective-permute-done.20
  252.8 7.6 %collective-permute-start.19 = (f32[512]{0:T(512)S(1)}, f32[512]{0:T(512)S(1)}, u32[]{:S(2)}, u32[]{:S(2)}) collective-permute-start(f32[512]{0:T(512)S(1)} %bitcast.60), channel_id=1, source_target_pairs={{16,0},{24,8},{32,16},{40,24},{48,32},{56,40},{64,48},{72,56},{80,... | collective-permute-start | bytes 6152 | tf_op jit(solution)/shard_map/ppermute | solution.py:39
  261.7 4.8 %collective-permute-start.30 = (bf16[2,512,256]{2,1,0:T(8,128)(2,1)S(1)}, bf16[2,512,256]{2,1,0:T(8,128)(2,1)S(1)}, u32[]{:S(2)}, u32[]{:S(2)}) collective-permute-start(bf16[2,512,256]{2,1,0:T(8,128)(2,1)S(1)} %get-tuple-element.48), channel_id=1, source_target_pairs={{0,16},{8,24},{16,0},{24,8},{32,48},{40,56},{48,32},{56,40},{64,80... | collective-permute-start | bytes 1572872 | tf_op jit(solution)/shard_map/ppermute | solution.py:51
  268.7 2.1 collective-permute-start.21
  271.6 2.1 add_convert_fusion.1
  273.7 15.3 %collective-permute-done.29.in_1 = bf16[2,512,256]{2,1,0:T(8,128)(2,1)S(1)} collective-permute-done((bf16[2,512,256]{2,1,0:T(8,128)(2,1)S(1)}, bf16[2,512,256]{2,1,0:T(8,128)(2,1)S(1)}, u32[]{:S(2)}, u32[]{:S(2)}) %collective-permute-start.29) | collective-permute-done | bytes 524320 | tf_op jit(solution)/shard_map/ppermute | solution.py:51
  289.0 2.5 collective-permute-start.28
  291.9 5.9 %collective-permute-start.32 = (bf16[2,512,256]{2,1,0:T(8,128)(2,1)S(1)}, bf16[2,512,256]{2,1,0:T(8,128)(2,1)S(1)}, u32[]{:S(2)}, u32[]{:S(2)}) collective-permute-start(bf16[2,512,256]{2,1,0:T(8,128)(2,1)S(1)} %add_convert_fusion), channel_id=1, source_target_pairs={{40,8},{48,16},{56,24},{72,40},{80,48},{88,56},{104,72},{112,80},{... | collective-permute-start | bytes 1572872 | tf_op jit(solution)/shard_map/ppermute | solution.py:39
  298.0 5.3 %collective-permute-start.24 = (bf16[2,512,128]{2,1,0:T(8,128)(2,1)S(1)}, bf16[2,512,128]{2,1,0:T(8,128)(2,1)S(1)}, u32[]{:S(2)}, u32[]{:S(2)}) collective-permute-start(bf16[2,512,128]{2,1,0:T(8,128)(2,1)S(1)} %add_convert_fusion.2), channel_id=1, source_target_pairs={{40,8},{48,16},{56,24},{72,40},{80,48},{88,56},{104,72},{112,80},{... | collective-permute-start | bytes 786440 | tf_op jit(solution)/shard_map/ppermute | solution.py:39
  304.3 35.4 %collective-permute-done.32.crossed = bf16[2,512,256]{2,1,0:T(8,128)(2,1)S(1)} collective-permute-done((bf16[2,512,256]{2,1,0:T(8,128)(2,1)S(1)}, bf16[2,512,256]{2,1,0:T(8,128)(2,1)S(1)}, u32[]{:S(2)}, u32[]{:S(2)}) %collective-permute-start.32) | collective-permute-done | bytes 524320 | tf_op jit(solution)/shard_map/ppermute | solution.py:39
  340.5 4.3 %shard_map.80.refs_0_ = f32[3,512,640]{2,1,0:T(8,128)} custom-call(s32[9]{0:T(128)} %copy-done.11, f32[2]{0:T(128)} %pad_maximum_fusion.1.keep_ref, f32[512,8]{1,0:T(8,128)} %bitcast.43, f32[1,640]{1,0:T(1,128)} %broadcast_in_dim.30.gain_q, f32[1,640]{1,0:T(1,128)} %copy-done.10, bf16[3,512,640]{2,1,0:T(8,128)(2,1)} %clean.5, bf16[3,512,640]{2,1,0:T(8,128)(2,1)} %noise.5, ...), custom_call_target="tpu_custom_call" | custom-call | flops 3932160 | bytes 6291456 | tf_op jit(solution)/shard_map/pallas_call | solution.py:246
  344.8 4.3 %shard_map.81.refs_0_ = f32[3,512,640]{2,1,0:T(8,128)} custom-call(s32[9]{0:T(128)} %copy-done.11, f32[2]{0:T(128)} %pad_maximum_fusion.1.keep_ref, f32[512,8]{1,0:T(8,128)} %bitcast.44, f32[1,640]{1,0:T(1,128)} %broadcast_in_dim.30.gain_q, f32[1,640]{1,0:T(1,128)} %copy-done.10, bf16[3,512,640]{2,1,0:T(8,128)(2,1)} %clean.5, ...), custom_call_target="tpu_custom_call", output_to_operand_aliasing={{}: (14, {})} | custom-call | flops 3932160 | bytes 6291456 | tf_op jit(solution)/shard_map/pallas_call | solution.py:246
  349.8 3.2 shard_map.82
  (156 shorter events, 25.2 us)
Async XLA Ops:
  3.3 145.7 %collective-permute-start.3 = (bf16[2,512,640]{2,1,0:T(8,128)(2,1)}, bf16[2,512,640]{2,1,0:T(8,128)(2,1)S(1)}, u32[]{:S(2)}, u32[]{:S(2)}) collective-permute-start(bf16[2,512,640]{2,1,0:T(8,128)(2,1)} %slice.76), channel_id=1, source_target_pairs={{0,8},{8,16},{16,24},{32,40},{40,48},{48,56},{64,72},{72,80},{80,8... | collective-permute-start | bytes 3932168 | tf_op jit(solution)/shard_map/ppermute | solution.py:51
  6.7 106.3 %collective-permute-start.6 = (bf16[2,512,128]{2,1,0:T(8,128)(2,1)S(1)}, bf16[2,512,128]{2,1,0:T(8,128)(2,1)}, u32[]{:S(2)}, u32[]{:S(2)}) collective-permute-start(bf16[2,512,128]{2,1,0:T(8,128)(2,1)S(1)} %slice.77), channel_id=1, source_target_pairs={{8,40},{16,48},{24,56},{40,72},{48,80},{56,88},{72,104},{80,112},{... | collective-permute-start | bytes 786440 | tf_op jit(solution)/shard_map/ppermute | solution.py:39
  16.8 98.0 %collective-permute-start.10 = (bf16[2,512,256]{2,1,0:T(8,128)(2,1)}, bf16[2,512,256]{2,1,0:T(8,128)(2,1)}, u32[]{:S(2)}, u32[]{:S(2)}) collective-permute-start(bf16[2,512,256]{2,1,0:T(8,128)(2,1)} %get-tuple-element.60), channel_id=1, source_target_pairs={{8,40},{16,48},{24,56},{40,72},{48,80},{56,88},{72,104},{80,112},{... | collective-permute-start | bytes 1572872 | tf_op jit(solution)/shard_map/ppermute | solution.py:39
  18.8 61.9 %collective-permute-start.14 = (bf16[2,512,256]{2,1,0:T(8,128)(2,1)}, bf16[2,512,256]{2,1,0:T(8,128)(2,1)}, u32[]{:S(2)}, u32[]{:S(2)}) collective-permute-start(bf16[2,512,256]{2,1,0:T(8,128)(2,1)} %get-tuple-element.59), channel_id=1, source_target_pairs={{8,40},{16,48},{24,56},{40,72},{48,80},{56,88},{72,104},{80,112},{... | collective-permute-start | bytes 1572872 | tf_op jit(solution)/shard_map/ppermute | solution.py:39
  25.9 98.7 %copy-start.36 = (f32[640]{0:T(1024)S(1)}, f32[640]{0:T(1024)}, u32[]{:S(2)}) copy-start(f32[640]{0:T(1024)} %param.10) | copy-start | bytes 7684
  25.9 98.8 %copy-start.38 = (f32[640]{0:T(1024)S(1)}, f32[640]{0:T(1024)}, u32[]{:S(2)}) copy-start(f32[640]{0:T(1024)} %param.9) | copy-start | bytes 7684
  80.6 47.2 %copy-start.34 = (f32[3,512]{1,0:T(4,128)}, f32[3,512]{1,0:T(4,128)S(1)}, u32[]{:S(2)}) copy-start(f32[3,512]{1,0:T(4,128)S(1)} %add_rsqrt_fusion) | copy-start | bytes 18436
  80.6 35.5 %collective-permute-start.15 = (bf16[2,512,256]{2,1,0:T(8,128)(2,1)}, bf16[2,512,256]{2,1,0:T(8,128)(2,1)S(1)}, u32[]{:S(2)}, u32[]{:S(2)}) collective-permute-start(bf16[2,512,256]{2,1,0:T(8,128)(2,1)} %collective-permute-done.14), channel_id=1, source_target_pairs={{24,0},{56,32},{88,64},{120,96},{152,128},{184,160},{216,192},{248... | collective-permute-start | bytes 1572872 | tf_op jit(solution)/shard_map/ppermute | solution.py:51
  81.3 5.5 %collective-permute-start = (f32[512]{0:T(512)S(1)}, f32[512]{0:T(512)S(1)}, u32[]{:S(2)}, u32[]{:S(2)}) collective-permute-start(f32[512]{0:T(512)S(1)} %bitcast.61), channel_id=1, source_target_pairs={{0,8},{8,16},{16,24},{24,32},{32,40},{40,48},{48,56},{56,64},{64,7... | collective-permute-start | bytes 6152 | tf_op jit(solution)/shard_map/ppermute | solution.py:39
  86.8 29.3 %copy-start.40 = (f32[512]{0:T(512)}, f32[512]{0:T(512)S(1)}, u32[]{:S(2)}) copy-start(f32[512]{0:T(512)S(1)} %collective-permute-done) | copy-start | bytes 6148
  86.8 12.7 %collective-permute-start.1 = (f32[512]{0:T(512)S(1)}, f32[512]{0:T(512)S(1)}, u32[]{:S(2)}, u32[]{:S(2)}) collective-permute-start(f32[512]{0:T(512)S(1)} %bitcast.62), channel_id=1, source_target_pairs={{0,16},{8,24},{16,32},{24,40},{32,48},{40,56},{48,64},{56,72},{64,... | collective-permute-start | bytes 6152 | tf_op jit(solution)/shard_map/ppermute | solution.py:39
  99.5 28.3 %copy-start.42 = (f32[512]{0:T(512)}, f32[512]{0:T(512)S(1)}, u32[]{:S(2)}) copy-start(f32[512]{0:T(512)S(1)} %collective-permute-done.1) | copy-start | bytes 6148
  99.5 11.2 %collective-permute-start.2 = (f32[512]{0:T(512)S(1)}, f32[512]{0:T(512)S(1)}, u32[]{:S(2)}, u32[]{:S(2)}) collective-permute-start(f32[512]{0:T(512)S(1)} %bitcast.63), channel_id=1, source_target_pairs={{0,24},{8,32},{16,40},{24,48},{32,56},{40,64},{48,72},{56,80},{64,... | collective-permute-start | bytes 6152 | tf_op jit(solution)/shard_map/ppermute | solution.py:39
  110.7 17.1 %copy-start.44 = (f32[512]{0:T(512)}, f32[512]{0:T(512)S(1)}, u32[]{:S(2)}) copy-start(f32[512]{0:T(512)S(1)} %collective-permute-done.2) | copy-start | bytes 6148
  110.7 45.5 %collective-permute-start.4 = (bf16[2,512,640]{2,1,0:T(8,128)(2,1)}, bf16[2,512,640]{2,1,0:T(8,128)(2,1)S(1)}, u32[]{:S(2)}, u32[]{:S(2)}) collective-permute-start(bf16[2,512,640]{2,1,0:T(8,128)(2,1)} %slice.76), channel_id=1, source_target_pairs={{0,16},{8,24},{32,48},{40,56},{64,80},{72,88},{96,112},{104,120},{... | collective-permute-start | bytes 3932168 | tf_op jit(solution)/shard_map/ppermute | solution.py:51
  113.0 44.9 %collective-permute-start.5 = (bf16[2,512,640]{2,1,0:T(8,128)(2,1)}, bf16[2,512,640]{2,1,0:T(8,128)(2,1)}, u32[]{:S(2)}, u32[]{:S(2)}) collective-permute-start(bf16[2,512,640]{2,1,0:T(8,128)(2,1)} %slice.76), channel_id=1, source_target_pairs={{0,24},{32,56},{64,88},{96,120},{128,152},{160,184},{192,216},{224... | collective-permute-start | bytes 3932168 | tf_op jit(solution)/shard_map/ppermute | solution.py:51
  114.8 17.9 %collective-permute-start.16 = (bf16[2,512,256]{2,1,0:T(8,128)(2,1)}, bf16[2,512,256]{2,1,0:T(8,128)(2,1)}, u32[]{:S(2)}, u32[]{:S(2)}) collective-permute-start(bf16[2,512,256]{2,1,0:T(8,128)(2,1)} %collective-permute-done.14), channel_id=1, source_target_pairs={{16,0},{24,8},{48,32},{56,40},{80,64},{88,72},{112,96},{120,104},{... | collective-permute-start | bytes 1572872 | tf_op jit(solution)/shard_map/ppermute | solution.py:51
  116.9 30.0 %collective-permute-start.17 = (bf16[2,512,256]{2,1,0:T(8,128)(2,1)}, bf16[2,512,256]{2,1,0:T(8,128)(2,1)S(1)}, u32[]{:S(2)}, u32[]{:S(2)}) collective-permute-start(bf16[2,512,256]{2,1,0:T(8,128)(2,1)} %collective-permute-done.14), channel_id=1, source_target_pairs={{8,0},{16,8},{24,16},{40,32},{48,40},{56,48},{72,64},{80,72},{88,8... | collective-permute-start | bytes 1572872 | tf_op jit(solution)/shard_map/ppermute | solution.py:51
  124.6 77.1 %copy-start.10 = (f32[1,640]{1,0:T(1,128)}, f32[1,640]{1,0:T(1,128)S(1)}, u32[]{:S(2)}) copy-start(f32[1,640]{1,0:T(1,128)S(1)} %broadcast_in_dim.28.gain.gain_k) | copy-start | bytes 7684
  124.7 77.0 %copy-start.11 = (s32[9]{0:T(128)}, s32[9]{0:T(128)S(1)}, u32[]{:S(2)}) copy-start(s32[9]{0:T(128)S(1)} %add_convert_fusion.3.flags) | copy-start | bytes 112
  127.8 26.9 %copy-start.41 = (f32[512]{0:T(512)S(1)}, f32[512]{0:T(512)}, u32[]{:S(2)}) copy-start(f32[512]{0:T(512)} %copy-done.40) | copy-start | bytes 6148
  132.7 22.0 %copy-start.43 = (f32[512]{0:T(512)S(1)}, f32[512]{0:T(512)}, u32[]{:S(2)}) copy-start(f32[512]{0:T(512)} %copy-done.42) | copy-start | bytes 6148
  132.7 22.0 %copy-start.45 = (f32[512]{0:T(512)S(1)}, f32[512]{0:T(512)}, u32[]{:S(2)}) copy-start(f32[512]{0:T(512)} %copy-done.44) | copy-start | bytes 6148
  132.7 47.6 %collective-permute-start.11 = (bf16[2,512,256]{2,1,0:T(8,128)(2,1)}, bf16[2,512,256]{2,1,0:T(8,128)(2,1)}, u32[]{:S(2)}, u32[]{:S(2)}) collective-permute-start(bf16[2,512,256]{2,1,0:T(8,128)(2,1)} %collective-permute-done.10), channel_id=1, source_target_pairs={{24,0},{56,32},{88,64},{120,96},{152,128},{184,160},{216,192},{248... | collective-permute-start | bytes 1572872 | tf_op jit(solution)/shard_map/ppermute | solution.py:51
  147.7 41.9 %collective-permute-start.12 = (bf16[2,512,256]{2,1,0:T(8,128)(2,1)}, bf16[2,512,256]{2,1,0:T(8,128)(2,1)}, u32[]{:S(2)}, u32[]{:S(2)}) collective-permute-start(bf16[2,512,256]{2,1,0:T(8,128)(2,1)} %collective-permute-done.10), channel_id=1, source_target_pairs={{16,0},{24,8},{48,32},{56,40},{80,64},{88,72},{112,96},{120,104},{... | collective-permute-start | bytes 1572872 | tf_op jit(solution)/shard_map/ppermute | solution.py:51
  149.0 40.6 %collective-permute-start.13 = (bf16[2,512,256]{2,1,0:T(8,128)(2,1)}, bf16[2,512,256]{2,1,0:T(8,128)(2,1)}, u32[]{:S(2)}, u32[]{:S(2)}) collective-permute-start(bf16[2,512,256]{2,1,0:T(8,128)(2,1)} %collective-permute-done.10), channel_id=1, source_target_pairs={{8,0},{16,8},{24,16},{40,32},{48,40},{56,48},{72,64},{80,72},{88,8... | collective-permute-start | bytes 1572872 | tf_op jit(solution)/shard_map/ppermute | solution.py:51
  157.3 44.4 %collective-permute-start.7 = (bf16[2,512,128]{2,1,0:T(8,128)(2,1)}, bf16[2,512,128]{2,1,0:T(8,128)(2,1)S(1)}, u32[]{:S(2)}, u32[]{:S(2)}) collective-permute-start(bf16[2,512,128]{2,1,0:T(8,128)(2,1)} %collective-permute-done.6), channel_id=1, source_target_pairs={{24,0},{56,32},{88,64},{120,96},{152,128},{184,160},{216,192},{248... | collective-permute-start | bytes 786440 | tf_op jit(solution)/shard_map/ppermute | solution.py:51
  158.0 43.7 %collective-permute-start.8 = (bf16[2,512,128]{2,1,0:T(8,128)(2,1)}, bf16[2,512,128]{2,1,0:T(8,128)(2,1)S(1)}, u32[]{:S(2)}, u32[]{:S(2)}) collective-permute-start(bf16[2,512,128]{2,1,0:T(8,128)(2,1)} %collective-permute-done.6), channel_id=1, source_target_pairs={{16,0},{24,8},{48,32},{56,40},{80,64},{88,72},{112,96},{120,104},{... | collective-permute-start | bytes 786440 | tf_op jit(solution)/shard_map/ppermute | solution.py:51
  180.3 21.4 %collective-permute-start.9 = (bf16[2,512,128]{2,1,0:T(8,128)(2,1)}, bf16[2,512,128]{2,1,0:T(8,128)(2,1)S(1)}, u32[]{:S(2)}, u32[]{:S(2)}) collective-permute-start(bf16[2,512,128]{2,1,0:T(8,128)(2,1)} %collective-permute-done.6), channel_id=1, source_target_pairs={{8,0},{16,8},{24,16},{40,32},{48,40},{56,48},{72,64},{80,72},{88,8... | collective-permute-start | bytes 786440 | tf_op jit(solution)/shard_map/ppermute | solution.py:51
  208.9 57.6 %collective-permute-start.25 = (bf16[2,512,256]{2,1,0:T(8,128)(2,1)}, bf16[2,512,256]{2,1,0:T(8,128)(2,1)S(1)}, u32[]{:S(2)}, u32[]{:S(2)}) collective-permute-start(bf16[2,512,256]{2,1,0:T(8,128)(2,1)} %get-tuple-element.44), channel_id=1, source_target_pairs={{0,24},{8,0},{16,8},{24,16},{32,56},{40,32},{48,40},{56,48},{64,88... | collective-permute-start | bytes 1572872 | tf_op jit(solution)/shard_map/ppermute | solution.py:51
  208.9 59.7 %collective-permute-start.26 = (bf16[2,512,256]{2,1,0:T(8,128)(2,1)}, bf16[2,512,256]{2,1,0:T(8,128)(2,1)}, u32[]{:S(2)}, u32[]{:S(2)}) collective-permute-start(bf16[2,512,256]{2,1,0:T(8,128)(2,1)} %get-tuple-element.45), channel_id=1, source_target_pairs={{0,16},{8,24},{16,0},{24,8},{32,48},{40,56},{48,32},{56,40},{64,80... | collective-permute-start | bytes 1572872 | tf_op jit(solution)/shard_map/ppermute | solution.py:51
  212.6 58.2 %collective-permute-start.27 = (bf16[2,512,256]{2,1,0:T(8,128)(2,1)}, bf16[2,512,256]{2,1,0:T(8,128)(2,1)}, u32[]{:S(2)}, u32[]{:S(2)}) collective-permute-start(bf16[2,512,256]{2,1,0:T(8,128)(2,1)} %get-tuple-element.46), channel_id=1, source_target_pairs={{0,8},{8,16},{16,24},{24,0},{32,40},{40,48},{48,56},{56,32},{64,72... | collective-permute-start | bytes 1572872 | tf_op jit(solution)/shard_map/ppermute | solution.py:51
  215.1 45.3 %copy-start.15 = (bf16[2,512,256]{2,1,0:T(8,128)(2,1)S(1)}, bf16[2,512,256]{2,1,0:T(8,128)(2,1)}, u32[]{:S(2)}) copy-start(bf16[2,512,256]{2,1,0:T(8,128)(2,1)} %copy-done.14) | copy-start | bytes 1572868
  215.1 52.2 %copy-start.13 = (bf16[2,512,256]{2,1,0:T(8,128)(2,1)S(1)}, bf16[2,512,256]{2,1,0:T(8,128)(2,1)}, u32[]{:S(2)}) copy-start(bf16[2,512,256]{2,1,0:T(8,128)(2,1)} %copy-done.12) | copy-start | bytes 1572868
  242.6 10.3 %collective-permute-start.20 = (f32[512]{0:T(512)S(1)}, f32[512]{0:T(512)S(1)}, u32[]{:S(2)}, u32[]{:S(2)}) collective-permute-start(f32[512]{0:T(512)S(1)} %bitcast.65), channel_id=1, source_target_pairs={{24,0},{32,8},{40,16},{48,24},{56,32},{64,40},{72,48},{80,56},{88,... | collective-permute-start | bytes 6152 | tf_op jit(solution)/shard_map/ppermute | solution.py:39
  247.9 12.6 %collective-permute-start.18 = (f32[512]{0:T(512)S(1)}, f32[512]{0:T(512)S(1)}, u32[]{:S(2)}, u32[]{:S(2)}) collective-permute-start(f32[512]{0:T(512)S(1)} %bitcast.64), channel_id=1, source_target_pairs={{8,0},{16,8},{24,16},{32,24},{40,32},{48,40},{56,48},{64,56},{72,6... | collective-permute-start | bytes 6152 | tf_op jit(solution)/shard_map/ppermute | solution.py:39
  252.8 8.9 %collective-permute-start.19 = (f32[512]{0:T(512)S(1)}, f32[512]{0:T(512)S(1)}, u32[]{:S(2)}, u32[]{:S(2)}) collective-permute-start(f32[512]{0:T(512)S(1)} %bitcast.60), channel_id=1, source_target_pairs={{16,0},{24,8},{32,16},{40,24},{48,32},{56,40},{64,48},{72,56},{80,... | collective-permute-start | bytes 6152 | tf_op jit(solution)/shard_map/ppermute | solution.py:39
  260.4 28.6 %collective-permute-start.29 = (bf16[2,512,256]{2,1,0:T(8,128)(2,1)S(1)}, bf16[2,512,256]{2,1,0:T(8,128)(2,1)S(1)}, u32[]{:S(2)}, u32[]{:S(2)}) collective-permute-start(bf16[2,512,256]{2,1,0:T(8,128)(2,1)S(1)} %copy-done.15), channel_id=1, source_target_pairs={{0,24},{8,0},{16,8},{24,16},{32,56},{40,32},{48,40},{56,48},{64,88... | collective-permute-start | bytes 1572872 | tf_op jit(solution)/shard_map/ppermute | solution.py:51
  261.7 27.3 %collective-permute-start.30 = (bf16[2,512,256]{2,1,0:T(8,128)(2,1)S(1)}, bf16[2,512,256]{2,1,0:T(8,128)(2,1)S(1)}, u32[]{:S(2)}, u32[]{:S(2)}) collective-permute-start(bf16[2,512,256]{2,1,0:T(8,128)(2,1)S(1)} %get-tuple-element.48), channel_id=1, source_target_pairs={{0,16},{8,24},{16,0},{24,8},{32,48},{40,56},{48,32},{56,40},{64,80... | collective-permute-start | bytes 1572872 | tf_op jit(solution)/shard_map/ppermute | solution.py:51
  267.3 24.2 %collective-permute-start.31 = (bf16[2,512,256]{2,1,0:T(8,128)(2,1)S(1)}, bf16[2,512,256]{2,1,0:T(8,128)(2,1)S(1)}, u32[]{:S(2)}, u32[]{:S(2)}) collective-permute-start(bf16[2,512,256]{2,1,0:T(8,128)(2,1)S(1)} %copy-done.13), channel_id=1, source_target_pairs={{0,8},{8,16},{16,24},{24,0},{32,40},{40,48},{48,56},{56,32},{64,72... | collective-permute-start | bytes 1572872 | tf_op jit(solution)/shard_map/ppermute | solution.py:51
  268.7 29.1 %collective-permute-start.21 = (bf16[2,512,128]{2,1,0:T(8,128)(2,1)}, bf16[2,512,128]{2,1,0:T(8,128)(2,1)S(1)}, u32[]{:S(2)}, u32[]{:S(2)}) collective-permute-start(bf16[2,512,128]{2,1,0:T(8,128)(2,1)} %copy-done.21), channel_id=1, source_target_pairs={{0,24},{8,0},{16,8},{24,16},{32,56},{40,32},{48,40},{56,48},{64,88... | collective-permute-start | bytes 786440 | tf_op jit(solution)/shard_map/ppermute | solution.py:51
  270.8 27.0 %collective-permute-start.22 = (bf16[2,512,128]{2,1,0:T(8,128)(2,1)}, bf16[2,512,128]{2,1,0:T(8,128)(2,1)S(1)}, u32[]{:S(2)}, u32[]{:S(2)}) collective-permute-start(bf16[2,512,128]{2,1,0:T(8,128)(2,1)} %copy-done.20), channel_id=1, source_target_pairs={{0,16},{8,24},{16,0},{24,8},{32,48},{40,56},{48,32},{56,40},{64,80... | collective-permute-start | bytes 786440 | tf_op jit(solution)/shard_map/ppermute | solution.py:51
  289.0 14.3 %copy-start.35 = (f32[3,512]{1,0:T(4,128)S(1)}, f32[3,512]{1,0:T(4,128)}, u32[]{:S(2)}) copy-start(f32[3,512]{1,0:T(4,128)} %copy-done.34) | copy-start | bytes 18436
  289.0 8.8 %collective-permute-start.23 = (bf16[2,512,128]{2,1,0:T(8,128)(2,1)S(1)}, bf16[2,512,128]{2,1,0:T(8,128)(2,1)S(1)}, u32[]{:S(2)}, u32[]{:S(2)}) collective-permute-start(bf16[2,512,128]{2,1,0:T(8,128)(2,1)S(1)} %get-tuple-element.43), channel_id=1, source_target_pairs={{0,8},{8,16},{16,24},{24,0},{32,40},{40,48},{48,56},{56,32},{64,72... | collective-permute-start | bytes 786440 | tf_op jit(solution)/shard_map/ppermute | solution.py:51
  289.0 55.8 %collective-permute-start.28 = (bf16[2,512,256]{2,1,0:T(8,128)(2,1)}, bf16[2,512,256]{2,1,0:T(8,128)(2,1)}, u32[]{:S(2)}, u32[]{:S(2)}) collective-permute-start(bf16[2,512,256]{2,1,0:T(8,128)(2,1)} %add_convert_fusion.1), channel_id=1, source_target_pairs={{40,8},{48,16},{56,24},{72,40},{80,48},{88,56},{104,72},{112,80},{... | collective-permute-start | bytes 1572872 | tf_op jit(solution)/shard_map/ppermute | solution.py:39
  291.9 47.8 %collective-permute-start.32 = (bf16[2,512,256]{2,1,0:T(8,128)(2,1)S(1)}, bf16[2,512,256]{2,1,0:T(8,128)(2,1)S(1)}, u32[]{:S(2)}, u32[]{:S(2)}) collective-permute-start(bf16[2,512,256]{2,1,0:T(8,128)(2,1)S(1)} %add_convert_fusion), channel_id=1, source_target_pairs={{40,8},{48,16},{56,24},{72,40},{80,48},{88,56},{104,72},{112,80},{... | collective-permute-start | bytes 1572872 | tf_op jit(solution)/shard_map/ppermute | solution.py:39
  297.8 47.0 %copy-start.31 = (bf16[2,512,128]{2,1,0:T(8,128)(2,1)}, bf16[2,512,128]{2,1,0:T(8,128)(2,1)S(1)}, u32[]{:S(2)}) copy-start(bf16[2,512,128]{2,1,0:T(8,128)(2,1)S(1)} %collective-permute-done.23.in_3) | copy-start | bytes 786436
  298.0 51.1 %collective-permute-start.24 = (bf16[2,512,128]{2,1,0:T(8,128)(2,1)S(1)}, bf16[2,512,128]{2,1,0:T(8,128)(2,1)S(1)}, u32[]{:S(2)}, u32[]{:S(2)}) collective-permute-start(bf16[2,512,128]{2,1,0:T(8,128)(2,1)S(1)} %add_convert_fusion.2), channel_id=1, source_target_pairs={{40,8},{48,16},{56,24},{72,40},{80,48},{88,56},{104,72},{112,80},{... | collective-permute-start | bytes 786440 | tf_op jit(solution)/shard_map/ppermute | solution.py:39
  (31 other events, 131.2 us)

commit v2 on v1

v2 whole, which is shorter than its diff:
```python
import math

import jax
import jax.numpy as jnp
from jax import lax
from jax.experimental import pallas as pl
from jax.experimental.pallas import tpu as pltpu
from jax.sharding import PartitionSpec as P

D = 5120
HEAD_DIM = 128
CONTEXT = 3
COLUMNS = 4
KEY_TILE = 256
VMEM_LIMIT = 60 * 2**20

epsilon = 1e-06
masked_score = -1e30
NT = (((1,), (1,)), ((), ()))
NN = (((1,), (0,)), ((), ()))


def dot(left, right, dims):
    return lax.dot_general(left, right, dims, preferred_element_type=jnp.float32)


def noise_share_of(timestep):
    level = timestep.astype(jnp.float32) / 1000.0
    return 5.0 * level / (1.0 + 4.0 * level)


def shift_spans(block, distance, columns=range(COLUMNS)):
    count = lax.axis_size("tm")
    route = [
        (i, i + distance)
        for i in range(count)
        if 0 <= i + distance < count and i % COLUMNS in columns
    ]
    return lax.ppermute(block, "tm", route)


def shift_columns(block, distance, kind):
    count = lax.axis_size("tm")
    route = []
    for i in range(count):
        row, column = divmod(i, COLUMNS)
        target = column + distance
        inside = 0 <= target < COLUMNS
        if kind == "both" or inside == (kind == "inside"):
            route.append((i, row * COLUMNS + target % COLUMNS))
    return lax.ppermute(block, "tm", route)


def as_columns(rows_ref):
    rows = rows_ref[...]
    return jnp.concatenate([rows] * (HEAD_DIM // 8), axis=0).T


def prepare_body(shares, clean, noise, sums, columns):
    f32 = jnp.float32
    keep, share = shares[0], shares[1]
    clean_key = clean[1].astype(f32)
    query = keep * clean[0].astype(f32) + share * noise[0].astype(f32)
    key = keep * clean_key + share * noise[1].astype(f32)
    lane = lax.broadcasted_iota(jnp.int32, columns.shape, 1)
    step = jnp.zeros(columns.shape, f32)
    for i, field in enumerate((query, key, clean_key)):
        step = jnp.where(lane == i, jnp.sum(field * field, axis=1, keepdims=True), step)

    @pl.when(pl.program_id(0) == 0)
    def _():
        columns[...] = step

    @pl.when(pl.program_id(0) > 0)
    def _():
        columns[...] += step

    @pl.when(pl.program_id(0) == pl.num_programs(0) - 1)
    def _():
        sums[...] = columns[...].T[0:8]


def prepare(shares, clean, noise):
    _, rows, width = clean.shape
    pair = pl.BlockSpec((2, rows, HEAD_DIM), lambda h: (0, 0, h))
    return pl.pallas_call(
        prepare_body,
        grid=(width // HEAD_DIM,),
        in_specs=[pl.BlockSpec(memory_space=pltpu.SMEM), pair, pair],
        out_specs=pl.BlockSpec((8, rows), lambda h: (0, 0)),
        out_shape=jax.ShapeDtypeStruct((8, rows), jnp.float32),
        scratch_shapes=[pltpu.VMEM((rows, HEAD_DIM), jnp.float32)],
        compiler_params=pltpu.CompilerParams(
            dimension_semantics=("arbitrary",), vmem_limit_bytes=VMEM_LIMIT
        ),
        cost_estimate=pl.CostEstimate(
            flops=rows * width * 12, bytes_accessed=rows * width * 8, transcendentals=0
        ),
    )(shares, clean, noise)


def attention_body(
    flags, shares, inverse, gain_q, gain_k, clean, noise, grad,
    first_1, first_2, first_3, both_1, both_2, both_3, last_1, last_2, last_3, *refs
):
    (attended, grad_query, grad_key, grad_value, back_1, back_2, back_3, inner,
     exps, probs, keys, values, cols, products) = refs[-14:]
    f32, bf16 = jnp.float32, jnp.bfloat16
    rows = grad.shape[0]
    scale = HEAD_DIM**-0.5
    exponent_scale = scale * math.log2(math.e)
    keep, share = shares[0], shares[1]
    gains_q, gains_k = gain_q[...], gain_k[...]
    sources = (
        (first_1, both_1, last_1),
        (first_2, both_2, last_2),
        (first_3, both_3, last_3),
    )
    backs = (back_1, back_2, back_3)

    @pl.when(pl.program_id(0) == 0)
    def _():
        products[...] = jnp.zeros_like(products)
        cols[...] = as_columns(inverse)

    field_query = keep * clean[0].astype(f32) + share * noise[0].astype(f32)
    field_key = keep * clean[1].astype(f32) + share * noise[1].astype(f32)
    field_value = keep * clean[2].astype(f32) + share * noise[2].astype(f32)
    queries = (field_query * cols[:, 0:1] * gains_q).astype(bf16)
    keys[0:rows] = (field_key * cols[:, 1:2] * gains_k).astype(bf16)
    values[0:rows] = field_value.astype(bf16)
    for hop, (first, both, last) in enumerate(sources):
        inside = flags[hop] > 0
        block = pl.ds((hop + 1) * rows, rows)
        keys[block] = jnp.where(inside, both[...], last[...])
        values[block] = jnp.where(inside, first[...], both[...])
    grads = grad[...]
    tiles = rows // KEY_TILE

    row_max = None
    for block in range(CONTEXT + 1):
        block_max = None
        for tile in range(tiles):
            part = pl.ds(block * rows + tile * KEY_TILE, KEY_TILE)
            scores = dot(keys[part], queries, NT)
            exps[part] = scores
            tile_max = jnp.max(scores, axis=0, keepdims=True)
            block_max = tile_max if block_max is None else jnp.maximum(block_max, tile_max)
        if block > 0:
            block_max = jnp.where(flags[2 + block] > 0, block_max, masked_score)
        row_max = block_max if row_max is None else jnp.maximum(row_max, block_max)
    offset = row_max * exponent_scale
    total = jnp.zeros((1, rows), f32)
    delta = jnp.zeros((1, rows), f32)
    for block in range(CONTEXT + 1):
        block_offset = offset
        if block > 0:
            block_offset = jnp.where(flags[2 + block] > 0, offset, -masked_score)
        for tile in range(tiles):
            part = pl.ds(block * rows + tile * KEY_TILE, KEY_TILE)
            exponent = jnp.exp2(exps[part] * exponent_scale - block_offset)
            grad_probs = dot(values[part], grads, NT)
            exps[part] = exponent
            probs[part] = grad_probs
            total = total + jnp.sum(exponent, axis=0, keepdims=True)
            delta = delta + jnp.sum(exponent * grad_probs, axis=0, keepdims=True)
    inverse_total = 1.0 / total
    delta = delta * inverse_total
    output = jnp.zeros((HEAD_DIM, rows), f32)
    query_grad = jnp.zeros((HEAD_DIM, rows), f32)
    lane = lax.broadcasted_iota(jnp.int32, (KEY_TILE, HEAD_DIM), 1)

    def add_product(here, index, product):
        product = jnp.sum(product, axis=1, keepdims=True)
        products[here] += jnp.where(lane == index, product, 0.0)

    for block in range(CONTEXT + 1):
        for tile in range(tiles):
            part = pl.ds(block * rows + tile * KEY_TILE, KEY_TILE)
            here = pl.ds(tile * KEY_TILE, KEY_TILE)
            attention = exps[part] * inverse_total
            weights = attention.astype(bf16)
            grad_scores = (attention * (probs[part] - delta) * scale).astype(bf16)
            output = output + dot(values[part].T, weights, NN)
            query_grad = query_grad + dot(keys[part].T, grad_scores, NN)
            value_part = dot(weights, grads, NN)
            key_part = dot(grad_scores, queries, NN)
            if block == 0:
                grad_key[here] = key_part
                grad_value[here] = value_part
                field = keep * clean[1, here].astype(f32) + share * noise[1, here].astype(f32)
                add_product(here, 1, field * gains_k * key_part)
            else:
                back = backs[block - 1]
                back[0, here] = key_part.astype(bf16)
                back[1, here] = value_part.astype(bf16)
                add_product(here, 1 + block, keys[part].astype(f32) * key_part)
    attended[...] = output.T.astype(bf16)
    grad_query[...] = query_grad.T
    for tile in range(tiles):
        here = pl.ds(tile * KEY_TILE, KEY_TILE)
        field = keep * clean[0, here].astype(f32) + share * noise[0, here].astype(f32)
        add_product(here, 0, field * gains_q * grad_query[here])

    @pl.when(pl.program_id(0) == pl.num_programs(0) - 1)
    def _():
        inner[...] = products[...].T[0:8]


def attention_chunk(first, heads, flags, shares, inverse, gains, fields, grad, gathered, last, last_at, previous):
    rows, width = grad.shape
    here = lambda h: (0, first + h)
    f32, bf16 = jnp.float32, jnp.bfloat16
    smem = pl.BlockSpec(memory_space=pltpu.SMEM)
    small = pl.BlockSpec((8, rows), lambda h: (0, 0))
    wide = pl.BlockSpec((rows, HEAD_DIM), here)
    gain_spec = pl.BlockSpec((1, HEAD_DIM), here)
    field_spec = pl.BlockSpec((3, rows, HEAD_DIM), lambda h: (0, 0, first + h))
    last_spec = pl.BlockSpec((rows, HEAD_DIM), lambda h: (0, last_at + h))
    pair = pl.BlockSpec((2, rows, HEAD_DIM), lambda h: (0, 0, h))
    in_specs = (
        [smem, smem, small]
        + [gain_spec] * 2
        + [field_spec] * 2
        + [wide] * 7
        + [last_spec] * 3
    )
    operands = [flags, shares, inverse, *gains, *fields, grad, *gathered, *last]
    aliases = {}
    for position, array in enumerate(previous):
        aliases[len(operands)] = position
        operands.append(array)
        in_specs.append(pl.BlockSpec(memory_space=pl.ANY))
    back = jax.ShapeDtypeStruct((2, rows, heads * HEAD_DIM), bf16)
    keys = (CONTEXT + 1) * rows
    flops = 6 * 2 * rows * keys * HEAD_DIM * heads
    return pl.pallas_call(
        attention_body,
        grid=(heads,),
        in_specs=in_specs,
        out_specs=[wide] * 4 + [pair] * 3 + [small],
        out_shape=[
            jax.ShapeDtypeStruct((rows, width), bf16),
            jax.ShapeDtypeStruct((rows, width), f32),
            jax.ShapeDtypeStruct((rows, width), f32),
            jax.ShapeDtypeStruct((rows, width), f32),
            back,
            back,
            back,
            jax.ShapeDtypeStruct((8, rows), f32),
        ],
        scratch_shapes=[
            pltpu.VMEM((keys, rows), f32),
            pltpu.VMEM((keys, rows), f32),
            pltpu.VMEM((keys, HEAD_DIM), bf16),
            pltpu.VMEM((keys, HEAD_DIM), bf16),
            pltpu.VMEM((rows, HEAD_DIM), f32),
            pltpu.VMEM((rows, HEAD_DIM), f32),
        ],
        input_output_aliases=aliases,
        compiler_params=pltpu.CompilerParams(
            dimension_semantics=("arbitrary",), vmem_limit_bytes=VMEM_LIMIT
        ),
        cost_estimate=pl.CostEstimate(
            flops=flops, bytes_accessed=heads * 4 * 2**20, transcendentals=rows * keys * heads
        ),
    )(*operands)


def finish_body(
    flags, shares, rows_ref, gain_q, gain_k, clean, noise, grad_query, grad_key, grad_value,
    in_1, in_2, in_3, crossed, *refs
):
    out, cols = refs[-2:]
    f32 = jnp.float32
    keep, share = shares[0], shares[1]

    @pl.when(pl.program_id(0) == 0)
    def _():
        cols[...] = as_columns(rows_ref)

    clean_key = clean[1].astype(f32)
    noisy_query = keep * clean[0].astype(f32) + share * noise[0].astype(f32)
    noisy_key = keep * clean_key + share * noise[1].astype(f32)
    key_grad = crossed[0].astype(f32)
    value_grad = crossed[1].astype(f32)
    for hop, received in enumerate((in_1, in_2, in_3)):
        inside = flags[6 + hop] > 0
        key_grad = key_grad + jnp.where(inside, received[0], 0).astype(f32)
        value_grad = value_grad + jnp.where(inside, received[1], 0).astype(f32)
    col = lambda i: cols[:, i : i + 1]
    gk = gain_k[...]
    out[0] = keep * (col(0) * gain_q[...] * grad_query[...] - noisy_query * col(3))
    own = col(1) * gk * grad_key[...] - noisy_key * col(4)
    out[1] = keep * own + (col(2) * gk * key_grad - clean_key * col(5))
    out[2] = keep * grad_value[...] + value_grad


def finish_chunk(first, heads, flags, shares, factors, gains, fields, grads, received, crossed, previous):
    _, rows, width = fields[0].shape
    here = lambda h: (0, first + h)
    wide = pl.BlockSpec((rows, HEAD_DIM), here)
    gain_spec = pl.BlockSpec((1, HEAD_DIM), here)
    two = pl.BlockSpec((2, rows, HEAD_DIM), lambda h: (0, 0, first + h))
    pair = pl.BlockSpec((2, rows, HEAD_DIM), lambda h: (0, 0, h))
    smem = pl.BlockSpec(memory_space=pltpu.SMEM)
    operands = [flags, shares, factors, *gains, *fields, *grads, *received, crossed]
    in_specs = (
        [smem, smem, pl.BlockSpec((8, rows), lambda h: (0, 0))]
        + [gain_spec] * 2
        + [two] * 2
        + [wide] * 3
        + [pair] * 4
    )
    aliases = {}
    if previous is not None:
        aliases[len(operands)] = 0
        operands.append(previous)
        in_specs.append(pl.BlockSpec(memory_space=pl.ANY))
    return pl.pallas_call(
        finish_body,
        grid=(heads,),
        in_specs=in_specs,
        out_specs=pl.BlockSpec((3, rows, HEAD_DIM), lambda h: (0, 0, first + h)),
        out_shape=jax.ShapeDtypeStruct((3, rows, width), jnp.float32),
        scratch_shapes=[pltpu.VMEM((rows, HEAD_DIM), jnp.float32)],
        input_output_aliases=aliases,
        compiler_params=pltpu.CompilerParams(
            dimension_semantics=("arbitrary",), vmem_limit_bytes=VMEM_LIMIT
        ),
        cost_estimate=pl.CostEstimate(
            flops=rows * HEAD_DIM * heads * 30,
            bytes_accessed=heads * rows * HEAD_DIM * 48,
            transcendentals=0,
        ),
    )(*operands)


def head_sum(block):
    count = lax.axis_size("head")
    distance = 1
    while distance < count:
        route = [(i, i ^ distance) for i in range(count)]
        block = block + lax.ppermute(block, "head", route)
        distance *= 2
    return block


def after(value, *earlier):
    return lax.optimization_barrier((value, *earlier))[0]


def on_device(clean_qkv, noise_qkv, timestep, gain_q, gain_k, attended_grad):
    f32, bf16 = jnp.float32, jnp.bfloat16
    span = lax.axis_index("tm")
    column = span % COLUMNS
    steps = range(1, CONTEXT + 1)
    crossers = range(1, COLUMNS)
    value_clean = clean_qkv[2]

    def lanes(block, first, heads):
        return block[:, first * HEAD_DIM : (first + heads) * HEAD_DIM]

    def mixed(own, wrap):
        return [
            shift_columns(jnp.where(column + hop < COLUMNS, own, wrap), hop, "both")
            for hop in steps
        ]

    cross_values = shift_spans(value_clean, COLUMNS, crossers)
    first = [shift_columns(value_clean, hop, "inside") for hop in steps]

    noise_share = noise_share_of(timestep[0])
    shares = jnp.stack([1.0 - noise_share, noise_share])
    squares = prepare(shares, clean_qkv, noise_qkv)
    inverse = lax.rsqrt(head_sum(squares) / D + epsilon)
    key_clean = (clean_qkv[1].astype(f32) * inverse[2][:, None] * gain_k).astype(bf16)
    both = mixed(after(key_clean, *first), cross_values)
    cross_a = shift_spans(after(lanes(key_clean, 0, 2), cross_values), COLUMNS, crossers)
    cross_b = shift_spans(after(lanes(key_clean, 2, 3), cross_a), COLUMNS, crossers)
    last_a = [shift_columns(after(cross_a, *both), hop, "wrapped") for hop in steps]
    last_b = [shift_columns(after(cross_b, *last_a), hop, "wrapped") for hop in steps]

    hops = jnp.arange(1, CONTEXT + 1, dtype=jnp.int32)
    flags = jnp.concatenate([column >= hops, span >= hops, column + hops < COLUMNS]).astype(
        jnp.int32
    )
    gains = (gain_q[None, :], gain_k[None, :])
    fields = (clean_qkv, noise_qkv)

    def attend(head, heads, last, last_at, previous):
        out = attention_chunk(
            head, heads, flags, shares, inverse, gains, fields, attended_grad,
            (*first, *both), last, last_at, previous,
        )
        return out[:4], out[4:7], out[7]

    def send_back(blocks):
        return [shift_columns(block, -hop, "both") for hop, block in zip(steps, blocks)]

    def cross_back(received):
        total = jnp.zeros(received[0].shape, f32)
        for hop, block in zip(steps, received):
            total = total + jnp.where(column + hop >= COLUMNS, block, 0).astype(f32)
        return shift_spans(total.astype(bf16), -COLUMNS, crossers)

    results, back, inner_0 = attend(0, 2, last_a, 0, ())
    back_0 = send_back(back)
    crossed_0 = cross_back(back_0)
    results, kept, inner_1 = attend(2, 2, last_b, 0, results)
    results, back, inner_2 = attend(4, 1, last_b, 2, results)
    attended, *grads = results

    totals = head_sum(after(inner_0 + inner_1 + inner_2, *back_0)) / D
    high = lax.reduce_precision(totals[2:5], 8, 7)
    halves = jnp.stack([high, totals[2:5] - high]).reshape(2, CONTEXT, -1, 2 * HEAD_DIM)
    halves = jnp.pad(halves.astype(bf16), ((0, 0), (0, 0), (0, 14), (0, 0)))
    rows = attended_grad.shape[0]
    kept = [jnp.concatenate([block, halves[:, i]], axis=1) for i, block in enumerate(kept)]
    back_1 = send_back(after(tuple(kept), *back_0))
    crossed_1 = cross_back(back_1)
    back_2 = send_back(after(tuple(back), *back_1, crossed_0))
    crossed_2 = cross_back(after(tuple(back_2), crossed_1))

    def products_of(block):
        pieces = block[:, rows : rows + 2].astype(f32)
        return (pieces[0] + pieces[1]).reshape(-1)

    clean_inner = products_of(crossed_1)
    for hop, block in zip(steps, back_1):
        clean_inner = clean_inner + jnp.where(column + hop < COLUMNS, products_of(block), 0.0)
    cubes = jnp.stack(
        [
            inverse[0] ** 3 * totals[0],
            inverse[1] ** 3 * totals[1],
            inverse[2] ** 2 * clean_inner,
        ]
    )
    factors = jnp.concatenate([inverse[:3], cubes, cubes[:2]])
    clean_grads = None
    for head, heads, received, crossed in (
        (0, 2, back_0, crossed_0),
        (2, 2, back_1, crossed_1),
        (4, 1, back_2, crossed_2),
    ):
        clean_grads = finish_chunk(
            head, heads, flags, shares, factors, gains, fields, grads, received, crossed,
            clean_grads,
        )
    return (attended, clean_grads)


def solution(mesh):
    placed = (
        P(None, "tm", "head"),
        P(None, "tm", "head"),
        P("tm"),
        P("head"),
        P("head"),
        P("tm", "head"),
    )
    return jax.shard_map(
        on_device,
        mesh=mesh,
        in_specs=placed,
        out_specs=(P("tm", "head"), P(None, "tm", "head")),
        check_vma=False,
    )
```

time: 354 us -> 242 us (0.68)
  the two profiles are of different devices: /device:TPU:26 before, /device:TPU:70 now
where the time goes in v2:
time: 242 us
  waiting for transfers between devices  98.6 us (41%)
  starting transfers between devices  78 us (32%)
  Pallas kernels  49.8 us (21%)
  other arithmetic  8.41 us (3%)
  local copies, waits for them, and re-layouts  4.93 us (2%)
    ppermute x21, starting transfers between devices, shift_columns(): return lax.ppermute(block, 'tm', route)  48.4 us
    ppermute x21, waiting for transfers between devices, shift_columns(): return lax.ppermute(block, 'tm', route)  44.4 us
    pallas_call x3, Pallas kernels, attention_chunk(): pl.pallas_call(attention_body, grid=(heads,), in_specs=in_specs, out_spec...  33.5 us
    ppermute x6, waiting for transfers between devices, head_sum(): block = block + lax.ppermute(block, 'head', route)  33 us
    ppermute x6, starting transfers between devices, shift_spans(): return lax.ppermute(block, 'tm', route)  26.1 us
    ppermute x6, waiting for transfers between devices, shift_spans(): return lax.ppermute(block, 'tm', route)  21.2 us
    pallas_call x3, Pallas kernels, finish_chunk(): pl.pallas_call(finish_body, grid=(heads,), in_specs=in_specs, out_specs=p...  11.5 us
  transfers between devices with their start and end apart: 33, of which 20 were waited for; matrix products, arithmetic and copies ran while one was open for 3% of the time, Pallas kernels for 19%

profile of v2, /device:TPU:70, one launch (start us, length us, event | category | flops | bytes accessed | tf_op | source)
XLA Modules:
  0.0 241.6 jit_solution(11949412117270873571)
XLA Ops:
  0.6 1.1 slice_bitcast_fusion
  1.8 1.3 collective-permute-start.3
  3.1 1.3 collective-permute-start.4
  4.4 1.3 collective-permute-start.5
  5.7 7.3 %collective-permute-start.6 = (bf16[512,640]{1,0:T(8,128)(2,1)S(1)}, bf16[512,640]{1,0:T(8,128)(2,1)S(1)}, u32[]{:S(2)}, u32[]{:S(2)}) collective-permute-start(bf16[512,640]{1,0:T(8,128)(2,1)S(1)} %slice_bitcast_fusion), channel_id=1, source_target_pairs={{8,40},{16,48},{24,56},{40,72},{48,80},{56,88},{72,104},{80,112},{... | collective-permute-start | bytes 1966088 | tf_op jit(solution)/shard_map/ppermute | solution.py:39
  14.3 4.8 %shard_map.77 = f32[8,512]{1,0:T(8,128)} custom-call(f32[2]{0:T(128)} %pad_maximum_fusion.3.shares, bf16[3,512,640]{2,1,0:T(8,128)(2,1)} %clean.13, bf16[3,512,640]{2,1,0:T(8,128)(2,1)} %noise.13), custom_call_target="tpu_custom_call" | custom-call | flops 3932160 | bytes 2621440 | tf_op jit(solution)/shard_map/pallas_call | solution.py:86
  19.1 1.4 collective-permute-done
  21.2 1.0 collective-permute-start.1
  22.2 19.9 %collective-permute-done.1 = f32[8,512]{1,0:T(8,128)S(1)} collective-permute-done((f32[8,512]{1,0:T(8,128)S(1)}, f32[8,512]{1,0:T(8,128)S(1)}, u32[]{:S(2)}, u32[]{:S(2)}) %collective-permute-start.1) | collective-permute-done | bytes 16416 | tf_op jit(solution)/shard_map/ppermute | solution.py:344
  42.2 2.2 collective-permute-start.2
  44.4 2.5 %collective-permute-done.2 = f32[8,512]{1,0:T(8,128)S(1)} collective-permute-done((f32[8,512]{1,0:T(8,128)S(1)}, f32[8,512]{1,0:T(8,128)S(1)}, u32[]{:S(2)}, u32[]{:S(2)}) %collective-permute-start.2) | collective-permute-done | bytes 16416 | tf_op jit(solution)/shard_map/ppermute | solution.py:344
  46.9 1.3 fusion.1
  49.5 3.8 %collective-permute-start.8 = (bf16[512,640]{1,0:T(8,128)(2,1)S(1)}, bf16[512,640]{1,0:T(8,128)(2,1)S(1)}, u32[]{:S(2)}, u32[]{:S(2)}) collective-permute-start(bf16[512,640]{1,0:T(8,128)(2,1)S(1)} %get-tuple-element.81), channel_id=1, source_target_pairs={{0,16},{8,24},{16,0},{24,8},{32,48},{40,56},{48,32},{56,40},{64,80... | collective-permute-start | bytes 1966088 | tf_op jit(solution)/shard_map/ppermute | solution.py:51
  54.2 5.2 %collective-permute-start.10 = (bf16[512,256]{1,0:T(8,128)(2,1)S(1)}, bf16[512,256]{1,0:T(8,128)(2,1)S(1)}, u32[]{:S(2)}, u32[]{:S(2)}) collective-permute-start(bf16[512,256]{1,0:T(8,128)(2,1)S(1)} %slice.110), channel_id=1, source_target_pairs={{8,40},{16,48},{24,56},{40,72},{48,80},{56,88},{72,104},{80,112},{... | collective-permute-start | bytes 786440 | tf_op jit(solution)/shard_map/ppermute | solution.py:39
  59.5 8.0 %collective-permute-done.10 = bf16[512,256]{1,0:T(8,128)(2,1)S(1)} collective-permute-done((bf16[512,256]{1,0:T(8,128)(2,1)S(1)}, bf16[512,256]{1,0:T(8,128)(2,1)S(1)}, u32[]{:S(2)}, u32[]{:S(2)}) %collective-permute-start.10) | collective-permute-done | bytes 262176 | tf_op jit(solution)/shard_map/ppermute | solution.py:39
  67.5 9.6 %collective-permute-start.11 = (bf16[512,384]{1,0:T(8,128)(2,1)S(1)}, bf16[512,384]{1,0:T(8,128)(2,1)}, u32[]{:S(2)}, u32[]{:S(2)}) collective-permute-start(bf16[512,384]{1,0:T(8,128)(2,1)S(1)} %slice.109), channel_id=1, source_target_pairs={{8,40},{16,48},{24,56},{40,72},{48,80},{56,88},{72,104},{80,112},{... | collective-permute-start | bytes 1179656 | tf_op jit(solution)/shard_map/ppermute | solution.py:39
  77.1 3.7 %collective-permute-done.9.both_3 = bf16[512,640]{1,0:T(8,128)(2,1)S(1)} collective-permute-done((bf16[512,640]{1,0:T(8,128)(2,1)S(1)}, bf16[512,640]{1,0:T(8,128)(2,1)S(1)}, u32[]{:S(2)}, u32[]{:S(2)}) %collective-permute-start.9) | collective-permute-done | bytes 655392 | tf_op jit(solution)/shard_map/ppermute | solution.py:51
  80.9 2.8 %collective-permute-start.12 = (bf16[512,256]{1,0:T(8,128)(2,1)S(1)}, bf16[512,256]{1,0:T(8,128)(2,1)S(1)}, u32[]{:S(2)}, u32[]{:S(2)}) collective-permute-start(bf16[512,256]{1,0:T(8,128)(2,1)S(1)} %collective-permute-done.10), channel_id=1, source_target_pairs={{24,0},{56,32},{88,64},{120,96},{152,128},{184,160},{216,192},{248... | collective-permute-start | bytes 786440 | tf_op jit(solution)/shard_map/ppermute | solution.py:51
  83.7 2.5 %collective-permute-start.13 = (bf16[512,256]{1,0:T(8,128)(2,1)S(1)}, bf16[512,256]{1,0:T(8,128)(2,1)S(1)}, u32[]{:S(2)}, u32[]{:S(2)}) collective-permute-start(bf16[512,256]{1,0:T(8,128)(2,1)S(1)} %collective-permute-done.10), channel_id=1, source_target_pairs={{16,0},{24,8},{48,32},{56,40},{80,64},{88,72},{112,96},{120,104},{... | collective-permute-start | bytes 786440 | tf_op jit(solution)/shard_map/ppermute | solution.py:51
  86.1 1.6 collective-permute-start.14
  88.9 4.8 %collective-permute-done.12.last_1 = bf16[512,256]{1,0:T(8,128)(2,1)S(1)} collective-permute-done((bf16[512,256]{1,0:T(8,128)(2,1)S(1)}, bf16[512,256]{1,0:T(8,128)(2,1)S(1)}, u32[]{:S(2)}, u32[]{:S(2)}) %collective-permute-start.12) | collective-permute-done | bytes 262176 | tf_op jit(solution)/shard_map/ppermute | solution.py:51
  93.8 3.1 %collective-permute-done.14.last_3 = bf16[512,256]{1,0:T(8,128)(2,1)S(1)} collective-permute-done((bf16[512,256]{1,0:T(8,128)(2,1)S(1)}, bf16[512,256]{1,0:T(8,128)(2,1)S(1)}, u32[]{:S(2)}, u32[]{:S(2)}) %collective-permute-start.14) | collective-permute-done | bytes 262176 | tf_op jit(solution)/shard_map/ppermute | solution.py:51
  96.9 2.5 %collective-permute-start.15 = (bf16[512,384]{1,0:T(8,128)(2,1)}, bf16[512,384]{1,0:T(8,128)(2,1)S(1)}, u32[]{:S(2)}, u32[]{:S(2)}) collective-permute-start(bf16[512,384]{1,0:T(8,128)(2,1)} %collective-permute-done.11), channel_id=1, source_target_pairs={{24,0},{56,32},{88,64},{120,96},{152,128},{184,160},{216,192},{248... | collective-permute-start | bytes 1179656 | tf_op jit(solution)/shard_map/ppermute | solution.py:51
  99.4 4.5 %collective-permute-start.16 = (bf16[512,384]{1,0:T(8,128)(2,1)}, bf16[512,384]{1,0:T(8,128)(2,1)}, u32[]{:S(2)}, u32[]{:S(2)}) collective-permute-start(bf16[512,384]{1,0:T(8,128)(2,1)} %collective-permute-done.11), channel_id=1, source_target_pairs={{16,0},{24,8},{48,32},{56,40},{80,64},{88,72},{112,96},{120,104},{... | collective-permute-start | bytes 1179656 | tf_op jit(solution)/shard_map/ppermute | solution.py:51
  104.0 2.0 collective-permute-start.17
  106.6 13.0 %shard_map.78 = (bf16[512,640]{1,0:T(8,128)(2,1)}, f32[512,640]{1,0:T(8,128)}, f32[512,640]{1,0:T(8,128)}, f32[512,640]{1,0:T(8,128)}, bf16[2,512,256]{2,1,0:T(8...) custom-call(s32[9]{0:T(128)} %add_convert_fusion.3.flags, ...), custom_call_target="tpu_custom_call" | custom-call | flops 3221225472 | bytes 8388608 | tf_op jit(solution)/shard_map/pallas_call | solution.py:237
  120.8 3.1 %collective-permute-start.20 = (bf16[2,512,256]{2,1,0:T(8,128)(2,1)}, bf16[2,512,256]{2,1,0:T(8,128)(2,1)S(1)}, u32[]{:S(2)}, u32[]{:S(2)}) collective-permute-start(bf16[2,512,256]{2,1,0:T(8,128)(2,1)} %get-tuple-element.60), channel_id=1, source_target_pairs={{0,8},{8,16},{16,24},{24,0},{32,40},{40,48},{48,56},{56,32},{64,72... | collective-permute-start | bytes 1572872 | tf_op jit(solution)/shard_map/ppermute | solution.py:51
  123.9 13.0 %shard_map.79 = (bf16[512,640]{1,0:T(8,128)(2,1)}, f32[512,640]{1,0:T(8,128)}, f32[512,640]{1,0:T(8,128)}, f32[512,640]{1,0:T(8,128)}, bf16[2,512,256]{2,1,0:T(8...) custom-call(s32[9]{0:T(128)} %add_convert_fusion.3.flags, ...), custom_call_target="tpu_custom_call", output_to_operand_aliasing={{0}: (17, {}), {1}: (18, {}), {2}: (19, {}), {3}: (20, {})} | custom-call | flops 3221225472 | bytes 8388608 | tf_op jit(solution)/shard_map/pallas_call | solution.py:237
  137.0 7.4 %shard_map.80 = (bf16[512,640]{1,0:T(8,128)(2,1)}, f32[512,640]{1,0:T(8,128)}, f32[512,640]{1,0:T(8,128)}, f32[512,640]{1,0:T(8,128)}, bf16[2,512,128]{2,1,0:T(8...) custom-call(s32[9]{0:T(128)} %add_convert_fusion.3.flags, ...), custom_call_target="tpu_custom_call", output_to_operand_aliasing={{0}: (17, {}), {1}: (18, {}), {2}: (19, {}), {3}: (20, {})} | custom-call | flops 1610612736 | bytes 4194304 | tf_op jit(solution)/shard_map/pallas_call | solution.py:237
  146.6 1.2 collective-permute-done.21
  147.8 3.7 %collective-permute-done.22 = f32[8,512]{1,0:T(8,128)S(1)} collective-permute-done((f32[8,512]{1,0:T(8,128)S(1)}, f32[8,512]{1,0:T(8,128)S(1)}, u32[]{:S(2)}, u32[]{:S(2)}) %collective-permute-start.22) | collective-permute-done | bytes 16416 | tf_op jit(solution)/shard_map/ppermute | solution.py:344
  151.8 4.4 %collective-permute-done.23 = f32[8,512]{1,0:T(8,128)S(1)} collective-permute-done((f32[8,512]{1,0:T(8,128)S(1)}, f32[8,512]{1,0:T(8,128)S(1)}, u32[]{:S(2)}, u32[]{:S(2)}) %collective-permute-start.23) | collective-permute-done | bytes 16416 | tf_op jit(solution)/shard_map/ppermute | solution.py:344
  158.8 2.6 %collective-permute-start.26 = (bf16[2,528,256]{2,1,0:T(8,128)(2,1)}, bf16[2,528,256]{2,1,0:T(8,128)(2,1)S(1)}, u32[]{:S(2)}, u32[]{:S(2)}) collective-permute-start(bf16[2,528,256]{2,1,0:T(8,128)(2,1)} %pad_maximum_fusion.2), channel_id=1, source_target_pairs={{0,8},{8,16},{16,24},{24,0},{32,40},{40,48},{48,56},{56,32},{64,72... | collective-permute-start | bytes 1622024 | tf_op jit(solution)/shard_map/ppermute | solution.py:51
  162.6 1.4 collective-permute-start.28
  164.1 18.8 %collective-permute-done.26.in_3 = bf16[2,528,256]{2,1,0:T(8,128)(2,1)S(1)} collective-permute-done((bf16[2,528,256]{2,1,0:T(8,128)(2,1)}, bf16[2,528,256]{2,1,0:T(8,128)(2,1)S(1)}, u32[]{:S(2)}, u32[]{:S(2)}) %collective-permute-start.26) | collective-permute-done | bytes 540704 | tf_op jit(solution)/shard_map/ppermute | solution.py:51
  182.9 3.3 %collective-permute-done.24.in_1 = bf16[2,528,256]{2,1,0:T(8,128)(2,1)S(1)} collective-permute-done((bf16[2,528,256]{2,1,0:T(8,128)(2,1)}, bf16[2,528,256]{2,1,0:T(8,128)(2,1)S(1)}, u32[]{:S(2)}, u32[]{:S(2)}) %collective-permute-start.24) | collective-permute-done | bytes 540704 | tf_op jit(solution)/shard_map/ppermute | solution.py:51
  186.5 1.3 collective-permute-start.27
  187.8 2.9 %collective-permute-done.28.crossed = bf16[2,512,256]{2,1,0:T(8,128)(2,1)S(1)} collective-permute-done((bf16[2,512,256]{2,1,0:T(8,128)(2,1)S(1)}, bf16[2,512,256]{2,1,0:T(8,128)(2,1)S(1)}, u32[]{:S(2)}, u32[]{:S(2)}) %collective-permute-start.28) | collective-permute-done | bytes 524320 | tf_op jit(solution)/shard_map/ppermute | solution.py:39
  190.7 14.0 %collective-permute-start.29 = (bf16[2,512,128]{2,1,0:T(8,128)(2,1)S(1)}, bf16[2,512,128]{2,1,0:T(8,128)(2,1)S(1)}, u32[]{:S(2)}, u32[]{:S(2)}) collective-permute-start(bf16[2,512,128]{2,1,0:T(8,128)(2,1)S(1)} %copy-done.29), channel_id=1, source_target_pairs={{0,24},{8,0},{16,8},{24,16},{32,56},{40,32},{48,40},{56,48},{64,88... | collective-permute-start | bytes 786440 | tf_op jit(solution)/shard_map/ppermute | solution.py:51
  204.7 2.8 %collective-permute-start.31 = (bf16[2,512,128]{2,1,0:T(8,128)(2,1)S(1)}, bf16[2,512,128]{2,1,0:T(8,128)(2,1)S(1)}, u32[]{:S(2)}, u32[]{:S(2)}) collective-permute-start(bf16[2,512,128]{2,1,0:T(8,128)(2,1)S(1)} %copy-done.27), channel_id=1, source_target_pairs={{0,8},{8,16},{16,24},{24,0},{32,40},{40,48},{48,56},{56,32},{64,72... | collective-permute-start | bytes 786440 | tf_op jit(solution)/shard_map/ppermute | solution.py:51
  207.5 3.9 %collective-permute-done.29.in_1 = bf16[2,512,128]{2,1,0:T(8,128)(2,1)S(1)} collective-permute-done((bf16[2,512,128]{2,1,0:T(8,128)(2,1)S(1)}, bf16[2,512,128]{2,1,0:T(8,128)(2,1)S(1)}, u32[]{:S(2)}, u32[]{:S(2)}) %collective-permute-start.29) | collective-permute-done | bytes 262176 | tf_op jit(solution)/shard_map/ppermute | solution.py:51
  211.4 4.6 %collective-permute-done.30.in_2 = bf16[2,512,128]{2,1,0:T(8,128)(2,1)S(1)} collective-permute-done((bf16[2,512,128]{2,1,0:T(8,128)(2,1)S(1)}, bf16[2,512,128]{2,1,0:T(8,128)(2,1)S(1)}, u32[]{:S(2)}, u32[]{:S(2)}) %collective-permute-start.30) | collective-permute-done | bytes 262176 | tf_op jit(solution)/shard_map/ppermute | solution.py:51
  216.8 6.2 %collective-permute-done.27.crossed = bf16[2,528,256]{2,1,0:T(8,128)(2,1)S(1)} collective-permute-done((bf16[2,528,256]{2,1,0:T(8,128)(2,1)S(1)}, bf16[2,528,256]{2,1,0:T(8,128)(2,1)S(1)}, u32[]{:S(2)}, u32[]{:S(2)}) %collective-permute-start.27) | collective-permute-done | bytes 540704 | tf_op jit(solution)/shard_map/ppermute | solution.py:39
  224.0 1.3 collective-permute-start.32
  226.0 4.2 %shard_map.81.refs_0_ = f32[3,512,640]{2,1,0:T(8,128)} custom-call(s32[9]{0:T(128)} %add_convert_fusion.3.flags, f32[2]{0:T(128)} %pad_maximum_fusion.3.shares, f32[8,512]{1,0:T(8,128)} %concatenate.24.rows_ref, f32[1,640]{1,0:T(1,128)} %broadcast_in_dim.31.gain_q, f32[1,640]{1,0:T(1,128)} %broadcast_in_dim.32.gain_k, bf16[3,512,640]{2,1,0:T(8,128)(2,1)} %clean.13, ...), custom_call_target="tpu_custom_call" | custom-call | flops 3932160 | bytes 6291456 | tf_op jit(solution)/shard_map/pallas_call | solution.py:320
  230.3 4.0 %shard_map.82.refs_0_ = f32[3,512,640]{2,1,0:T(8,128)} custom-call(s32[9]{0:T(128)} %add_convert_fusion.3.flags, f32[2]{0:T(128)} %pad_maximum_fusion.3.shares, f32[8,512]{1,0:T(8,128)} %concatenate.24.rows_ref, f32[1,640]{1,0:T(1,128)} %broadcast_in_dim.31.gain_q, f32[1,640]{1,0:T(1,128)} %broadcast_in_dim.32.gain_k, ...), custom_call_target="tpu_custom_call", output_to_operand_aliasing={{}: (14, {})} | custom-call | flops 3932160 | bytes 6291456 | tf_op jit(solution)/shard_map/pallas_call | solution.py:320
  234.3 4.1 %collective-permute-done.32.crossed = bf16[2,512,128]{2,1,0:T(8,128)(2,1)} collective-permute-done((bf16[2,512,128]{2,1,0:T(8,128)(2,1)}, bf16[2,512,128]{2,1,0:T(8,128)(2,1)}, u32[]{:S(2)}, u32[]{:S(2)}) %collective-permute-start.32) | collective-permute-done | bytes 262176 | tf_op jit(solution)/shard_map/ppermute | solution.py:39
  238.3 3.2 %shard_map.83 = f32[3,512,640]{2,1,0:T(8,128)} custom-call(s32[9]{0:T(128)} %add_convert_fusion.3.flags, f32[2]{0:T(128)} %pad_maximum_fusion.3.shares, f32[8,512]{1,0:T(8,128)} %concatenate.24.rows_ref, f32[1,640]{1,0:T(1,128)} %broadcast_in_dim.31.gain_q, f32[1,640]{1,0:T(1,128)} %broadcast_in_dim.32.gain_k, ...), custom_call_target="tpu_custom_call", output_to_operand_aliasing={{}: (14, {})} | custom-call | flops 1966080 | bytes 3145728 | tf_op jit(solution)/shard_map/pallas_call | solution.py:320
  (131 shorter events, 15.5 us)
Async XLA Ops:
  1.8 46.4 %collective-permute-start.3 = (bf16[512,640]{1,0:T(8,128)(2,1)S(1)}, bf16[512,640]{1,0:T(8,128)(2,1)S(1)}, u32[]{:S(2)}, u32[]{:S(2)}) collective-permute-start(bf16[512,640]{1,0:T(8,128)(2,1)S(1)} %slice_bitcast_fusion), channel_id=1, source_target_pairs={{0,8},{8,16},{16,24},{32,40},{40,48},{48,56},{64,72},{72,80},{80,8... | collective-permute-start | bytes 1966088 | tf_op jit(solution)/shard_map/ppermute | solution.py:51
  3.1 45.1 %collective-permute-start.4 = (bf16[512,640]{1,0:T(8,128)(2,1)S(1)}, bf16[512,640]{1,0:T(8,128)(2,1)S(1)}, u32[]{:S(2)}, u32[]{:S(2)}) collective-permute-start(bf16[512,640]{1,0:T(8,128)(2,1)S(1)} %slice_bitcast_fusion), channel_id=1, source_target_pairs={{0,16},{8,24},{32,48},{40,56},{64,80},{72,88},{96,112},{104,120},{... | collective-permute-start | bytes 1966088 | tf_op jit(solution)/shard_map/ppermute | solution.py:51
  4.4 43.9 %collective-permute-start.5 = (bf16[512,640]{1,0:T(8,128)(2,1)S(1)}, bf16[512,640]{1,0:T(8,128)(2,1)S(1)}, u32[]{:S(2)}, u32[]{:S(2)}) collective-permute-start(bf16[512,640]{1,0:T(8,128)(2,1)S(1)} %slice_bitcast_fusion), channel_id=1, source_target_pairs={{0,24},{32,56},{64,88},{96,120},{128,152},{160,184},{192,216},{224... | collective-permute-start | bytes 1966088 | tf_op jit(solution)/shard_map/ppermute | solution.py:51
  5.7 42.6 %collective-permute-start.6 = (bf16[512,640]{1,0:T(8,128)(2,1)S(1)}, bf16[512,640]{1,0:T(8,128)(2,1)S(1)}, u32[]{:S(2)}, u32[]{:S(2)}) collective-permute-start(bf16[512,640]{1,0:T(8,128)(2,1)S(1)} %slice_bitcast_fusion), channel_id=1, source_target_pairs={{8,40},{16,48},{24,56},{40,72},{48,80},{56,88},{72,104},{80,112},{... | collective-permute-start | bytes 1966088 | tf_op jit(solution)/shard_map/ppermute | solution.py:39
  14.3 32.6 %copy-start.23 = (f32[640]{0:T(1024)S(1)}, f32[640]{0:T(1024)}, u32[]{:S(2)}) copy-start(f32[640]{0:T(1024)} %param.10) | copy-start | bytes 7684
  19.1 1.4 collective-permute-start
  21.2 21.0 %collective-permute-start.1 = (f32[8,512]{1,0:T(8,128)S(1)}, f32[8,512]{1,0:T(8,128)S(1)}, u32[]{:S(2)}, u32[]{:S(2)}) collective-permute-start(f32[8,512]{1,0:T(8,128)S(1)} %add.176), channel_id=1, source_target_pairs={{0,2},{1,3},{2,0},{3,1},{4,6},{5,7},{6,4},{7,5},{8,10},{9,11},{10,... | collective-permute-start | bytes 49160 | tf_op jit(solution)/shard_map/ppermute | solution.py:344
  42.2 4.6 %collective-permute-start.2 = (f32[8,512]{1,0:T(8,128)S(1)}, f32[8,512]{1,0:T(8,128)S(1)}, u32[]{:S(2)}, u32[]{:S(2)}) collective-permute-start(f32[8,512]{1,0:T(8,128)S(1)} %add.177), channel_id=1, source_target_pairs={{0,4},{1,5},{2,6},{3,7},{4,0},{5,1},{6,2},{7,3},{8,12},{9,13},{10,... | collective-permute-start | bytes 49160 | tf_op jit(solution)/shard_map/ppermute | solution.py:344
  49.5 38.8 %copy-start.26 = (f32[640]{0:T(1024)S(1)}, f32[640]{0:T(1024)}, u32[]{:S(2)}) copy-start(f32[640]{0:T(1024)} %param.9) | copy-start | bytes 7684
  49.5 27.6 %collective-permute-start.7 = (bf16[512,640]{1,0:T(8,128)(2,1)S(1)}, bf16[512,640]{1,0:T(8,128)(2,1)S(1)}, u32[]{:S(2)}, u32[]{:S(2)}) collective-permute-start(bf16[512,640]{1,0:T(8,128)(2,1)S(1)} %get-tuple-element.82), channel_id=1, source_target_pairs={{0,8},{8,16},{16,24},{24,0},{32,40},{40,48},{48,56},{56,32},{64,72... | collective-permute-start | bytes 1966088 | tf_op jit(solution)/shard_map/ppermute | solution.py:51
  49.5 27.6 %collective-permute-start.8 = (bf16[512,640]{1,0:T(8,128)(2,1)S(1)}, bf16[512,640]{1,0:T(8,128)(2,1)S(1)}, u32[]{:S(2)}, u32[]{:S(2)}) collective-permute-start(bf16[512,640]{1,0:T(8,128)(2,1)S(1)} %get-tuple-element.81), channel_id=1, source_target_pairs={{0,16},{8,24},{16,0},{24,8},{32,48},{40,56},{48,32},{56,40},{64,80... | collective-permute-start | bytes 1966088 | tf_op jit(solution)/shard_map/ppermute | solution.py:51
  53.3 27.5 %collective-permute-start.9 = (bf16[512,640]{1,0:T(8,128)(2,1)S(1)}, bf16[512,640]{1,0:T(8,128)(2,1)S(1)}, u32[]{:S(2)}, u32[]{:S(2)}) collective-permute-start(bf16[512,640]{1,0:T(8,128)(2,1)S(1)} %get-tuple-element.80), channel_id=1, source_target_pairs={{0,24},{8,0},{16,8},{24,16},{32,56},{40,32},{48,40},{56,48},{64,88... | collective-permute-start | bytes 1966088 | tf_op jit(solution)/shard_map/ppermute | solution.py:51
  54.2 13.3 %collective-permute-start.10 = (bf16[512,256]{1,0:T(8,128)(2,1)S(1)}, bf16[512,256]{1,0:T(8,128)(2,1)S(1)}, u32[]{:S(2)}, u32[]{:S(2)}) collective-permute-start(bf16[512,256]{1,0:T(8,128)(2,1)S(1)} %slice.110), channel_id=1, source_target_pairs={{8,40},{16,48},{24,56},{40,72},{48,80},{56,88},{72,104},{80,112},{... | collective-permute-start | bytes 786440 | tf_op jit(solution)/shard_map/ppermute | solution.py:39
  67.5 21.4 %collective-permute-start.11 = (bf16[512,384]{1,0:T(8,128)(2,1)S(1)}, bf16[512,384]{1,0:T(8,128)(2,1)}, u32[]{:S(2)}, u32[]{:S(2)}) collective-permute-start(bf16[512,384]{1,0:T(8,128)(2,1)S(1)} %slice.109), channel_id=1, source_target_pairs={{8,40},{16,48},{24,56},{40,72},{48,80},{56,88},{72,104},{80,112},{... | collective-permute-start | bytes 1179656 | tf_op jit(solution)/shard_map/ppermute | solution.py:39
  77.1 29.5 %copy-start.3 = (bf16[512,640]{1,0:T(8,128)(2,1)}, bf16[512,640]{1,0:T(8,128)(2,1)S(1)}, u32[]{:S(2)}) copy-start(bf16[512,640]{1,0:T(8,128)(2,1)S(1)} %collective-permute-done.7.both_1) | copy-start | bytes 1966084
  77.1 29.5 %copy-start.4 = (bf16[512,640]{1,0:T(8,128)(2,1)}, bf16[512,640]{1,0:T(8,128)(2,1)S(1)}, u32[]{:S(2)}) copy-start(bf16[512,640]{1,0:T(8,128)(2,1)S(1)} %collective-permute-done.8.both_2) | copy-start | bytes 1966084
  80.9 25.8 %copy-start.5 = (bf16[512,640]{1,0:T(8,128)(2,1)}, bf16[512,640]{1,0:T(8,128)(2,1)S(1)}, u32[]{:S(2)}) copy-start(bf16[512,640]{1,0:T(8,128)(2,1)S(1)} %collective-permute-done.9.both_3) | copy-start | bytes 1966084
  80.9 12.9 %collective-permute-start.12 = (bf16[512,256]{1,0:T(8,128)(2,1)S(1)}, bf16[512,256]{1,0:T(8,128)(2,1)S(1)}, u32[]{:S(2)}, u32[]{:S(2)}) collective-permute-start(bf16[512,256]{1,0:T(8,128)(2,1)S(1)} %collective-permute-done.10), channel_id=1, source_target_pairs={{24,0},{56,32},{88,64},{120,96},{152,128},{184,160},{216,192},{248... | collective-permute-start | bytes 786440 | tf_op jit(solution)/shard_map/ppermute | solution.py:51
  83.7 10.1 %collective-permute-start.13 = (bf16[512,256]{1,0:T(8,128)(2,1)S(1)}, bf16[512,256]{1,0:T(8,128)(2,1)S(1)}, u32[]{:S(2)}, u32[]{:S(2)}) collective-permute-start(bf16[512,256]{1,0:T(8,128)(2,1)S(1)} %collective-permute-done.10), channel_id=1, source_target_pairs={{16,0},{24,8},{48,32},{56,40},{80,64},{88,72},{112,96},{120,104},{... | collective-permute-start | bytes 786440 | tf_op jit(solution)/shard_map/ppermute | solution.py:51
  86.1 10.7 %collective-permute-start.14 = (bf16[512,256]{1,0:T(8,128)(2,1)S(1)}, bf16[512,256]{1,0:T(8,128)(2,1)S(1)}, u32[]{:S(2)}, u32[]{:S(2)}) collective-permute-start(bf16[512,256]{1,0:T(8,128)(2,1)S(1)} %collective-permute-done.10), channel_id=1, source_target_pairs={{8,0},{16,8},{24,16},{40,32},{48,40},{56,48},{72,64},{80,72},{88,8... | collective-permute-start | bytes 786440 | tf_op jit(solution)/shard_map/ppermute | solution.py:51
  96.9 23.2 %collective-permute-start.15 = (bf16[512,384]{1,0:T(8,128)(2,1)}, bf16[512,384]{1,0:T(8,128)(2,1)S(1)}, u32[]{:S(2)}, u32[]{:S(2)}) collective-permute-start(bf16[512,384]{1,0:T(8,128)(2,1)} %collective-permute-done.11), channel_id=1, source_target_pairs={{24,0},{56,32},{88,64},{120,96},{152,128},{184,160},{216,192},{248... | collective-permute-start | bytes 1179656 | tf_op jit(solution)/shard_map/ppermute | solution.py:51
  99.4 24.5 %collective-permute-start.16 = (bf16[512,384]{1,0:T(8,128)(2,1)}, bf16[512,384]{1,0:T(8,128)(2,1)}, u32[]{:S(2)}, u32[]{:S(2)}) collective-permute-start(bf16[512,384]{1,0:T(8,128)(2,1)} %collective-permute-done.11), channel_id=1, source_target_pairs={{16,0},{24,8},{48,32},{56,40},{80,64},{88,72},{112,96},{120,104},{... | collective-permute-start | bytes 1179656 | tf_op jit(solution)/shard_map/ppermute | solution.py:51
  104.0 20.0 %collective-permute-start.17 = (bf16[512,384]{1,0:T(8,128)(2,1)}, bf16[512,384]{1,0:T(8,128)(2,1)}, u32[]{:S(2)}, u32[]{:S(2)}) collective-permute-start(bf16[512,384]{1,0:T(8,128)(2,1)} %collective-permute-done.11), channel_id=1, source_target_pairs={{8,0},{16,8},{24,16},{40,32},{48,40},{56,48},{72,64},{80,72},{88,8... | collective-permute-start | bytes 1179656 | tf_op jit(solution)/shard_map/ppermute | solution.py:51
  119.7 26.3 %collective-permute-start.18 = (bf16[2,512,256]{2,1,0:T(8,128)(2,1)}, bf16[2,512,256]{2,1,0:T(8,128)(2,1)S(1)}, u32[]{:S(2)}, u32[]{:S(2)}) collective-permute-start(bf16[2,512,256]{2,1,0:T(8,128)(2,1)} %get-tuple-element.58), channel_id=1, source_target_pairs={{0,24},{8,0},{16,8},{24,16},{32,56},{40,32},{48,40},{56,48},{64,88... | collective-permute-start | bytes 1572872 | tf_op jit(solution)/shard_map/ppermute | solution.py:51
  119.9 26.0 %collective-permute-start.19 = (bf16[2,512,256]{2,1,0:T(8,128)(2,1)}, bf16[2,512,256]{2,1,0:T(8,128)(2,1)S(1)}, u32[]{:S(2)}, u32[]{:S(2)}) collective-permute-start(bf16[2,512,256]{2,1,0:T(8,128)(2,1)} %get-tuple-element.59), channel_id=1, source_target_pairs={{0,16},{8,24},{16,0},{24,8},{32,48},{40,56},{48,32},{56,40},{64,80... | collective-permute-start | bytes 1572872 | tf_op jit(solution)/shard_map/ppermute | solution.py:51
  120.8 25.8 %collective-permute-start.20 = (bf16[2,512,256]{2,1,0:T(8,128)(2,1)}, bf16[2,512,256]{2,1,0:T(8,128)(2,1)S(1)}, u32[]{:S(2)}, u32[]{:S(2)}) collective-permute-start(bf16[2,512,256]{2,1,0:T(8,128)(2,1)} %get-tuple-element.60), channel_id=1, source_target_pairs={{0,8},{8,16},{16,24},{24,0},{32,40},{40,48},{48,56},{56,32},{64,72... | collective-permute-start | bytes 1572872 | tf_op jit(solution)/shard_map/ppermute | solution.py:51
  137.0 19.2 %copy-start.20 = (bf16[2,512,256]{2,1,0:T(8,128)(2,1)S(1)}, bf16[2,512,256]{2,1,0:T(8,128)(2,1)}, u32[]{:S(2)}) copy-start(bf16[2,512,256]{2,1,0:T(8,128)(2,1)} %get-tuple-element.62) | copy-start | bytes 1572868
  146.6 1.2 collective-permute-start.21
  147.8 3.7 %collective-permute-start.22 = (f32[8,512]{1,0:T(8,128)S(1)}, f32[8,512]{1,0:T(8,128)S(1)}, u32[]{:S(2)}, u32[]{:S(2)}) collective-permute-start(f32[8,512]{1,0:T(8,128)S(1)} %add.186), channel_id=1, source_target_pairs={{0,2},{1,3},{2,0},{3,1},{4,6},{5,7},{6,4},{7,5},{8,10},{9,11},{10,... | collective-permute-start | bytes 49160 | tf_op jit(solution)/shard_map/ppermute | solution.py:344
  151.5 4.6 %collective-permute-start.23 = (f32[8,512]{1,0:T(8,128)S(1)}, f32[8,512]{1,0:T(8,128)S(1)}, u32[]{:S(2)}, u32[]{:S(2)}) collective-permute-start(f32[8,512]{1,0:T(8,128)S(1)} %add.187), channel_id=1, source_target_pairs={{0,4},{1,5},{2,6},{3,7},{4,0},{5,1},{6,2},{7,3},{8,12},{9,13},{10,... | collective-permute-start | bytes 49160 | tf_op jit(solution)/shard_map/ppermute | solution.py:344
  158.8 24.1 %collective-permute-start.26 = (bf16[2,528,256]{2,1,0:T(8,128)(2,1)}, bf16[2,528,256]{2,1,0:T(8,128)(2,1)S(1)}, u32[]{:S(2)}, u32[]{:S(2)}) collective-permute-start(bf16[2,528,256]{2,1,0:T(8,128)(2,1)} %pad_maximum_fusion.2), channel_id=1, source_target_pairs={{0,8},{8,16},{16,24},{24,0},{32,40},{40,48},{48,56},{56,32},{64,72... | collective-permute-start | bytes 1622024 | tf_op jit(solution)/shard_map/ppermute | solution.py:51
  161.4 21.5 %collective-permute-start.25 = (bf16[2,528,256]{2,1,0:T(8,128)(2,1)}, bf16[2,528,256]{2,1,0:T(8,128)(2,1)S(1)}, u32[]{:S(2)}, u32[]{:S(2)}) collective-permute-start(bf16[2,528,256]{2,1,0:T(8,128)(2,1)} %pad_maximum_fusion.1), channel_id=1, source_target_pairs={{0,16},{8,24},{16,0},{24,8},{32,48},{40,56},{48,32},{56,40},{64,80... | collective-permute-start | bytes 1622024 | tf_op jit(solution)/shard_map/ppermute | solution.py:51
  161.4 24.8 %collective-permute-start.24 = (bf16[2,528,256]{2,1,0:T(8,128)(2,1)}, bf16[2,528,256]{2,1,0:T(8,128)(2,1)S(1)}, u32[]{:S(2)}, u32[]{:S(2)}) collective-permute-start(bf16[2,528,256]{2,1,0:T(8,128)(2,1)} %pad_maximum_fusion), channel_id=1, source_target_pairs={{0,24},{8,0},{16,8},{24,16},{32,56},{40,32},{48,40},{56,48},{64,88... | collective-permute-start | bytes 1622024 | tf_op jit(solution)/shard_map/ppermute | solution.py:51
  162.6 28.1 %copy-start.29 = (bf16[2,512,128]{2,1,0:T(8,128)(2,1)S(1)}, bf16[2,512,128]{2,1,0:T(8,128)(2,1)}, u32[]{:S(2)}) copy-start(bf16[2,512,128]{2,1,0:T(8,128)(2,1)} %get-tuple-element.74) | copy-start | bytes 786436
  162.6 42.1 %copy-start.28 = (bf16[2,512,128]{2,1,0:T(8,128)(2,1)S(1)}, bf16[2,512,128]{2,1,0:T(8,128)(2,1)}, u32[]{:S(2)}) copy-start(bf16[2,512,128]{2,1,0:T(8,128)(2,1)} %get-tuple-element.75) | copy-start | bytes 786436
  162.6 42.1 %copy-start.27 = (bf16[2,512,128]{2,1,0:T(8,128)(2,1)S(1)}, bf16[2,512,128]{2,1,0:T(8,128)(2,1)}, u32[]{:S(2)}) copy-start(bf16[2,512,128]{2,1,0:T(8,128)(2,1)} %get-tuple-element.76) | copy-start | bytes 786436
  162.6 28.0 %collective-permute-start.28 = (bf16[2,512,256]{2,1,0:T(8,128)(2,1)S(1)}, bf16[2,512,256]{2,1,0:T(8,128)(2,1)S(1)}, u32[]{:S(2)}, u32[]{:S(2)}) collective-permute-start(bf16[2,512,256]{2,1,0:T(8,128)(2,1)S(1)} %add_convert_fusion.1), channel_id=1, source_target_pairs={{40,8},{48,16},{56,24},{72,40},{80,48},{88,56},{104,72},{112,80},{... | collective-permute-start | bytes 1572872 | tf_op jit(solution)/shard_map/ppermute | solution.py:39
  164.1 61.3 %copy-start.22 = (f32[8,512]{1,0:T(8,128)S(1)}, f32[8,512]{1,0:T(8,128)}, u32[]{:S(2)}) copy-start(f32[8,512]{1,0:T(8,128)} %copy-done.21) | copy-start | bytes 49156
  164.1 61.3 %slice-start = ((f32[8,512]{1,0:T(8,128)}), f32[3,512]{1,0:T(4,128)S(1)}, s32[]{:S(2)}) async-start(f32[8,512]{1,0:T(8,128)} %copy-done.21), calls=%async_computation | async-start | bytes 16384 | tf_op jit(solution)/shard_map/slice | solution.py:439
  182.9 41.1 %copy-start.6 = (bf16[2,528,256]{2,1,0:T(8,128)(2,1)}, bf16[2,528,256]{2,1,0:T(8,128)(2,1)S(1)}, u32[]{:S(2)}) copy-start(bf16[2,528,256]{2,1,0:T(8,128)(2,1)S(1)} %collective-permute-done.26.in_3) | copy-start | bytes 1622020
  182.9 41.1 %copy-start.7 = (bf16[2,528,256]{2,1,0:T(8,128)(2,1)}, bf16[2,528,256]{2,1,0:T(8,128)(2,1)S(1)}, u32[]{:S(2)}) copy-start(bf16[2,528,256]{2,1,0:T(8,128)(2,1)S(1)} %collective-permute-done.25.in_2) | copy-start | bytes 1622020
  186.2 37.8 %copy-start.8 = (bf16[2,528,256]{2,1,0:T(8,128)(2,1)}, bf16[2,528,256]{2,1,0:T(8,128)(2,1)S(1)}, u32[]{:S(2)}) copy-start(bf16[2,528,256]{2,1,0:T(8,128)(2,1)S(1)} %collective-permute-done.24.in_1) | copy-start | bytes 1622020
  186.5 36.6 %collective-permute-start.27 = (bf16[2,528,256]{2,1,0:T(8,128)(2,1)S(1)}, bf16[2,528,256]{2,1,0:T(8,128)(2,1)S(1)}, u32[]{:S(2)}, u32[]{:S(2)}) collective-permute-start(bf16[2,528,256]{2,1,0:T(8,128)(2,1)S(1)} %add_convert_fusion), channel_id=1, source_target_pairs={{40,8},{48,16},{56,24},{72,40},{80,48},{88,56},{104,72},{112,80},{... | collective-permute-start | bytes 1622024 | tf_op jit(solution)/shard_map/ppermute | solution.py:39
  190.7 35.3 %copy-start.17 = (bf16[2,512,256]{2,1,0:T(8,128)(2,1)}, bf16[2,512,256]{2,1,0:T(8,128)(2,1)S(1)}, u32[]{:S(2)}) copy-start(bf16[2,512,256]{2,1,0:T(8,128)(2,1)S(1)} %collective-permute-done.28.crossed) | copy-start | bytes 1572868
  190.7 20.7 %collective-permute-start.29 = (bf16[2,512,128]{2,1,0:T(8,128)(2,1)S(1)}, bf16[2,512,128]{2,1,0:T(8,128)(2,1)S(1)}, u32[]{:S(2)}, u32[]{:S(2)}) collective-permute-start(bf16[2,512,128]{2,1,0:T(8,128)(2,1)S(1)} %copy-done.29), channel_id=1, source_target_pairs={{0,24},{8,0},{16,8},{24,16},{32,56},{40,32},{48,40},{56,48},{64,88... | collective-permute-start | bytes 786440 | tf_op jit(solution)/shard_map/ppermute | solution.py:51
  204.7 11.3 %collective-permute-start.30 = (bf16[2,512,128]{2,1,0:T(8,128)(2,1)S(1)}, bf16[2,512,128]{2,1,0:T(8,128)(2,1)S(1)}, u32[]{:S(2)}, u32[]{:S(2)}) collective-permute-start(bf16[2,512,128]{2,1,0:T(8,128)(2,1)S(1)} %copy-done.28), channel_id=1, source_target_pairs={{0,16},{8,24},{16,0},{24,8},{32,48},{40,56},{48,32},{56,40},{64,80... | collective-permute-start | bytes 786440 | tf_op jit(solution)/shard_map/ppermute | solution.py:51
  204.7 12.1 %collective-permute-start.31 = (bf16[2,512,128]{2,1,0:T(8,128)(2,1)S(1)}, bf16[2,512,128]{2,1,0:T(8,128)(2,1)S(1)}, u32[]{:S(2)}, u32[]{:S(2)}) collective-permute-start(bf16[2,512,128]{2,1,0:T(8,128)(2,1)S(1)} %copy-done.27), channel_id=1, source_target_pairs={{0,8},{8,16},{16,24},{24,0},{32,40},{40,48},{48,56},{56,32},{64,72... | collective-permute-start | bytes 786440 | tf_op jit(solution)/shard_map/ppermute | solution.py:51
  224.0 14.3 %collective-permute-start.32 = (bf16[2,512,128]{2,1,0:T(8,128)(2,1)}, bf16[2,512,128]{2,1,0:T(8,128)(2,1)}, u32[]{:S(2)}, u32[]{:S(2)}) collective-permute-start(bf16[2,512,128]{2,1,0:T(8,128)(2,1)} %add_convert_fusion.2), channel_id=1, source_target_pairs={{40,8},{48,16},{56,24},{72,40},{80,48},{88,56},{104,72},{112,80},{... | collective-permute-start | bytes 786440 | tf_op jit(solution)/shard_map/ppermute | solution.py:39
  (19 other events, 184.1 us)

commit v3 on v2

--- a/solution.py
+++ b/solution.py
@@ -11,7 +11,7 @@
 HEAD_DIM = 128
 CONTEXT = 3
 COLUMNS = 4
-KEY_TILE = 256
+KEY_TILE = 512
 VMEM_LIMIT = 60 * 2**20
 
 epsilon = 1e-06
@@ -207,7 +207,7 @@
         inner[...] = products[...].T[0:8]
 
 
-def attention_chunk(first, heads, flags, shares, inverse, gains, fields, grad, gathered, last, last_at, previous):
+def attention_chunk(first, heads, flags, shares, inverse, gains, fields, grad, gathered, last, last_at, spare, previous):
     rows, width = grad.shape
     here = lambda h: (0, first + h)
     f32, bf16 = jnp.float32, jnp.bfloat16
@@ -231,7 +231,7 @@
         aliases[len(operands)] = position
         operands.append(array)
         in_specs.append(pl.BlockSpec(memory_space=pl.ANY))
-    back = jax.ShapeDtypeStruct((2, rows, heads * HEAD_DIM), bf16)
+    back = jax.ShapeDtypeStruct((2, rows + spare, heads * HEAD_DIM), bf16)
     keys = (CONTEXT + 1) * rows
     flops = 6 * 2 * rows * keys * HEAD_DIM * heads
     return pl.pallas_call(
@@ -379,7 +379,7 @@
     cross_a = shift_spans(after(lanes(key_clean, 0, 2), cross_values), COLUMNS, crossers)
     cross_b = shift_spans(after(lanes(key_clean, 2, 3), cross_a), COLUMNS, crossers)
     last_a = [shift_columns(after(cross_a, *both), hop, "wrapped") for hop in steps]
-    last_b = [shift_columns(after(cross_b, *last_a), hop, "wrapped") for hop in steps]
+    last_b = [shift_columns(after(cross_b, *both), hop, "wrapped") for hop in steps]
 
     hops = jnp.arange(1, CONTEXT + 1, dtype=jnp.int32)
     flags = jnp.concatenate([column >= hops, span >= hops, column + hops < COLUMNS]).astype(
@@ -388,10 +388,10 @@
     gains = (gain_q[None, :], gain_k[None, :])
     fields = (clean_qkv, noise_qkv)
 
-    def attend(head, heads, last, last_at, previous):
+    def attend(head, heads, last, last_at, spare, previous):
         out = attention_chunk(
             head, heads, flags, shares, inverse, gains, fields, attended_grad,
-            (*first, *both), last, last_at, previous,
+            (*first, *both), last, last_at, spare, previous,
         )
         return out[:4], out[4:7], out[7]
 
@@ -404,11 +404,11 @@
             total = total + jnp.where(column + hop >= COLUMNS, block, 0).astype(f32)
         return shift_spans(total.astype(bf16), -COLUMNS, crossers)
 
-    results, back, inner_0 = attend(0, 2, last_a, 0, ())
+    results, back, inner_0 = attend(0, 2, last_a, 0, 0, ())
     back_0 = send_back(back)
     crossed_0 = cross_back(back_0)
-    results, kept, inner_1 = attend(2, 2, last_b, 0, results)
-    results, back, inner_2 = attend(4, 1, last_b, 2, results)
+    results, kept, inner_1 = attend(2, 2, last_b, 0, 16, results)
+    results, back, inner_2 = attend(4, 1, last_b, 2, 0, results)
     attended, *grads = results
 
     totals = head_sum(after(inner_0 + inner_1 + inner_2, *back_0)) / D
@@ -416,11 +416,14 @@
     halves = jnp.stack([high, totals[2:5] - high]).reshape(2, CONTEXT, -1, 2 * HEAD_DIM)
     halves = jnp.pad(halves.astype(bf16), ((0, 0), (0, 0), (0, 14), (0, 0)))
     rows = attended_grad.shape[0]
-    kept = [jnp.concatenate([block, halves[:, i]], axis=1) for i, block in enumerate(kept)]
+    kept = [
+        lax.dynamic_update_slice(block, halves[:, i], (0, rows, 0))
+        for i, block in enumerate(kept)
+    ]
     back_1 = send_back(after(tuple(kept), *back_0))
     crossed_1 = cross_back(back_1)
     back_2 = send_back(after(tuple(back), *back_1, crossed_0))
-    crossed_2 = cross_back(after(tuple(back_2), crossed_1))
+    crossed_2 = cross_back(back_2)
 
     def products_of(block):
         pieces = block[:, rows : rows + 2].astype(f32)

time: 242 us -> 236 us (0.975)
  the two profiles are of different devices: /device:TPU:70 before, /device:TPU:26 now
where the time goes in v3:
time: 236 us; the launch traced here: 233 us
  waiting for transfers between devices  98.2 us (42%)
  starting transfers between devices  72.1 us (31%)
  Pallas kernels  47 us (20%)
  local copies, waits for them, and re-layouts  8.4 us (4%)
  other arithmetic  4.99 us (2%)
    ppermute x21, starting transfers between devices, shift_columns(): return lax.ppermute(block, 'tm', route)  43.4 us
    ppermute x21, waiting for transfers between devices, shift_columns(): return lax.ppermute(block, 'tm', route)  38.1 us
    ppermute x6, waiting for transfers between devices, head_sum(): block = block + lax.ppermute(block, 'head', route)  33.7 us
    pallas_call x3, Pallas kernels, attention_chunk(): pl.pallas_call(attention_body, grid=(heads,), in_specs=in_specs, out_spec...  30.8 us
    ppermute x6, waiting for transfers between devices, shift_spans(): return lax.ppermute(block, 'tm', route)  26.4 us
    ppermute x6, starting transfers between devices, shift_spans(): return lax.ppermute(block, 'tm', route)  25.4 us
    pallas_call x3, Pallas kernels, finish_chunk(): pl.pallas_call(finish_body, grid=(heads,), in_specs=in_specs, out_specs=p...  11.4 us
    pallas_call x1, Pallas kernels, prepare(): pl.pallas_call(prepare_body, grid=(width // HEAD_DIM,), in_specs=[pl.Bloc...  4.79 us
  transfers between devices with their start and end apart: 33, of which 16 were waited for; matrix products, arithmetic and copies ran while one was open for 3% of the time, Pallas kernels for 19%

profile of v3, /device:TPU:26, one launch (start us, length us, event | category | flops | bytes accessed | tf_op | source)
XLA Modules:
  0.0 232.7 jit_solution(17248173265024206486)
XLA Ops:
  0.6 1.1 slice_bitcast_fusion
  1.8 3.4 %collective-permute-start.3 = (bf16[512,640]{1,0:T(8,128)(2,1)S(1)}, bf16[512,640]{1,0:T(8,128)(2,1)S(1)}, u32[]{:S(2)}, u32[]{:S(2)}) collective-permute-start(bf16[512,640]{1,0:T(8,128)(2,1)S(1)} %slice_bitcast_fusion), channel_id=1, source_target_pairs={{0,8},{8,16},{16,24},{32,40},{40,48},{48,56},{64,72},{72,80},{80,8... | collective-permute-start | bytes 1966088 | tf_op jit(solution)/shard_map/ppermute | solution.py:51
  5.2 2.0 collective-permute-start.4
  7.9 9.1 %collective-permute-start.6 = (bf16[512,640]{1,0:T(8,128)(2,1)S(1)}, bf16[512,640]{1,0:T(8,128)(2,1)S(1)}, u32[]{:S(2)}, u32[]{:S(2)}) collective-permute-start(bf16[512,640]{1,0:T(8,128)(2,1)S(1)} %slice_bitcast_fusion), channel_id=1, source_target_pairs={{8,40},{16,48},{24,56},{40,72},{48,80},{56,88},{72,104},{80,112},{... | collective-permute-start | bytes 1966088 | tf_op jit(solution)/shard_map/ppermute | solution.py:39
  18.3 4.8 %shard_map.77 = f32[8,512]{1,0:T(8,128)} custom-call(f32[2]{0:T(128)} %pad_maximum_fusion.shares, bf16[3,512,640]{2,1,0:T(8,128)(2,1)} %clean.13, bf16[3,512,640]{2,1,0:T(8,128)(2,1)} %noise.13), custom_call_target="tpu_custom_call" | custom-call | flops 3932160 | bytes 2621440 | tf_op jit(solution)/shard_map/pallas_call | solution.py:86
  23.1 1.4 collective-permute-done
  25.2 1.0 collective-permute-start.1
  26.2 20.3 %collective-permute-done.1 = f32[8,512]{1,0:T(8,128)S(1)} collective-permute-done((f32[8,512]{1,0:T(8,128)S(1)}, f32[8,512]{1,0:T(8,128)S(1)}, u32[]{:S(2)}, u32[]{:S(2)}) %collective-permute-start.1) | collective-permute-done | bytes 16416 | tf_op jit(solution)/shard_map/ppermute | solution.py:344
  46.6 4.6 %collective-permute-done.2 = f32[8,512]{1,0:T(8,128)S(1)} collective-permute-done((f32[8,512]{1,0:T(8,128)S(1)}, f32[8,512]{1,0:T(8,128)S(1)}, u32[]{:S(2)}, u32[]{:S(2)}) %collective-permute-start.2) | collective-permute-done | bytes 16416 | tf_op jit(solution)/shard_map/ppermute | solution.py:344
  51.2 1.3 fusion.1
  54.4 2.3 collective-permute-start.9
  56.7 1.9 collective-permute-start.10
  58.7 12.2 %collective-permute-done.10 = bf16[512,256]{1,0:T(8,128)(2,1)S(1)} collective-permute-done((bf16[512,256]{1,0:T(8,128)(2,1)S(1)}, bf16[512,256]{1,0:T(8,128)(2,1)S(1)}, u32[]{:S(2)}, u32[]{:S(2)}) %collective-permute-start.10) | collective-permute-done | bytes 262176 | tf_op jit(solution)/shard_map/ppermute | solution.py:39
  70.9 1.9 collective-permute-start.11
  73.5 9.8 %collective-permute-done.9.both_3 = bf16[512,640]{1,0:T(8,128)(2,1)S(1)} collective-permute-done((bf16[512,640]{1,0:T(8,128)(2,1)S(1)}, bf16[512,640]{1,0:T(8,128)(2,1)S(1)}, u32[]{:S(2)}, u32[]{:S(2)}) %collective-permute-start.9) | collective-permute-done | bytes 655392 | tf_op jit(solution)/shard_map/ppermute | solution.py:51
  84.0 1.3 collective-permute-start.16
  85.3 2.2 collective-permute-start.17
  88.7 5.2 %collective-permute-done.11 = bf16[512,384]{1,0:T(8,128)(2,1)} collective-permute-done((bf16[512,384]{1,0:T(8,128)(2,1)S(1)}, bf16[512,384]{1,0:T(8,128)(2,1)}, u32[]{:S(2)}, u32[]{:S(2)}) %collective-permute-start.11) | collective-permute-done | bytes 393248 | tf_op jit(solution)/shard_map/ppermute | solution.py:39
  94.5 1.3 collective-permute-start.13
  95.9 14.8 %collective-permute-start.14 = (bf16[512,384]{1,0:T(8,128)(2,1)}, bf16[512,384]{1,0:T(8,128)(2,1)}, u32[]{:S(2)}, u32[]{:S(2)}) collective-permute-start(bf16[512,384]{1,0:T(8,128)(2,1)} %collective-permute-done.11), channel_id=1, source_target_pairs={{8,0},{16,8},{24,16},{40,32},{48,40},{56,48},{72,64},{80,72},{88,8... | collective-permute-start | bytes 1179656 | tf_op jit(solution)/shard_map/ppermute | solution.py:51
  112.6 11.9 %shard_map.78 = (bf16[512,640]{1,0:T(8,128)(2,1)}, f32[512,640]{1,0:T(8,128)}, f32[512,640]{1,0:T(8,128)}, f32[512,640]{1,0:T(8,128)}, bf16[2,512,256]{2,1,0:T(8...) custom-call(s32[9]{0:T(128)} %add_convert_fusion.3.flags, ...), custom_call_target="tpu_custom_call" | custom-call | flops 3221225472 | bytes 8388608 | tf_op jit(solution)/shard_map/pallas_call | solution.py:237
  124.9 0.7 copy-done.12
  125.7 1.7 collective-permute-start.20
  127.4 12.0 %shard_map.79 = (bf16[512,640]{1,0:T(8,128)(2,1)}, f32[512,640]{1,0:T(8,128)}, f32[512,640]{1,0:T(8,128)}, f32[512,640]{1,0:T(8,128)}, bf16[2,528,256]{2,1,0:T(8...) custom-call(s32[9]{0:T(128)} %add_convert_fusion.3.flags, ...), custom_call_target="tpu_custom_call", output_to_operand_aliasing={{0}: (17, {}), {1}: (18, {}), {2}: (19, {}), {3}: (20, {})} | custom-call | flops 3221225472 | bytes 8388608 | tf_op jit(solution)/shard_map/pallas_call | solution.py:237
  139.4 6.9 %shard_map.80 = (bf16[512,640]{1,0:T(8,128)(2,1)}, f32[512,640]{1,0:T(8,128)}, f32[512,640]{1,0:T(8,128)}, f32[512,640]{1,0:T(8,128)}, bf16[2,512,128]{2,1,0:T(8...) custom-call(s32[9]{0:T(128)} %add_convert_fusion.3.flags, ...), custom_call_target="tpu_custom_call", output_to_operand_aliasing={{0}: (17, {}), {1}: (18, {}), {2}: (19, {}), {3}: (20, {})} | custom-call | flops 1610612736 | bytes 4194304 | tf_op jit(solution)/shard_map/pallas_call | solution.py:237
  147.2 1.2 collective-permute-done.21
  148.4 1.5 collective-permute-start.22
  149.8 2.3 collective-permute-done.22
  152.1 0.8 collective-permute-start.23
  152.9 3.9 %collective-permute-done.23 = f32[8,512]{1,0:T(8,128)S(1)} collective-permute-done((f32[8,512]{1,0:T(8,128)S(1)}, f32[8,512]{1,0:T(8,128)S(1)}, u32[]{:S(2)}, u32[]{:S(2)}) %collective-permute-start.23) | collective-permute-done | bytes 16416 | tf_op jit(solution)/shard_map/ppermute | solution.py:344
  157.5 2.3 %collective-permute-start.26 = (bf16[2,528,256]{2,1,0:T(8,128)(2,1)}, bf16[2,528,256]{2,1,0:T(8,128)(2,1)S(1)}, u32[]{:S(2)}, u32[]{:S(2)}) collective-permute-start(bf16[2,528,256]{2,1,0:T(8,128)(2,1)} %get-tuple-element.64), channel_id=1, source_target_pairs={{0,8},{8,16},{16,24},{24,0},{32,40},{40,48},{48,56},{56,32},{64,72... | collective-permute-start | bytes 1622024 | tf_op jit(solution)/shard_map/ppermute | solution.py:51
  159.8 1.8 collective-permute-start.25
  161.6 2.6 %collective-permute-start.24 = (bf16[2,528,256]{2,1,0:T(8,128)(2,1)}, bf16[2,528,256]{2,1,0:T(8,128)(2,1)S(1)}, u32[]{:S(2)}, u32[]{:S(2)}) collective-permute-start(bf16[2,528,256]{2,1,0:T(8,128)(2,1)} %get-tuple-element.62), channel_id=1, source_target_pairs={{0,24},{8,0},{16,8},{24,16},{32,56},{40,32},{48,40},{56,48},{64,88... | collective-permute-start | bytes 1622024 | tf_op jit(solution)/shard_map/ppermute | solution.py:51
  164.6 3.3 %collective-permute-start.28 = (bf16[2,512,256]{2,1,0:T(8,128)(2,1)S(1)}, bf16[2,512,256]{2,1,0:T(8,128)(2,1)S(1)}, u32[]{:S(2)}, u32[]{:S(2)}) collective-permute-start(bf16[2,512,256]{2,1,0:T(8,128)(2,1)S(1)} %add_convert_fusion.1), channel_id=1, source_target_pairs={{40,8},{48,16},{56,24},{72,40},{80,48},{88,56},{104,72},{112,80},{... | collective-permute-start | bytes 1572872 | tf_op jit(solution)/shard_map/ppermute | solution.py:39
  167.9 13.4 %collective-permute-done.26.in_3 = bf16[2,528,256]{2,1,0:T(8,128)(2,1)S(1)} collective-permute-done((bf16[2,528,256]{2,1,0:T(8,128)(2,1)}, bf16[2,528,256]{2,1,0:T(8,128)(2,1)S(1)}, u32[]{:S(2)}, u32[]{:S(2)}) %collective-permute-start.26) | collective-permute-done | bytes 540704 | tf_op jit(solution)/shard_map/ppermute | solution.py:51
  181.3 3.6 %collective-permute-done.24.in_1 = bf16[2,528,256]{2,1,0:T(8,128)(2,1)S(1)} collective-permute-done((bf16[2,528,256]{2,1,0:T(8,128)(2,1)}, bf16[2,528,256]{2,1,0:T(8,128)(2,1)S(1)}, u32[]{:S(2)}, u32[]{:S(2)}) %collective-permute-start.24) | collective-permute-done | bytes 540704 | tf_op jit(solution)/shard_map/ppermute | solution.py:51
  185.2 3.2 %collective-permute-start.27 = (bf16[2,528,256]{2,1,0:T(8,128)(2,1)S(1)}, bf16[2,528,256]{2,1,0:T(8,128)(2,1)S(1)}, u32[]{:S(2)}, u32[]{:S(2)}) collective-permute-start(bf16[2,528,256]{2,1,0:T(8,128)(2,1)S(1)} %add_convert_fusion), channel_id=1, source_target_pairs={{40,8},{48,16},{56,24},{72,40},{80,48},{88,56},{104,72},{112,80},{... | collective-permute-start | bytes 1622024 | tf_op jit(solution)/shard_map/ppermute | solution.py:39
  188.6 2.2 collective-permute-start.30
  190.7 2.5 %collective-permute-start.31 = (bf16[2,512,128]{2,1,0:T(8,128)(2,1)S(1)}, bf16[2,512,128]{2,1,0:T(8,128)(2,1)S(1)}, u32[]{:S(2)}, u32[]{:S(2)}) collective-permute-start(bf16[2,512,128]{2,1,0:T(8,128)(2,1)S(1)} %copy-done.25), channel_id=1, source_target_pairs={{0,8},{8,16},{16,24},{24,0},{32,40},{40,48},{48,56},{56,32},{64,72... | collective-permute-start | bytes 786440 | tf_op jit(solution)/shard_map/ppermute | solution.py:51
  193.3 3.8 %collective-permute-done.29.in_1 = bf16[2,512,128]{2,1,0:T(8,128)(2,1)S(1)} collective-permute-done((bf16[2,512,128]{2,1,0:T(8,128)(2,1)S(1)}, bf16[2,512,128]{2,1,0:T(8,128)(2,1)S(1)}, u32[]{:S(2)}, u32[]{:S(2)}) %collective-permute-start.29) | collective-permute-done | bytes 262176 | tf_op jit(solution)/shard_map/ppermute | solution.py:51
  197.1 5.4 %collective-permute-done.30.in_2 = bf16[2,512,128]{2,1,0:T(8,128)(2,1)S(1)} collective-permute-done((bf16[2,512,128]{2,1,0:T(8,128)(2,1)S(1)}, bf16[2,512,128]{2,1,0:T(8,128)(2,1)S(1)}, u32[]{:S(2)}, u32[]{:S(2)}) %collective-permute-start.30) | collective-permute-done | bytes 262176 | tf_op jit(solution)/shard_map/ppermute | solution.py:51
  202.4 1.5 collective-permute-done.31.in_3
  204.1 5.9 %collective-permute-start.32 = (bf16[2,512,128]{2,1,0:T(8,128)(2,1)S(1)}, bf16[2,512,128]{2,1,0:T(8,128)(2,1)S(1)}, u32[]{:S(2)}, u32[]{:S(2)}) collective-permute-start(bf16[2,512,128]{2,1,0:T(8,128)(2,1)S(1)} %add_convert_fusion.2), channel_id=1, source_target_pairs={{40,8},{48,16},{56,24},{72,40},{80,48},{88,56},{104,72},{112,80},{... | collective-permute-start | bytes 786440 | tf_op jit(solution)/shard_map/ppermute | solution.py:39
  210.0 9.0 %collective-permute-done.27.crossed = bf16[2,528,256]{2,1,0:T(8,128)(2,1)S(1)} collective-permute-done((bf16[2,528,256]{2,1,0:T(8,128)(2,1)S(1)}, bf16[2,528,256]{2,1,0:T(8,128)(2,1)S(1)}, u32[]{:S(2)}, u32[]{:S(2)}) %collective-permute-start.27) | collective-permute-done | bytes 540704 | tf_op jit(solution)/shard_map/ppermute | solution.py:39
  219.1 0.8 copy-done.16
  220.6 4.2 %shard_map.81.refs_0_ = f32[3,512,640]{2,1,0:T(8,128)} custom-call(s32[9]{0:T(128)} %add_convert_fusion.3.flags, f32[2]{0:T(128)} %pad_maximum_fusion.shares, f32[8,512]{1,0:T(8,128)} %concatenate.12.rows_ref, f32[1,640]{1,0:T(1,128)} %broadcast_in_dim.31.gain_q, f32[1,640]{1,0:T(1,128)} %broadcast_in_dim.32.gain_k, bf16[3,512,640]{2,1,0:T(8,128)(2,1)} %clean.13, ...), custom_call_target="tpu_custom_call" | custom-call | flops 3932160 | bytes 6291456 | tf_op jit(solution)/shard_map/pallas_call | solution.py:320
  224.8 4.0 %shard_map.82.refs_0_ = f32[3,512,640]{2,1,0:T(8,128)} custom-call(s32[9]{0:T(128)} %add_convert_fusion.3.flags, f32[2]{0:T(128)} %pad_maximum_fusion.shares, f32[8,512]{1,0:T(8,128)} %concatenate.12.rows_ref, f32[1,640]{1,0:T(1,128)} %broadcast_in_dim.31.gain_q, f32[1,640]{1,0:T(1,128)} %broadcast_in_dim.32.gain_k, ...), custom_call_target="tpu_custom_call", output_to_operand_aliasing={{}: (14, {})} | custom-call | flops 3932160 | bytes 6291456 | tf_op jit(solution)/shard_map/pallas_call | solution.py:320
  229.5 3.2 %shard_map.83 = f32[3,512,640]{2,1,0:T(8,128)} custom-call(s32[9]{0:T(128)} %add_convert_fusion.3.flags, f32[2]{0:T(128)} %pad_maximum_fusion.shares, f32[8,512]{1,0:T(8,128)} %concatenate.12.rows_ref, f32[1,640]{1,0:T(1,128)} %broadcast_in_dim.31.gain_q, f32[1,640]{1,0:T(1,128)} %broadcast_in_dim.32.gain_k, ...), custom_call_target="tpu_custom_call", output_to_operand_aliasing={{}: (14, {})} | custom-call | flops 1966080 | bytes 3145728 | tf_op jit(solution)/shard_map/pallas_call | solution.py:320
  (124 shorter events, 13.3 us)
Async XLA Ops:
  1.8 50.8 %collective-permute-start.3 = (bf16[512,640]{1,0:T(8,128)(2,1)S(1)}, bf16[512,640]{1,0:T(8,128)(2,1)S(1)}, u32[]{:S(2)}, u32[]{:S(2)}) collective-permute-start(bf16[512,640]{1,0:T(8,128)(2,1)S(1)} %slice_bitcast_fusion), channel_id=1, source_target_pairs={{0,8},{8,16},{16,24},{32,40},{40,48},{48,56},{64,72},{72,80},{80,8... | collective-permute-start | bytes 1966088 | tf_op jit(solution)/shard_map/ppermute | solution.py:51
  5.2 47.4 %collective-permute-start.4 = (bf16[512,640]{1,0:T(8,128)(2,1)S(1)}, bf16[512,640]{1,0:T(8,128)(2,1)S(1)}, u32[]{:S(2)}, u32[]{:S(2)}) collective-permute-start(bf16[512,640]{1,0:T(8,128)(2,1)S(1)} %slice_bitcast_fusion), channel_id=1, source_target_pairs={{0,16},{8,24},{32,48},{40,56},{64,80},{72,88},{96,112},{104,120},{... | collective-permute-start | bytes 1966088 | tf_op jit(solution)/shard_map/ppermute | solution.py:51
  7.2 45.4 %collective-permute-start.5 = (bf16[512,640]{1,0:T(8,128)(2,1)S(1)}, bf16[512,640]{1,0:T(8,128)(2,1)S(1)}, u32[]{:S(2)}, u32[]{:S(2)}) collective-permute-start(bf16[512,640]{1,0:T(8,128)(2,1)S(1)} %slice_bitcast_fusion), channel_id=1, source_target_pairs={{0,24},{32,56},{64,88},{96,120},{128,152},{160,184},{192,216},{224... | collective-permute-start | bytes 1966088 | tf_op jit(solution)/shard_map/ppermute | solution.py:51
  7.9 44.7 %collective-permute-start.6 = (bf16[512,640]{1,0:T(8,128)(2,1)S(1)}, bf16[512,640]{1,0:T(8,128)(2,1)S(1)}, u32[]{:S(2)}, u32[]{:S(2)}) collective-permute-start(bf16[512,640]{1,0:T(8,128)(2,1)S(1)} %slice_bitcast_fusion), channel_id=1, source_target_pairs={{8,40},{16,48},{24,56},{40,72},{48,80},{56,88},{72,104},{80,112},{... | collective-permute-start | bytes 1966088 | tf_op jit(solution)/shard_map/ppermute | solution.py:39
  18.3 32.9 %copy-start.21 = (f32[640]{0:T(1024)S(1)}, f32[640]{0:T(1024)}, u32[]{:S(2)}) copy-start(f32[640]{0:T(1024)} %param.10) | copy-start | bytes 7684
  23.1 1.4 collective-permute-start
  25.2 21.3 %collective-permute-start.1 = (f32[8,512]{1,0:T(8,128)S(1)}, f32[8,512]{1,0:T(8,128)S(1)}, u32[]{:S(2)}, u32[]{:S(2)}) collective-permute-start(f32[8,512]{1,0:T(8,128)S(1)} %add.176), channel_id=1, source_target_pairs={{0,2},{1,3},{2,0},{3,1},{4,6},{5,7},{6,4},{7,5},{8,10},{9,11},{10,... | collective-permute-start | bytes 49160 | tf_op jit(solution)/shard_map/ppermute | solution.py:344
  46.5 4.6 %collective-permute-start.2 = (f32[8,512]{1,0:T(8,128)S(1)}, f32[8,512]{1,0:T(8,128)S(1)}, u32[]{:S(2)}, u32[]{:S(2)}) collective-permute-start(f32[8,512]{1,0:T(8,128)S(1)} %add.177), channel_id=1, source_target_pairs={{0,4},{1,5},{2,6},{3,7},{4,0},{5,1},{6,2},{7,3},{8,12},{9,13},{10,... | collective-permute-start | bytes 49160 | tf_op jit(solution)/shard_map/ppermute | solution.py:344
  53.8 34.3 %copy-start.24 = (f32[640]{0:T(1024)S(1)}, f32[640]{0:T(1024)}, u32[]{:S(2)}) copy-start(f32[640]{0:T(1024)} %param.9) | copy-start | bytes 7684
  53.8 19.0 %collective-permute-start.7 = (bf16[512,640]{1,0:T(8,128)(2,1)S(1)}, bf16[512,640]{1,0:T(8,128)(2,1)S(1)}, u32[]{:S(2)}, u32[]{:S(2)}) collective-permute-start(bf16[512,640]{1,0:T(8,128)(2,1)S(1)} %get-tuple-element.76), channel_id=1, source_target_pairs={{0,8},{8,16},{16,24},{24,0},{32,40},{40,48},{48,56},{56,32},{64,72... | collective-permute-start | bytes 1966088 | tf_op jit(solution)/shard_map/ppermute | solution.py:51
  54.4 19.2 %collective-permute-start.8 = (bf16[512,640]{1,0:T(8,128)(2,1)S(1)}, bf16[512,640]{1,0:T(8,128)(2,1)S(1)}, u32[]{:S(2)}, u32[]{:S(2)}) collective-permute-start(bf16[512,640]{1,0:T(8,128)(2,1)S(1)} %get-tuple-element.75), channel_id=1, source_target_pairs={{0,16},{8,24},{16,0},{24,8},{32,48},{40,56},{48,32},{56,40},{64,80... | collective-permute-start | bytes 1966088 | tf_op jit(solution)/shard_map/ppermute | solution.py:51
  54.4 28.9 %collective-permute-start.9 = (bf16[512,640]{1,0:T(8,128)(2,1)S(1)}, bf16[512,640]{1,0:T(8,128)(2,1)S(1)}, u32[]{:S(2)}, u32[]{:S(2)}) collective-permute-start(bf16[512,640]{1,0:T(8,128)(2,1)S(1)} %get-tuple-element.74), channel_id=1, source_target_pairs={{0,24},{8,0},{16,8},{24,16},{32,56},{40,32},{48,40},{56,48},{64,88... | collective-permute-start | bytes 1966088 | tf_op jit(solution)/shard_map/ppermute | solution.py:51
  56.7 14.2 %collective-permute-start.10 = (bf16[512,256]{1,0:T(8,128)(2,1)S(1)}, bf16[512,256]{1,0:T(8,128)(2,1)S(1)}, u32[]{:S(2)}, u32[]{:S(2)}) collective-permute-start(bf16[512,256]{1,0:T(8,128)(2,1)S(1)} %slice.110), channel_id=1, source_target_pairs={{8,40},{16,48},{24,56},{40,72},{48,80},{56,88},{72,104},{80,112},{... | collective-permute-start | bytes 786440 | tf_op jit(solution)/shard_map/ppermute | solution.py:39
  70.9 23.0 %collective-permute-start.11 = (bf16[512,384]{1,0:T(8,128)(2,1)S(1)}, bf16[512,384]{1,0:T(8,128)(2,1)}, u32[]{:S(2)}, u32[]{:S(2)}) collective-permute-start(bf16[512,384]{1,0:T(8,128)(2,1)S(1)} %slice.109), channel_id=1, source_target_pairs={{8,40},{16,48},{24,56},{40,72},{48,80},{56,88},{72,104},{80,112},{... | collective-permute-start | bytes 1179656 | tf_op jit(solution)/shard_map/ppermute | solution.py:39
  72.8 38.4 %copy-start.3 = (bf16[512,640]{1,0:T(8,128)(2,1)}, bf16[512,640]{1,0:T(8,128)(2,1)S(1)}, u32[]{:S(2)}) copy-start(bf16[512,640]{1,0:T(8,128)(2,1)S(1)} %collective-permute-done.7.both_1) | copy-start | bytes 1966084
  73.5 37.7 %copy-start.4 = (bf16[512,640]{1,0:T(8,128)(2,1)}, bf16[512,640]{1,0:T(8,128)(2,1)S(1)}, u32[]{:S(2)}) copy-start(bf16[512,640]{1,0:T(8,128)(2,1)S(1)} %collective-permute-done.8.both_2) | copy-start | bytes 1966084
  83.3 27.9 %copy-start.5 = (bf16[512,640]{1,0:T(8,128)(2,1)}, bf16[512,640]{1,0:T(8,128)(2,1)S(1)}, u32[]{:S(2)}) copy-start(bf16[512,640]{1,0:T(8,128)(2,1)S(1)} %collective-permute-done.9.both_3) | copy-start | bytes 1966084
  83.3 12.5 %collective-permute-start.15 = (bf16[512,256]{1,0:T(8,128)(2,1)S(1)}, bf16[512,256]{1,0:T(8,128)(2,1)S(1)}, u32[]{:S(2)}, u32[]{:S(2)}) collective-permute-start(bf16[512,256]{1,0:T(8,128)(2,1)S(1)} %collective-permute-done.10), channel_id=1, source_target_pairs={{24,0},{56,32},{88,64},{120,96},{152,128},{184,160},{216,192},{248... | collective-permute-start | bytes 786440 | tf_op jit(solution)/shard_map/ppermute | solution.py:51
  84.0 27.2 %collective-permute-start.16 = (bf16[512,256]{1,0:T(8,128)(2,1)S(1)}, bf16[512,256]{1,0:T(8,128)(2,1)S(1)}, u32[]{:S(2)}, u32[]{:S(2)}) collective-permute-start(bf16[512,256]{1,0:T(8,128)(2,1)S(1)} %collective-permute-done.10), channel_id=1, source_target_pairs={{16,0},{24,8},{48,32},{56,40},{80,64},{88,72},{112,96},{120,104},{... | collective-permute-start | bytes 786440 | tf_op jit(solution)/shard_map/ppermute | solution.py:51
  85.3 25.9 %collective-permute-start.17 = (bf16[512,256]{1,0:T(8,128)(2,1)S(1)}, bf16[512,256]{1,0:T(8,128)(2,1)S(1)}, u32[]{:S(2)}, u32[]{:S(2)}) collective-permute-start(bf16[512,256]{1,0:T(8,128)(2,1)S(1)} %collective-permute-done.10), channel_id=1, source_target_pairs={{8,0},{16,8},{24,16},{40,32},{48,40},{56,48},{72,64},{80,72},{88,8... | collective-permute-start | bytes 786440 | tf_op jit(solution)/shard_map/ppermute | solution.py:51
  93.9 31.0 %collective-permute-start.12 = (bf16[512,384]{1,0:T(8,128)(2,1)}, bf16[512,384]{1,0:T(8,128)(2,1)S(1)}, u32[]{:S(2)}, u32[]{:S(2)}) collective-permute-start(bf16[512,384]{1,0:T(8,128)(2,1)} %collective-permute-done.11), channel_id=1, source_target_pairs={{24,0},{56,32},{88,64},{120,96},{152,128},{184,160},{216,192},{248... | collective-permute-start | bytes 1179656 | tf_op jit(solution)/shard_map/ppermute | solution.py:51
  94.5 32.8 %collective-permute-start.13 = (bf16[512,384]{1,0:T(8,128)(2,1)}, bf16[512,384]{1,0:T(8,128)(2,1)}, u32[]{:S(2)}, u32[]{:S(2)}) collective-permute-start(bf16[512,384]{1,0:T(8,128)(2,1)} %collective-permute-done.11), channel_id=1, source_target_pairs={{16,0},{24,8},{48,32},{56,40},{80,64},{88,72},{112,96},{120,104},{... | collective-permute-start | bytes 1179656 | tf_op jit(solution)/shard_map/ppermute | solution.py:51
  95.9 31.5 %collective-permute-start.14 = (bf16[512,384]{1,0:T(8,128)(2,1)}, bf16[512,384]{1,0:T(8,128)(2,1)}, u32[]{:S(2)}, u32[]{:S(2)}) collective-permute-start(bf16[512,384]{1,0:T(8,128)(2,1)} %collective-permute-done.11), channel_id=1, source_target_pairs={{8,0},{16,8},{24,16},{40,32},{48,40},{56,48},{72,64},{80,72},{88,8... | collective-permute-start | bytes 1179656 | tf_op jit(solution)/shard_map/ppermute | solution.py:51
  124.5 22.5 %collective-permute-start.18 = (bf16[2,512,256]{2,1,0:T(8,128)(2,1)}, bf16[2,512,256]{2,1,0:T(8,128)(2,1)S(1)}, u32[]{:S(2)}, u32[]{:S(2)}) collective-permute-start(bf16[2,512,256]{2,1,0:T(8,128)(2,1)} %get-tuple-element.55), channel_id=1, source_target_pairs={{0,24},{8,0},{16,8},{24,16},{32,56},{40,32},{48,40},{56,48},{64,88... | collective-permute-start | bytes 1572872 | tf_op jit(solution)/shard_map/ppermute | solution.py:51
  124.6 22.4 %collective-permute-start.19 = (bf16[2,512,256]{2,1,0:T(8,128)(2,1)}, bf16[2,512,256]{2,1,0:T(8,128)(2,1)S(1)}, u32[]{:S(2)}, u32[]{:S(2)}) collective-permute-start(bf16[2,512,256]{2,1,0:T(8,128)(2,1)} %get-tuple-element.56), channel_id=1, source_target_pairs={{0,16},{8,24},{16,0},{24,8},{32,48},{40,56},{48,32},{56,40},{64,80... | collective-permute-start | bytes 1572872 | tf_op jit(solution)/shard_map/ppermute | solution.py:51
  125.7 21.4 %collective-permute-start.20 = (bf16[2,512,256]{2,1,0:T(8,128)(2,1)}, bf16[2,512,256]{2,1,0:T(8,128)(2,1)S(1)}, u32[]{:S(2)}, u32[]{:S(2)}) collective-permute-start(bf16[2,512,256]{2,1,0:T(8,128)(2,1)} %get-tuple-element.57), channel_id=1, source_target_pairs={{0,8},{8,16},{16,24},{24,0},{32,40},{40,48},{48,56},{56,32},{64,72... | collective-permute-start | bytes 1572872 | tf_op jit(solution)/shard_map/ppermute | solution.py:51
  147.1 38.1 %copy-start.9 = (bf16[2,512,256]{2,1,0:T(8,128)(2,1)}, bf16[2,512,256]{2,1,0:T(8,128)(2,1)S(1)}, u32[]{:S(2)}) copy-start(bf16[2,512,256]{2,1,0:T(8,128)(2,1)S(1)} %collective-permute-done.18.in_1) | copy-start | bytes 1572868
  147.1 38.1 %copy-start.10 = (bf16[2,512,256]{2,1,0:T(8,128)(2,1)}, bf16[2,512,256]{2,1,0:T(8,128)(2,1)S(1)}, u32[]{:S(2)}) copy-start(bf16[2,512,256]{2,1,0:T(8,128)(2,1)S(1)} %collective-permute-done.19.in_2) | copy-start | bytes 1572868
  147.1 38.1 %copy-start.11 = (bf16[2,512,256]{2,1,0:T(8,128)(2,1)}, bf16[2,512,256]{2,1,0:T(8,128)(2,1)S(1)}, u32[]{:S(2)}) copy-start(bf16[2,512,256]{2,1,0:T(8,128)(2,1)S(1)} %collective-permute-done.20.in_3) | copy-start | bytes 1572868
  147.1 1.3 collective-permute-start.21
  148.4 3.7 %collective-permute-start.22 = (f32[8,512]{1,0:T(8,128)S(1)}, f32[8,512]{1,0:T(8,128)S(1)}, u32[]{:S(2)}, u32[]{:S(2)}) collective-permute-start(f32[8,512]{1,0:T(8,128)S(1)} %add.186), channel_id=1, source_target_pairs={{0,2},{1,3},{2,0},{3,1},{4,6},{5,7},{6,4},{7,5},{8,10},{9,11},{10,... | collective-permute-start | bytes 49160 | tf_op jit(solution)/shard_map/ppermute | solution.py:344
  152.1 4.6 %collective-permute-start.23 = (f32[8,512]{1,0:T(8,128)S(1)}, f32[8,512]{1,0:T(8,128)S(1)}, u32[]{:S(2)}, u32[]{:S(2)}) collective-permute-start(f32[8,512]{1,0:T(8,128)S(1)} %add.187), channel_id=1, source_target_pairs={{0,4},{1,5},{2,6},{3,7},{4,0},{5,1},{6,2},{7,3},{8,12},{9,13},{10,... | collective-permute-start | bytes 49160 | tf_op jit(solution)/shard_map/ppermute | solution.py:344
  157.5 23.8 %collective-permute-start.26 = (bf16[2,528,256]{2,1,0:T(8,128)(2,1)}, bf16[2,528,256]{2,1,0:T(8,128)(2,1)S(1)}, u32[]{:S(2)}, u32[]{:S(2)}) collective-permute-start(bf16[2,528,256]{2,1,0:T(8,128)(2,1)} %get-tuple-element.64), channel_id=1, source_target_pairs={{0,8},{8,16},{16,24},{24,0},{32,40},{40,48},{48,56},{56,32},{64,72... | collective-permute-start | bytes 1622024 | tf_op jit(solution)/shard_map/ppermute | solution.py:51
  159.8 21.5 %collective-permute-start.25 = (bf16[2,528,256]{2,1,0:T(8,128)(2,1)}, bf16[2,528,256]{2,1,0:T(8,128)(2,1)S(1)}, u32[]{:S(2)}, u32[]{:S(2)}) collective-permute-start(bf16[2,528,256]{2,1,0:T(8,128)(2,1)} %get-tuple-element.63), channel_id=1, source_target_pairs={{0,16},{8,24},{16,0},{24,8},{32,48},{40,56},{48,32},{56,40},{64,80... | collective-permute-start | bytes 1622024 | tf_op jit(solution)/shard_map/ppermute | solution.py:51
  161.6 23.3 %collective-permute-start.24 = (bf16[2,528,256]{2,1,0:T(8,128)(2,1)}, bf16[2,528,256]{2,1,0:T(8,128)(2,1)S(1)}, u32[]{:S(2)}, u32[]{:S(2)}) collective-permute-start(bf16[2,528,256]{2,1,0:T(8,128)(2,1)} %get-tuple-element.62), channel_id=1, source_target_pairs={{0,24},{8,0},{16,8},{24,16},{32,56},{40,32},{48,40},{56,48},{64,88... | collective-permute-start | bytes 1622024 | tf_op jit(solution)/shard_map/ppermute | solution.py:51
  164.5 23.9 %copy-start.27 = (bf16[2,512,128]{2,1,0:T(8,128)(2,1)S(1)}, bf16[2,512,128]{2,1,0:T(8,128)(2,1)}, u32[]{:S(2)}) copy-start(bf16[2,512,128]{2,1,0:T(8,128)(2,1)} %get-tuple-element.71) | copy-start | bytes 786436
  164.6 24.0 %copy-start.26 = (bf16[2,512,128]{2,1,0:T(8,128)(2,1)S(1)}, bf16[2,512,128]{2,1,0:T(8,128)(2,1)}, u32[]{:S(2)}) copy-start(bf16[2,512,128]{2,1,0:T(8,128)(2,1)} %get-tuple-element.72) | copy-start | bytes 786436
  164.6 26.2 %copy-start.25 = (bf16[2,512,128]{2,1,0:T(8,128)(2,1)S(1)}, bf16[2,512,128]{2,1,0:T(8,128)(2,1)}, u32[]{:S(2)}) copy-start(bf16[2,512,128]{2,1,0:T(8,128)(2,1)} %get-tuple-element.73) | copy-start | bytes 786436
  164.6 23.8 %collective-permute-start.28 = (bf16[2,512,256]{2,1,0:T(8,128)(2,1)S(1)}, bf16[2,512,256]{2,1,0:T(8,128)(2,1)S(1)}, u32[]{:S(2)}, u32[]{:S(2)}) collective-permute-start(bf16[2,512,256]{2,1,0:T(8,128)(2,1)S(1)} %add_convert_fusion.1), channel_id=1, source_target_pairs={{40,8},{48,16},{56,24},{72,40},{80,48},{88,56},{104,72},{112,80},{... | collective-permute-start | bytes 1572872 | tf_op jit(solution)/shard_map/ppermute | solution.py:39
  167.9 52.0 %copy-start.20 = (f32[8,512]{1,0:T(8,128)S(1)}, f32[8,512]{1,0:T(8,128)}, u32[]{:S(2)}) copy-start(f32[8,512]{1,0:T(8,128)} %copy-done.19) | copy-start | bytes 49156
  167.9 52.0 %slice-start = ((f32[8,512]{1,0:T(8,128)}), f32[3,512]{1,0:T(4,128)S(1)}, s32[]{:S(2)}) async-start(f32[8,512]{1,0:T(8,128)} %copy-done.19), calls=%async_computation | async-start | bytes 16384 | tf_op jit(solution)/shard_map/slice | solution.py:442
  185.2 33.8 %collective-permute-start.27 = (bf16[2,528,256]{2,1,0:T(8,128)(2,1)S(1)}, bf16[2,528,256]{2,1,0:T(8,128)(2,1)S(1)}, u32[]{:S(2)}, u32[]{:S(2)}) collective-permute-start(bf16[2,528,256]{2,1,0:T(8,128)(2,1)S(1)} %add_convert_fusion), channel_id=1, source_target_pairs={{40,8},{48,16},{56,24},{72,40},{80,48},{88,56},{104,72},{112,80},{... | collective-permute-start | bytes 1622024 | tf_op jit(solution)/shard_map/ppermute | solution.py:39
  188.4 31.4 %copy-start.17 = (bf16[2,512,256]{2,1,0:T(8,128)(2,1)}, bf16[2,512,256]{2,1,0:T(8,128)(2,1)S(1)}, u32[]{:S(2)}) copy-start(bf16[2,512,256]{2,1,0:T(8,128)(2,1)S(1)} %collective-permute-done.28.crossed) | copy-start | bytes 1572868
  188.5 8.6 %collective-permute-start.29 = (bf16[2,512,128]{2,1,0:T(8,128)(2,1)S(1)}, bf16[2,512,128]{2,1,0:T(8,128)(2,1)S(1)}, u32[]{:S(2)}, u32[]{:S(2)}) collective-permute-start(bf16[2,512,128]{2,1,0:T(8,128)(2,1)S(1)} %copy-done.27), channel_id=1, source_target_pairs={{0,24},{8,0},{16,8},{24,16},{32,56},{40,32},{48,40},{56,48},{64,88... | collective-permute-start | bytes 786440 | tf_op jit(solution)/shard_map/ppermute | solution.py:51
  188.6 13.9 %collective-permute-start.30 = (bf16[2,512,128]{2,1,0:T(8,128)(2,1)S(1)}, bf16[2,512,128]{2,1,0:T(8,128)(2,1)S(1)}, u32[]{:S(2)}, u32[]{:S(2)}) collective-permute-start(bf16[2,512,128]{2,1,0:T(8,128)(2,1)S(1)} %copy-done.26), channel_id=1, source_target_pairs={{0,16},{8,24},{16,0},{24,8},{32,48},{40,56},{48,32},{56,40},{64,80... | collective-permute-start | bytes 786440 | tf_op jit(solution)/shard_map/ppermute | solution.py:51
  190.7 13.2 %collective-permute-start.31 = (bf16[2,512,128]{2,1,0:T(8,128)(2,1)S(1)}, bf16[2,512,128]{2,1,0:T(8,128)(2,1)S(1)}, u32[]{:S(2)}, u32[]{:S(2)}) collective-permute-start(bf16[2,512,128]{2,1,0:T(8,128)(2,1)S(1)} %copy-done.25), channel_id=1, source_target_pairs={{0,8},{8,16},{16,24},{24,0},{32,40},{40,48},{48,56},{56,32},{64,72... | collective-permute-start | bytes 786440 | tf_op jit(solution)/shard_map/ppermute | solution.py:51
  197.1 27.7 %copy-start.13 = (bf16[2,512,128]{2,1,0:T(8,128)(2,1)}, bf16[2,512,128]{2,1,0:T(8,128)(2,1)S(1)}, u32[]{:S(2)}) copy-start(bf16[2,512,128]{2,1,0:T(8,128)(2,1)S(1)} %collective-permute-done.29.in_1) | copy-start | bytes 786436
  204.1 24.7 %collective-permute-start.32 = (bf16[2,512,128]{2,1,0:T(8,128)(2,1)S(1)}, bf16[2,512,128]{2,1,0:T(8,128)(2,1)S(1)}, u32[]{:S(2)}, u32[]{:S(2)}) collective-permute-start(bf16[2,512,128]{2,1,0:T(8,128)(2,1)S(1)} %add_convert_fusion.2), channel_id=1, source_target_pairs={{40,8},{48,16},{56,24},{72,40},{80,48},{88,56},{104,72},{112,80},{... | collective-permute-start | bytes 786440 | tf_op jit(solution)/shard_map/ppermute | solution.py:39
  (17 other events, 145.7 us)

commit v4 on v3

--- a/solution.py
+++ b/solution.py
@@ -378,7 +378,7 @@
     both = mixed(after(key_clean, *first), cross_values)
     cross_a = shift_spans(after(lanes(key_clean, 0, 2), cross_values), COLUMNS, crossers)
     cross_b = shift_spans(after(lanes(key_clean, 2, 3), cross_a), COLUMNS, crossers)
-    last_a = [shift_columns(after(cross_a, *both), hop, "wrapped") for hop in steps]
+    last_a = [shift_columns(cross_a, hop, "wrapped") for hop in steps]
     last_b = [shift_columns(after(cross_b, *both), hop, "wrapped") for hop in steps]
 
     hops = jnp.arange(1, CONTEXT + 1, dtype=jnp.int32)

time: 236 us -> 232 us (0.983)
  waiting for transfers between devices: 98.2 us -> 90.5 us
  starting transfers between devices: 72.1 us -> 75 us
    ppermute x21, waiting for transfers between devices: 38.1 us -> 26.9 us  [shift_columns(): return lax.ppermute(block, 'tm', route)]
    ppermute x6, starting transfers between devices: 25.4 us -> 31.6 us  [shift_spans(): return lax.ppermute(block, 'tm', route)]
  transfers between devices with their start and end apart: 33 -> 33, of which waited for: 16 -> 17; matrix products, arithmetic and copies ran while one was open for 3% -> 3% of each run, Pallas kernels for 19% -> 19%
where the time goes in v4:
time: 232 us; the launch traced here: 228 us
  waiting for transfers between devices  90.5 us (39%)
  starting transfers between devices  75 us (32%)
  Pallas kernels  47 us (20%)
  local copies, waits for them, and re-layouts  8.41 us (4%)
  other arithmetic  4.99 us (2%)
    ppermute x21, starting transfers between devices, shift_columns(): return lax.ppermute(block, 'tm', route)  42.2 us
    ppermute x6, waiting for transfers between devices, head_sum(): block = block + lax.ppermute(block, 'head', route)  35.7 us
    ppermute x6, starting transfers between devices, shift_spans(): return lax.ppermute(block, 'tm', route)  31.6 us
    pallas_call x3, Pallas kernels, attention_chunk(): pl.pallas_call(attention_body, grid=(heads,), in_specs=in_specs, out_spec...  30.8 us
    ppermute x6, waiting for transfers between devices, shift_spans(): return lax.ppermute(block, 'tm', route)  27.9 us
    ppermute x21, waiting for transfers between devices, shift_columns(): return lax.ppermute(block, 'tm', route)  26.9 us
    pallas_call x3, Pallas kernels, finish_chunk(): pl.pallas_call(finish_body, grid=(heads,), in_specs=in_specs, out_specs=p...  11.4 us
    pallas_call x1, Pallas kernels, prepare(): pl.pallas_call(prepare_body, grid=(width // HEAD_DIM,), in_specs=[pl.Bloc...  4.79 us
  transfers between devices with their start and end apart: 33, of which 17 were waited for; matrix products, arithmetic and copies ran while one was open for 3% of the time, Pallas kernels for 19%

profile of v4, /device:TPU:26, one launch (start us, length us, event | category | flops | bytes accessed | tf_op | source)
XLA Modules:
  0.0 227.9 jit_solution(1942515507714058670)
XLA Ops:
  0.6 1.1 slice_bitcast_fusion
  1.8 3.4 %collective-permute-start.3 = (bf16[512,640]{1,0:T(8,128)(2,1)S(1)}, bf16[512,640]{1,0:T(8,128)(2,1)S(1)}, u32[]{:S(2)}, u32[]{:S(2)}) collective-permute-start(bf16[512,640]{1,0:T(8,128)(2,1)S(1)} %slice_bitcast_fusion), channel_id=1, source_target_pairs={{0,8},{8,16},{16,24},{32,40},{40,48},{48,56},{64,72},{72,80},{80,8... | collective-permute-start | bytes 1966088 | tf_op jit(solution)/shard_map/ppermute | solution.py:51
  5.2 2.0 collective-permute-start.4
  7.9 9.1 %collective-permute-start.6 = (bf16[512,640]{1,0:T(8,128)(2,1)S(1)}, bf16[512,640]{1,0:T(8,128)(2,1)S(1)}, u32[]{:S(2)}, u32[]{:S(2)}) collective-permute-start(bf16[512,640]{1,0:T(8,128)(2,1)S(1)} %slice_bitcast_fusion), channel_id=1, source_target_pairs={{8,40},{16,48},{24,56},{40,72},{48,80},{56,88},{72,104},{80,112},{... | collective-permute-start | bytes 1966088 | tf_op jit(solution)/shard_map/ppermute | solution.py:39
  18.3 4.8 %shard_map.77 = f32[8,512]{1,0:T(8,128)} custom-call(f32[2]{0:T(128)} %pad_maximum_fusion.shares, bf16[3,512,640]{2,1,0:T(8,128)(2,1)} %clean.13, bf16[3,512,640]{2,1,0:T(8,128)(2,1)} %noise.13), custom_call_target="tpu_custom_call" | custom-call | flops 3932160 | bytes 2621440 | tf_op jit(solution)/shard_map/pallas_call | solution.py:86
  23.1 1.4 collective-permute-done
  25.2 1.0 collective-permute-start.1
  26.2 20.3 %collective-permute-done.1 = f32[8,512]{1,0:T(8,128)S(1)} collective-permute-done((f32[8,512]{1,0:T(8,128)S(1)}, f32[8,512]{1,0:T(8,128)S(1)}, u32[]{:S(2)}, u32[]{:S(2)}) %collective-permute-start.1) | collective-permute-done | bytes 16416 | tf_op jit(solution)/shard_map/ppermute | solution.py:344
  46.6 4.6 %collective-permute-done.2 = f32[8,512]{1,0:T(8,128)S(1)} collective-permute-done((f32[8,512]{1,0:T(8,128)S(1)}, f32[8,512]{1,0:T(8,128)S(1)}, u32[]{:S(2)}, u32[]{:S(2)}) %collective-permute-start.2) | collective-permute-done | bytes 16416 | tf_op jit(solution)/shard_map/ppermute | solution.py:344
  51.2 1.3 fusion.1
  54.4 1.9 collective-permute-start.10
  56.3 1.2 collective-permute-start.9
  57.5 14.7 %collective-permute-done.10 = bf16[512,256]{1,0:T(8,128)(2,1)S(1)} collective-permute-done((bf16[512,256]{1,0:T(8,128)(2,1)S(1)}, bf16[512,256]{1,0:T(8,128)(2,1)S(1)}, u32[]{:S(2)}, u32[]{:S(2)}) %collective-permute-start.10) | collective-permute-done | bytes 262176 | tf_op jit(solution)/shard_map/ppermute | solution.py:39
  72.2 1.9 collective-permute-start.11
  74.8 1.3 collective-permute-start.16
  76.2 11.6 %collective-permute-start.17 = (bf16[512,256]{1,0:T(8,128)(2,1)S(1)}, bf16[512,256]{1,0:T(8,128)(2,1)S(1)}, u32[]{:S(2)}, u32[]{:S(2)}) collective-permute-start(bf16[512,256]{1,0:T(8,128)(2,1)S(1)} %collective-permute-done.10), channel_id=1, source_target_pairs={{8,0},{16,8},{24,16},{40,32},{48,40},{56,48},{72,64},{80,72},{88,8... | collective-permute-start | bytes 786440 | tf_op jit(solution)/shard_map/ppermute | solution.py:51
  89.0 3.7 %collective-permute-done.11 = bf16[512,384]{1,0:T(8,128)(2,1)} collective-permute-done((bf16[512,384]{1,0:T(8,128)(2,1)S(1)}, bf16[512,384]{1,0:T(8,128)(2,1)}, u32[]{:S(2)}, u32[]{:S(2)}) %collective-permute-start.11) | collective-permute-done | bytes 393248 | tf_op jit(solution)/shard_map/ppermute | solution.py:39
  93.4 1.3 collective-permute-start.13
  94.7 5.7 %collective-permute-start.14 = (bf16[512,384]{1,0:T(8,128)(2,1)}, bf16[512,384]{1,0:T(8,128)(2,1)}, u32[]{:S(2)}, u32[]{:S(2)}) collective-permute-start(bf16[512,384]{1,0:T(8,128)(2,1)} %collective-permute-done.11), channel_id=1, source_target_pairs={{8,0},{16,8},{24,16},{40,32},{48,40},{56,48},{72,64},{80,72},{88,8... | collective-permute-start | bytes 1179656 | tf_op jit(solution)/shard_map/ppermute | solution.py:51
  102.4 11.9 %shard_map.78 = (bf16[512,640]{1,0:T(8,128)(2,1)}, f32[512,640]{1,0:T(8,128)}, f32[512,640]{1,0:T(8,128)}, f32[512,640]{1,0:T(8,128)}, bf16[2,512,256]{2,1,0:T(8...) custom-call(s32[9]{0:T(128)} %add_convert_fusion.3.flags, ...), custom_call_target="tpu_custom_call" | custom-call | flops 3221225472 | bytes 8388608 | tf_op jit(solution)/shard_map/pallas_call | solution.py:237
  114.4 2.1 collective-permute-start.19
  116.5 0.7 copy-done.12
  117.2 2.4 %collective-permute-start.20 = (bf16[2,512,256]{2,1,0:T(8,128)(2,1)}, bf16[2,512,256]{2,1,0:T(8,128)(2,1)S(1)}, u32[]{:S(2)}, u32[]{:S(2)}) collective-permute-start(bf16[2,512,256]{2,1,0:T(8,128)(2,1)} %get-tuple-element.55), channel_id=1, source_target_pairs={{0,8},{8,16},{16,24},{24,0},{32,40},{40,48},{48,56},{56,32},{64,72... | collective-permute-start | bytes 1572872 | tf_op jit(solution)/shard_map/ppermute | solution.py:51
  119.6 11.9 %shard_map.79 = (bf16[512,640]{1,0:T(8,128)(2,1)}, f32[512,640]{1,0:T(8,128)}, f32[512,640]{1,0:T(8,128)}, f32[512,640]{1,0:T(8,128)}, bf16[2,528,256]{2,1,0:T(8...) custom-call(s32[9]{0:T(128)} %add_convert_fusion.3.flags, ...), custom_call_target="tpu_custom_call", output_to_operand_aliasing={{0}: (17, {}), {1}: (18, {}), {2}: (19, {}), {3}: (20, {})} | custom-call | flops 3221225472 | bytes 8388608 | tf_op jit(solution)/shard_map/pallas_call | solution.py:237
  131.6 6.9 %shard_map.80 = (bf16[512,640]{1,0:T(8,128)(2,1)}, f32[512,640]{1,0:T(8,128)}, f32[512,640]{1,0:T(8,128)}, f32[512,640]{1,0:T(8,128)}, bf16[2,512,128]{2,1,0:T(8...) custom-call(s32[9]{0:T(128)} %add_convert_fusion.3.flags, ...), custom_call_target="tpu_custom_call", output_to_operand_aliasing={{0}: (17, {}), {1}: (18, {}), {2}: (19, {}), {3}: (20, {})} | custom-call | flops 1610612736 | bytes 4194304 | tf_op jit(solution)/shard_map/pallas_call | solution.py:237
  139.3 1.8 collective-permute-done.20.in_3
  141.1 1.2 collective-permute-done.21
  142.5 3.5 %collective-permute-done.22 = f32[8,512]{1,0:T(8,128)S(1)} collective-permute-done((f32[8,512]{1,0:T(8,128)S(1)}, f32[8,512]{1,0:T(8,128)S(1)}, u32[]{:S(2)}, u32[]{:S(2)}) %collective-permute-start.22) | collective-permute-done | bytes 16416 | tf_op jit(solution)/shard_map/ppermute | solution.py:344
  146.1 4.6 %collective-permute-done.23 = f32[8,512]{1,0:T(8,128)S(1)} collective-permute-done((f32[8,512]{1,0:T(8,128)S(1)}, f32[8,512]{1,0:T(8,128)S(1)}, u32[]{:S(2)}, u32[]{:S(2)}) %collective-permute-start.23) | collective-permute-done | bytes 16416 | tf_op jit(solution)/shard_map/ppermute | solution.py:344
  152.1 1.7 collective-permute-start.25
  153.7 2.6 %collective-permute-start.24 = (bf16[2,528,256]{2,1,0:T(8,128)(2,1)}, bf16[2,528,256]{2,1,0:T(8,128)(2,1)S(1)}, u32[]{:S(2)}, u32[]{:S(2)}) collective-permute-start(bf16[2,528,256]{2,1,0:T(8,128)(2,1)} %get-tuple-element.60), channel_id=1, source_target_pairs={{0,24},{8,0},{16,8},{24,16},{32,56},{40,32},{48,40},{56,48},{64,88... | collective-permute-start | bytes 1622024 | tf_op jit(solution)/shard_map/ppermute | solution.py:51
  156.7 6.3 %collective-permute-start.28 = (bf16[2,512,256]{2,1,0:T(8,128)(2,1)S(1)}, bf16[2,512,256]{2,1,0:T(8,128)(2,1)S(1)}, u32[]{:S(2)}, u32[]{:S(2)}) collective-permute-start(bf16[2,512,256]{2,1,0:T(8,128)(2,1)S(1)} %add_convert_fusion.1), channel_id=1, source_target_pairs={{40,8},{48,16},{56,24},{72,40},{80,48},{88,56},{104,72},{112,80},{... | collective-permute-start | bytes 1572872 | tf_op jit(solution)/shard_map/ppermute | solution.py:39
  163.1 3.8 %collective-permute-done.26.in_3 = bf16[2,528,256]{2,1,0:T(8,128)(2,1)S(1)} collective-permute-done((bf16[2,528,256]{2,1,0:T(8,128)(2,1)}, bf16[2,528,256]{2,1,0:T(8,128)(2,1)S(1)}, u32[]{:S(2)}, u32[]{:S(2)}) %collective-permute-start.26) | collective-permute-done | bytes 540704 | tf_op jit(solution)/shard_map/ppermute | solution.py:51
  166.8 2.2 collective-permute-done.25.in_2
  169.0 8.3 %collective-permute-done.24.in_1 = bf16[2,528,256]{2,1,0:T(8,128)(2,1)S(1)} collective-permute-done((bf16[2,528,256]{2,1,0:T(8,128)(2,1)}, bf16[2,528,256]{2,1,0:T(8,128)(2,1)S(1)}, u32[]{:S(2)}, u32[]{:S(2)}) %collective-permute-start.24) | collective-permute-done | bytes 540704 | tf_op jit(solution)/shard_map/ppermute | solution.py:51
  177.6 6.8 %collective-permute-start.27 = (bf16[2,528,256]{2,1,0:T(8,128)(2,1)S(1)}, bf16[2,528,256]{2,1,0:T(8,128)(2,1)S(1)}, u32[]{:S(2)}, u32[]{:S(2)}) collective-permute-start(bf16[2,528,256]{2,1,0:T(8,128)(2,1)S(1)} %add_convert_fusion), channel_id=1, source_target_pairs={{40,8},{48,16},{56,24},{72,40},{80,48},{88,56},{104,72},{112,80},{... | collective-permute-start | bytes 1622024 | tf_op jit(solution)/shard_map/ppermute | solution.py:39
  184.5 0.8 collective-permute-done.28.crossed
  185.2 1.5 collective-permute-start.30
  186.8 2.2 collective-permute-start.31
  189.0 4.6 %collective-permute-done.29.in_1 = bf16[2,512,128]{2,1,0:T(8,128)(2,1)S(1)} collective-permute-done((bf16[2,512,128]{2,1,0:T(8,128)(2,1)S(1)}, bf16[2,512,128]{2,1,0:T(8,128)(2,1)S(1)}, u32[]{:S(2)}, u32[]{:S(2)}) %collective-permute-start.29) | collective-permute-done | bytes 262176 | tf_op jit(solution)/shard_map/ppermute | solution.py:51
  193.6 4.6 %collective-permute-done.30.in_2 = bf16[2,512,128]{2,1,0:T(8,128)(2,1)S(1)} collective-permute-done((bf16[2,512,128]{2,1,0:T(8,128)(2,1)S(1)}, bf16[2,512,128]{2,1,0:T(8,128)(2,1)S(1)}, u32[]{:S(2)}, u32[]{:S(2)}) %collective-permute-start.30) | collective-permute-done | bytes 262176 | tf_op jit(solution)/shard_map/ppermute | solution.py:51
  198.2 1.6 collective-permute-done.31.in_3
  200.0 5.5 %collective-permute-start.32 = (bf16[2,512,128]{2,1,0:T(8,128)(2,1)S(1)}, bf16[2,512,128]{2,1,0:T(8,128)(2,1)S(1)}, u32[]{:S(2)}, u32[]{:S(2)}) collective-permute-start(bf16[2,512,128]{2,1,0:T(8,128)(2,1)S(1)} %add_convert_fusion.2), channel_id=1, source_target_pairs={{40,8},{48,16},{56,24},{72,40},{80,48},{88,56},{104,72},{112,80},{... | collective-permute-start | bytes 786440 | tf_op jit(solution)/shard_map/ppermute | solution.py:39
  205.5 8.7 %collective-permute-done.27.crossed = bf16[2,528,256]{2,1,0:T(8,128)(2,1)S(1)} collective-permute-done((bf16[2,528,256]{2,1,0:T(8,128)(2,1)S(1)}, bf16[2,528,256]{2,1,0:T(8,128)(2,1)S(1)}, u32[]{:S(2)}, u32[]{:S(2)}) %collective-permute-start.27) | collective-permute-done | bytes 540704 | tf_op jit(solution)/shard_map/ppermute | solution.py:39
  214.3 0.8 copy-done.16
  215.8 4.2 %shard_map.81.refs_0_ = f32[3,512,640]{2,1,0:T(8,128)} custom-call(s32[9]{0:T(128)} %add_convert_fusion.3.flags, f32[2]{0:T(128)} %pad_maximum_fusion.shares, f32[8,512]{1,0:T(8,128)} %concatenate.12.rows_ref, f32[1,640]{1,0:T(1,128)} %broadcast_in_dim.31.gain_q, f32[1,640]{1,0:T(1,128)} %broadcast_in_dim.32.gain_k, bf16[3,512,640]{2,1,0:T(8,128)(2,1)} %clean.13, ...), custom_call_target="tpu_custom_call" | custom-call | flops 3932160 | bytes 6291456 | tf_op jit(solution)/shard_map/pallas_call | solution.py:320
  220.0 4.0 %shard_map.82.refs_0_ = f32[3,512,640]{2,1,0:T(8,128)} custom-call(s32[9]{0:T(128)} %add_convert_fusion.3.flags, f32[2]{0:T(128)} %pad_maximum_fusion.shares, f32[8,512]{1,0:T(8,128)} %concatenate.12.rows_ref, f32[1,640]{1,0:T(1,128)} %broadcast_in_dim.31.gain_q, f32[1,640]{1,0:T(1,128)} %broadcast_in_dim.32.gain_k, ...), custom_call_target="tpu_custom_call", output_to_operand_aliasing={{}: (14, {})} | custom-call | flops 3932160 | bytes 6291456 | tf_op jit(solution)/shard_map/pallas_call | solution.py:320
  224.7 3.2 %shard_map.83 = f32[3,512,640]{2,1,0:T(8,128)} custom-call(s32[9]{0:T(128)} %add_convert_fusion.3.flags, f32[2]{0:T(128)} %pad_maximum_fusion.shares, f32[8,512]{1,0:T(8,128)} %concatenate.12.rows_ref, f32[1,640]{1,0:T(1,128)} %broadcast_in_dim.31.gain_q, f32[1,640]{1,0:T(1,128)} %broadcast_in_dim.32.gain_k, ...), custom_call_target="tpu_custom_call", output_to_operand_aliasing={{}: (14, {})} | custom-call | flops 1966080 | bytes 3145728 | tf_op jit(solution)/shard_map/pallas_call | solution.py:320
  (124 shorter events, 13.0 us)
Async XLA Ops:
  1.8 50.8 %collective-permute-start.3 = (bf16[512,640]{1,0:T(8,128)(2,1)S(1)}, bf16[512,640]{1,0:T(8,128)(2,1)S(1)}, u32[]{:S(2)}, u32[]{:S(2)}) collective-permute-start(bf16[512,640]{1,0:T(8,128)(2,1)S(1)} %slice_bitcast_fusion), channel_id=1, source_target_pairs={{0,8},{8,16},{16,24},{32,40},{40,48},{48,56},{64,72},{72,80},{80,8... | collective-permute-start | bytes 1966088 | tf_op jit(solution)/shard_map/ppermute | solution.py:51
  5.2 47.4 %collective-permute-start.4 = (bf16[512,640]{1,0:T(8,128)(2,1)S(1)}, bf16[512,640]{1,0:T(8,128)(2,1)S(1)}, u32[]{:S(2)}, u32[]{:S(2)}) collective-permute-start(bf16[512,640]{1,0:T(8,128)(2,1)S(1)} %slice_bitcast_fusion), channel_id=1, source_target_pairs={{0,16},{8,24},{32,48},{40,56},{64,80},{72,88},{96,112},{104,120},{... | collective-permute-start | bytes 1966088 | tf_op jit(solution)/shard_map/ppermute | solution.py:51
  7.2 45.4 %collective-permute-start.5 = (bf16[512,640]{1,0:T(8,128)(2,1)S(1)}, bf16[512,640]{1,0:T(8,128)(2,1)S(1)}, u32[]{:S(2)}, u32[]{:S(2)}) collective-permute-start(bf16[512,640]{1,0:T(8,128)(2,1)S(1)} %slice_bitcast_fusion), channel_id=1, source_target_pairs={{0,24},{32,56},{64,88},{96,120},{128,152},{160,184},{192,216},{224... | collective-permute-start | bytes 1966088 | tf_op jit(solution)/shard_map/ppermute | solution.py:51
  7.9 44.7 %collective-permute-start.6 = (bf16[512,640]{1,0:T(8,128)(2,1)S(1)}, bf16[512,640]{1,0:T(8,128)(2,1)S(1)}, u32[]{:S(2)}, u32[]{:S(2)}) collective-permute-start(bf16[512,640]{1,0:T(8,128)(2,1)S(1)} %slice_bitcast_fusion), channel_id=1, source_target_pairs={{8,40},{16,48},{24,56},{40,72},{48,80},{56,88},{72,104},{80,112},{... | collective-permute-start | bytes 1966088 | tf_op jit(solution)/shard_map/ppermute | solution.py:39
  18.3 32.9 %copy-start.21 = (f32[640]{0:T(1024)S(1)}, f32[640]{0:T(1024)}, u32[]{:S(2)}) copy-start(f32[640]{0:T(1024)} %param.10) | copy-start | bytes 7684
  23.1 1.4 collective-permute-start
  25.2 21.3 %collective-permute-start.1 = (f32[8,512]{1,0:T(8,128)S(1)}, f32[8,512]{1,0:T(8,128)S(1)}, u32[]{:S(2)}, u32[]{:S(2)}) collective-permute-start(f32[8,512]{1,0:T(8,128)S(1)} %add.176), channel_id=1, source_target_pairs={{0,2},{1,3},{2,0},{3,1},{4,6},{5,7},{6,4},{7,5},{8,10},{9,11},{10,... | collective-permute-start | bytes 49160 | tf_op jit(solution)/shard_map/ppermute | solution.py:344
  46.5 4.6 %collective-permute-start.2 = (f32[8,512]{1,0:T(8,128)S(1)}, f32[8,512]{1,0:T(8,128)S(1)}, u32[]{:S(2)}, u32[]{:S(2)}) collective-permute-start(f32[8,512]{1,0:T(8,128)S(1)} %add.177), channel_id=1, source_target_pairs={{0,4},{1,5},{2,6},{3,7},{4,0},{5,1},{6,2},{7,3},{8,12},{9,13},{10,... | collective-permute-start | bytes 49160 | tf_op jit(solution)/shard_map/ppermute | solution.py:344
  53.8 34.6 %copy-start.24 = (f32[640]{0:T(1024)S(1)}, f32[640]{0:T(1024)}, u32[]{:S(2)}) copy-start(f32[640]{0:T(1024)} %param.9) | copy-start | bytes 7684
  53.8 21.0 %collective-permute-start.7 = (bf16[512,640]{1,0:T(8,128)(2,1)S(1)}, bf16[512,640]{1,0:T(8,128)(2,1)S(1)}, u32[]{:S(2)}, u32[]{:S(2)}) collective-permute-start(bf16[512,640]{1,0:T(8,128)(2,1)S(1)} %get-tuple-element.74), channel_id=1, source_target_pairs={{0,8},{8,16},{16,24},{24,0},{32,40},{40,48},{48,56},{56,32},{64,72... | collective-permute-start | bytes 1966088 | tf_op jit(solution)/shard_map/ppermute | solution.py:51
  54.4 21.8 %collective-permute-start.8 = (bf16[512,640]{1,0:T(8,128)(2,1)S(1)}, bf16[512,640]{1,0:T(8,128)(2,1)S(1)}, u32[]{:S(2)}, u32[]{:S(2)}) collective-permute-start(bf16[512,640]{1,0:T(8,128)(2,1)S(1)} %get-tuple-element.73), channel_id=1, source_target_pairs={{0,16},{8,24},{16,0},{24,8},{32,48},{40,56},{48,32},{56,40},{64,80... | collective-permute-start | bytes 1966088 | tf_op jit(solution)/shard_map/ppermute | solution.py:51
  54.4 17.8 %collective-permute-start.10 = (bf16[512,256]{1,0:T(8,128)(2,1)S(1)}, bf16[512,256]{1,0:T(8,128)(2,1)S(1)}, u32[]{:S(2)}, u32[]{:S(2)}) collective-permute-start(bf16[512,256]{1,0:T(8,128)(2,1)S(1)} %slice.110), channel_id=1, source_target_pairs={{8,40},{16,48},{24,56},{40,72},{48,80},{56,88},{72,104},{80,112},{... | collective-permute-start | bytes 786440 | tf_op jit(solution)/shard_map/ppermute | solution.py:39
  56.3 32.7 %collective-permute-start.9 = (bf16[512,640]{1,0:T(8,128)(2,1)S(1)}, bf16[512,640]{1,0:T(8,128)(2,1)S(1)}, u32[]{:S(2)}, u32[]{:S(2)}) collective-permute-start(bf16[512,640]{1,0:T(8,128)(2,1)S(1)} %get-tuple-element.72), channel_id=1, source_target_pairs={{0,24},{8,0},{16,8},{24,16},{32,56},{40,32},{48,40},{56,48},{64,88... | collective-permute-start | bytes 1966088 | tf_op jit(solution)/shard_map/ppermute | solution.py:51
  72.2 20.5 %collective-permute-start.11 = (bf16[512,384]{1,0:T(8,128)(2,1)S(1)}, bf16[512,384]{1,0:T(8,128)(2,1)}, u32[]{:S(2)}, u32[]{:S(2)}) collective-permute-start(bf16[512,384]{1,0:T(8,128)(2,1)S(1)} %slice.109), channel_id=1, source_target_pairs={{8,40},{16,48},{24,56},{40,72},{48,80},{56,88},{72,104},{80,112},{... | collective-permute-start | bytes 1179656 | tf_op jit(solution)/shard_map/ppermute | solution.py:39
  74.1 20.6 %collective-permute-start.15 = (bf16[512,256]{1,0:T(8,128)(2,1)S(1)}, bf16[512,256]{1,0:T(8,128)(2,1)S(1)}, u32[]{:S(2)}, u32[]{:S(2)}) collective-permute-start(bf16[512,256]{1,0:T(8,128)(2,1)S(1)} %collective-permute-done.10), channel_id=1, source_target_pairs={{24,0},{56,32},{88,64},{120,96},{152,128},{184,160},{216,192},{248... | collective-permute-start | bytes 786440 | tf_op jit(solution)/shard_map/ppermute | solution.py:51
  74.8 26.2 %copy-start.3 = (bf16[512,640]{1,0:T(8,128)(2,1)}, bf16[512,640]{1,0:T(8,128)(2,1)S(1)}, u32[]{:S(2)}) copy-start(bf16[512,640]{1,0:T(8,128)(2,1)S(1)} %collective-permute-done.7.both_1) | copy-start | bytes 1966084
  74.8 26.1 %collective-permute-start.16 = (bf16[512,256]{1,0:T(8,128)(2,1)S(1)}, bf16[512,256]{1,0:T(8,128)(2,1)S(1)}, u32[]{:S(2)}, u32[]{:S(2)}) collective-permute-start(bf16[512,256]{1,0:T(8,128)(2,1)S(1)} %collective-permute-done.10), channel_id=1, source_target_pairs={{16,0},{24,8},{48,32},{56,40},{80,64},{88,72},{112,96},{120,104},{... | collective-permute-start | bytes 786440 | tf_op jit(solution)/shard_map/ppermute | solution.py:51
  76.2 24.8 %collective-permute-start.17 = (bf16[512,256]{1,0:T(8,128)(2,1)S(1)}, bf16[512,256]{1,0:T(8,128)(2,1)S(1)}, u32[]{:S(2)}, u32[]{:S(2)}) collective-permute-start(bf16[512,256]{1,0:T(8,128)(2,1)S(1)} %collective-permute-done.10), channel_id=1, source_target_pairs={{8,0},{16,8},{24,16},{40,32},{48,40},{56,48},{72,64},{80,72},{88,8... | collective-permute-start | bytes 786440 | tf_op jit(solution)/shard_map/ppermute | solution.py:51
  92.7 23.8 %collective-permute-start.12 = (bf16[512,384]{1,0:T(8,128)(2,1)}, bf16[512,384]{1,0:T(8,128)(2,1)S(1)}, u32[]{:S(2)}, u32[]{:S(2)}) collective-permute-start(bf16[512,384]{1,0:T(8,128)(2,1)} %collective-permute-done.11), channel_id=1, source_target_pairs={{24,0},{56,32},{88,64},{120,96},{152,128},{184,160},{216,192},{248... | collective-permute-start | bytes 1179656 | tf_op jit(solution)/shard_map/ppermute | solution.py:51
  93.4 26.2 %collective-permute-start.13 = (bf16[512,384]{1,0:T(8,128)(2,1)}, bf16[512,384]{1,0:T(8,128)(2,1)}, u32[]{:S(2)}, u32[]{:S(2)}) collective-permute-start(bf16[512,384]{1,0:T(8,128)(2,1)} %collective-permute-done.11), channel_id=1, source_target_pairs={{16,0},{24,8},{48,32},{56,40},{80,64},{88,72},{112,96},{120,104},{... | collective-permute-start | bytes 1179656 | tf_op jit(solution)/shard_map/ppermute | solution.py:51
  94.7 24.9 %collective-permute-start.14 = (bf16[512,384]{1,0:T(8,128)(2,1)}, bf16[512,384]{1,0:T(8,128)(2,1)}, u32[]{:S(2)}, u32[]{:S(2)}) collective-permute-start(bf16[512,384]{1,0:T(8,128)(2,1)} %collective-permute-done.11), channel_id=1, source_target_pairs={{8,0},{16,8},{24,16},{40,32},{48,40},{56,48},{72,64},{80,72},{88,8... | collective-permute-start | bytes 1179656 | tf_op jit(solution)/shard_map/ppermute | solution.py:51
  114.3 25.0 %collective-permute-start.18 = (bf16[2,512,256]{2,1,0:T(8,128)(2,1)}, bf16[2,512,256]{2,1,0:T(8,128)(2,1)S(1)}, u32[]{:S(2)}, u32[]{:S(2)}) collective-permute-start(bf16[2,512,256]{2,1,0:T(8,128)(2,1)} %get-tuple-element.53), channel_id=1, source_target_pairs={{0,24},{8,0},{16,8},{24,16},{32,56},{40,32},{48,40},{56,48},{64,88... | collective-permute-start | bytes 1572872 | tf_op jit(solution)/shard_map/ppermute | solution.py:51
  114.4 24.9 %collective-permute-start.19 = (bf16[2,512,256]{2,1,0:T(8,128)(2,1)}, bf16[2,512,256]{2,1,0:T(8,128)(2,1)S(1)}, u32[]{:S(2)}, u32[]{:S(2)}) collective-permute-start(bf16[2,512,256]{2,1,0:T(8,128)(2,1)} %get-tuple-element.54), channel_id=1, source_target_pairs={{0,16},{8,24},{16,0},{24,8},{32,48},{40,56},{48,32},{56,40},{64,80... | collective-permute-start | bytes 1572872 | tf_op jit(solution)/shard_map/ppermute | solution.py:51
  117.2 23.9 %collective-permute-start.20 = (bf16[2,512,256]{2,1,0:T(8,128)(2,1)}, bf16[2,512,256]{2,1,0:T(8,128)(2,1)S(1)}, u32[]{:S(2)}, u32[]{:S(2)}) collective-permute-start(bf16[2,512,256]{2,1,0:T(8,128)(2,1)} %get-tuple-element.55), channel_id=1, source_target_pairs={{0,8},{8,16},{16,24},{24,0},{32,40},{40,48},{48,56},{56,32},{64,72... | collective-permute-start | bytes 1572872 | tf_op jit(solution)/shard_map/ppermute | solution.py:51
  139.3 38.3 %copy-start.9 = (bf16[2,512,256]{2,1,0:T(8,128)(2,1)}, bf16[2,512,256]{2,1,0:T(8,128)(2,1)S(1)}, u32[]{:S(2)}) copy-start(bf16[2,512,256]{2,1,0:T(8,128)(2,1)S(1)} %collective-permute-done.18.in_1) | copy-start | bytes 1572868
  139.3 38.3 %copy-start.10 = (bf16[2,512,256]{2,1,0:T(8,128)(2,1)}, bf16[2,512,256]{2,1,0:T(8,128)(2,1)S(1)}, u32[]{:S(2)}) copy-start(bf16[2,512,256]{2,1,0:T(8,128)(2,1)S(1)} %collective-permute-done.19.in_2) | copy-start | bytes 1572868
  141.1 36.5 %copy-start.11 = (bf16[2,512,256]{2,1,0:T(8,128)(2,1)}, bf16[2,512,256]{2,1,0:T(8,128)(2,1)S(1)}, u32[]{:S(2)}) copy-start(bf16[2,512,256]{2,1,0:T(8,128)(2,1)S(1)} %collective-permute-done.20.in_3) | copy-start | bytes 1572868
  141.1 1.2 collective-permute-start.21
  142.3 3.7 %collective-permute-start.22 = (f32[8,512]{1,0:T(8,128)S(1)}, f32[8,512]{1,0:T(8,128)S(1)}, u32[]{:S(2)}, u32[]{:S(2)}) collective-permute-start(f32[8,512]{1,0:T(8,128)S(1)} %add.186), channel_id=1, source_target_pairs={{0,2},{1,3},{2,0},{3,1},{4,6},{5,7},{6,4},{7,5},{8,10},{9,11},{10,... | collective-permute-start | bytes 49160 | tf_op jit(solution)/shard_map/ppermute | solution.py:344
  146.1 4.6 %collective-permute-start.23 = (f32[8,512]{1,0:T(8,128)S(1)}, f32[8,512]{1,0:T(8,128)S(1)}, u32[]{:S(2)}, u32[]{:S(2)}) collective-permute-start(f32[8,512]{1,0:T(8,128)S(1)} %add.187), channel_id=1, source_target_pairs={{0,4},{1,5},{2,6},{3,7},{4,0},{5,1},{6,2},{7,3},{8,12},{9,13},{10,... | collective-permute-start | bytes 49160 | tf_op jit(solution)/shard_map/ppermute | solution.py:344
  151.4 15.4 %collective-permute-start.26 = (bf16[2,528,256]{2,1,0:T(8,128)(2,1)}, bf16[2,528,256]{2,1,0:T(8,128)(2,1)S(1)}, u32[]{:S(2)}, u32[]{:S(2)}) collective-permute-start(bf16[2,528,256]{2,1,0:T(8,128)(2,1)} %get-tuple-element.62), channel_id=1, source_target_pairs={{0,8},{8,16},{16,24},{24,0},{32,40},{40,48},{48,56},{56,32},{64,72... | collective-permute-start | bytes 1622024 | tf_op jit(solution)/shard_map/ppermute | solution.py:51
  152.1 16.9 %collective-permute-start.25 = (bf16[2,528,256]{2,1,0:T(8,128)(2,1)}, bf16[2,528,256]{2,1,0:T(8,128)(2,1)S(1)}, u32[]{:S(2)}, u32[]{:S(2)}) collective-permute-start(bf16[2,528,256]{2,1,0:T(8,128)(2,1)} %get-tuple-element.61), channel_id=1, source_target_pairs={{0,16},{8,24},{16,0},{24,8},{32,48},{40,56},{48,32},{56,40},{64,80... | collective-permute-start | bytes 1622024 | tf_op jit(solution)/shard_map/ppermute | solution.py:51
  153.7 23.5 %collective-permute-start.24 = (bf16[2,528,256]{2,1,0:T(8,128)(2,1)}, bf16[2,528,256]{2,1,0:T(8,128)(2,1)S(1)}, u32[]{:S(2)}, u32[]{:S(2)}) collective-permute-start(bf16[2,528,256]{2,1,0:T(8,128)(2,1)} %get-tuple-element.60), channel_id=1, source_target_pairs={{0,24},{8,0},{16,8},{24,16},{32,56},{40,32},{48,40},{56,48},{64,88... | collective-permute-start | bytes 1622024 | tf_op jit(solution)/shard_map/ppermute | solution.py:51
  156.7 28.6 %copy-start.27 = (bf16[2,512,128]{2,1,0:T(8,128)(2,1)S(1)}, bf16[2,512,128]{2,1,0:T(8,128)(2,1)}, u32[]{:S(2)}) copy-start(bf16[2,512,128]{2,1,0:T(8,128)(2,1)} %get-tuple-element.69) | copy-start | bytes 786436
  156.7 28.6 %copy-start.26 = (bf16[2,512,128]{2,1,0:T(8,128)(2,1)S(1)}, bf16[2,512,128]{2,1,0:T(8,128)(2,1)}, u32[]{:S(2)}) copy-start(bf16[2,512,128]{2,1,0:T(8,128)(2,1)} %get-tuple-element.70) | copy-start | bytes 786436
  156.7 30.1 %copy-start.25 = (bf16[2,512,128]{2,1,0:T(8,128)(2,1)S(1)}, bf16[2,512,128]{2,1,0:T(8,128)(2,1)}, u32[]{:S(2)}) copy-start(bf16[2,512,128]{2,1,0:T(8,128)(2,1)} %get-tuple-element.71) | copy-start | bytes 786436
  156.7 28.5 %collective-permute-start.28 = (bf16[2,512,256]{2,1,0:T(8,128)(2,1)S(1)}, bf16[2,512,256]{2,1,0:T(8,128)(2,1)S(1)}, u32[]{:S(2)}, u32[]{:S(2)}) collective-permute-start(bf16[2,512,256]{2,1,0:T(8,128)(2,1)S(1)} %add_convert_fusion.1), channel_id=1, source_target_pairs={{40,8},{48,16},{56,24},{72,40},{80,48},{88,56},{104,72},{112,80},{... | collective-permute-start | bytes 1572872 | tf_op jit(solution)/shard_map/ppermute | solution.py:39
  163.0 52.1 %copy-start.20 = (f32[8,512]{1,0:T(8,128)S(1)}, f32[8,512]{1,0:T(8,128)}, u32[]{:S(2)}) copy-start(f32[8,512]{1,0:T(8,128)} %copy-done.19) | copy-start | bytes 49156
  163.1 52.1 %slice-start = ((f32[8,512]{1,0:T(8,128)}), f32[3,512]{1,0:T(4,128)S(1)}, s32[]{:S(2)}) async-start(f32[8,512]{1,0:T(8,128)} %copy-done.19), calls=%async_computation | async-start | bytes 16384 | tf_op jit(solution)/shard_map/slice | solution.py:442
  166.8 33.2 %copy-start.6 = (bf16[2,528,256]{2,1,0:T(8,128)(2,1)}, bf16[2,528,256]{2,1,0:T(8,128)(2,1)S(1)}, u32[]{:S(2)}) copy-start(bf16[2,528,256]{2,1,0:T(8,128)(2,1)S(1)} %collective-permute-done.26.in_3) | copy-start | bytes 1622020
  169.0 31.0 %copy-start.7 = (bf16[2,528,256]{2,1,0:T(8,128)(2,1)}, bf16[2,528,256]{2,1,0:T(8,128)(2,1)S(1)}, u32[]{:S(2)}) copy-start(bf16[2,528,256]{2,1,0:T(8,128)(2,1)S(1)} %collective-permute-done.25.in_2) | copy-start | bytes 1622020
  177.6 36.6 %collective-permute-start.27 = (bf16[2,528,256]{2,1,0:T(8,128)(2,1)S(1)}, bf16[2,528,256]{2,1,0:T(8,128)(2,1)S(1)}, u32[]{:S(2)}, u32[]{:S(2)}) collective-permute-start(bf16[2,528,256]{2,1,0:T(8,128)(2,1)S(1)} %add_convert_fusion), channel_id=1, source_target_pairs={{40,8},{48,16},{56,24},{72,40},{80,48},{88,56},{104,72},{112,80},{... | collective-permute-start | bytes 1622024 | tf_op jit(solution)/shard_map/ppermute | solution.py:39
  185.2 29.8 %copy-start.17 = (bf16[2,512,256]{2,1,0:T(8,128)(2,1)}, bf16[2,512,256]{2,1,0:T(8,128)(2,1)S(1)}, u32[]{:S(2)}) copy-start(bf16[2,512,256]{2,1,0:T(8,128)(2,1)S(1)} %collective-permute-done.28.crossed) | copy-start | bytes 1572868
  185.2 8.4 %collective-permute-start.29 = (bf16[2,512,128]{2,1,0:T(8,128)(2,1)S(1)}, bf16[2,512,128]{2,1,0:T(8,128)(2,1)S(1)}, u32[]{:S(2)}, u32[]{:S(2)}) collective-permute-start(bf16[2,512,128]{2,1,0:T(8,128)(2,1)S(1)} %copy-done.27), channel_id=1, source_target_pairs={{0,24},{8,0},{16,8},{24,16},{32,56},{40,32},{48,40},{56,48},{64,88... | collective-permute-start | bytes 786440 | tf_op jit(solution)/shard_map/ppermute | solution.py:51
  185.2 12.9 %collective-permute-start.30 = (bf16[2,512,128]{2,1,0:T(8,128)(2,1)S(1)}, bf16[2,512,128]{2,1,0:T(8,128)(2,1)S(1)}, u32[]{:S(2)}, u32[]{:S(2)}) collective-permute-start(bf16[2,512,128]{2,1,0:T(8,128)(2,1)S(1)} %copy-done.26), channel_id=1, source_target_pairs={{0,16},{8,24},{16,0},{24,8},{32,48},{40,56},{48,32},{56,40},{64,80... | collective-permute-start | bytes 786440 | tf_op jit(solution)/shard_map/ppermute | solution.py:51
  186.8 13.0 %collective-permute-start.31 = (bf16[2,512,128]{2,1,0:T(8,128)(2,1)S(1)}, bf16[2,512,128]{2,1,0:T(8,128)(2,1)S(1)}, u32[]{:S(2)}, u32[]{:S(2)}) collective-permute-start(bf16[2,512,128]{2,1,0:T(8,128)(2,1)S(1)} %copy-done.25), channel_id=1, source_target_pairs={{0,8},{8,16},{16,24},{24,0},{32,40},{40,48},{48,56},{56,32},{64,72... | collective-permute-start | bytes 786440 | tf_op jit(solution)/shard_map/ppermute | solution.py:51
  193.6 26.4 %copy-start.13 = (bf16[2,512,128]{2,1,0:T(8,128)(2,1)}, bf16[2,512,128]{2,1,0:T(8,128)(2,1)S(1)}, u32[]{:S(2)}) copy-start(bf16[2,512,128]{2,1,0:T(8,128)(2,1)S(1)} %collective-permute-done.29.in_1) | copy-start | bytes 786436
  200.0 24.0 %collective-permute-start.32 = (bf16[2,512,128]{2,1,0:T(8,128)(2,1)S(1)}, bf16[2,512,128]{2,1,0:T(8,128)(2,1)S(1)}, u32[]{:S(2)}, u32[]{:S(2)}) collective-permute-start(bf16[2,512,128]{2,1,0:T(8,128)(2,1)S(1)} %add_convert_fusion.2), channel_id=1, source_target_pairs={{40,8},{48,16},{56,24},{72,40},{80,48},{88,56},{104,72},{112,80},{... | collective-permute-start | bytes 786440 | tf_op jit(solution)/shard_map/ppermute | solution.py:39
  (17 other events, 130.2 us)

commit v5 on v4

--- a/solution.py
+++ b/solution.py
@@ -422,7 +422,7 @@
     ]
     back_1 = send_back(after(tuple(kept), *back_0))
     crossed_1 = cross_back(back_1)
-    back_2 = send_back(after(tuple(back), *back_1, crossed_0))
+    back_2 = send_back(after(tuple(back), totals, crossed_0))
     crossed_2 = cross_back(back_2)
 
     def products_of(block):

time: 232 us -> 239 us (1.030)
  waiting for transfers between devices: 90.5 us -> 99.7 us
    ppermute x6, waiting for transfers between devices: 27.9 us -> 57 us  [shift_spans(): return lax.ppermute(block, 'tm', route)]
    ppermute x21, waiting for transfers between devices: 26.9 us -> 7.04 us  [shift_columns(): return lax.ppermute(block, 'tm', route)]
  transfers between devices with their start and end apart: 33 -> 33, of which waited for: 17 -> 14; matrix products, arithmetic and copies ran while one was open for 3% -> 3% of each run, Pallas kernels for 19% -> 19%
where the time goes in v5:
time: 239 us; the launch traced here: 236 us
  waiting for transfers between devices  99.7 us (42%)
  starting transfers between devices  73.5 us (31%)
  Pallas kernels  46.9 us (20%)
  local copies, waits for them, and re-layouts  8.4 us (4%)
  other arithmetic  4.99 us (2%)
    ppermute x6, waiting for transfers between devices, shift_spans(): return lax.ppermute(block, 'tm', route)  57 us
    ppermute x21, starting transfers between devices, shift_columns(): return lax.ppermute(block, 'tm', route)  40.6 us
    ppermute x6, waiting for transfers between devices, head_sum(): block = block + lax.ppermute(block, 'head', route)  35.7 us
    ppermute x6, starting transfers between devices, shift_spans(): return lax.ppermute(block, 'tm', route)  31.7 us
    pallas_call x3, Pallas kernels, attention_chunk(): pl.pallas_call(attention_body, grid=(heads,), in_specs=in_specs, out_spec...  30.8 us
    pallas_call x3, Pallas kernels, finish_chunk(): pl.pallas_call(finish_body, grid=(heads,), in_specs=in_specs, out_specs=p...  11.4 us
    ppermute x21, waiting for transfers between devices, shift_columns(): return lax.ppermute(block, 'tm', route)  7.04 us
    pallas_call x1, Pallas kernels, prepare(): pl.pallas_call(prepare_body, grid=(width // HEAD_DIM,), in_specs=[pl.Bloc...  4.79 us
  transfers between devices with their start and end apart: 33, of which 14 were waited for; matrix products, arithmetic and copies ran while one was open for 3% of the time, Pallas kernels for 19%

profile of v5, /device:TPU:26, one launch (start us, length us, event | category | flops | bytes accessed | tf_op | source)
XLA Modules:
  0.0 235.6 jit_solution(8425383839138693514)
XLA Ops:
  0.6 1.1 slice_bitcast_fusion
  1.8 3.4 %collective-permute-start.3 = (bf16[512,640]{1,0:T(8,128)(2,1)S(1)}, bf16[512,640]{1,0:T(8,128)(2,1)S(1)}, u32[]{:S(2)}, u32[]{:S(2)}) collective-permute-start(bf16[512,640]{1,0:T(8,128)(2,1)S(1)} %slice_bitcast_fusion), channel_id=1, source_target_pairs={{0,8},{8,16},{16,24},{32,40},{40,48},{48,56},{64,72},{72,80},{80,8... | collective-permute-start | bytes 1966088 | tf_op jit(solution)/shard_map/ppermute | solution.py:51
  5.2 2.0 collective-permute-start.4
  7.2 0.7 collective-permute-start.5
  7.9 9.1 %collective-permute-start.6 = (bf16[512,640]{1,0:T(8,128)(2,1)S(1)}, bf16[512,640]{1,0:T(8,128)(2,1)S(1)}, u32[]{:S(2)}, u32[]{:S(2)}) collective-permute-start(bf16[512,640]{1,0:T(8,128)(2,1)S(1)} %slice_bitcast_fusion), channel_id=1, source_target_pairs={{8,40},{16,48},{24,56},{40,72},{48,80},{56,88},{72,104},{80,112},{... | collective-permute-start | bytes 1966088 | tf_op jit(solution)/shard_map/ppermute | solution.py:39
  18.3 4.8 %shard_map.77 = f32[8,512]{1,0:T(8,128)} custom-call(f32[2]{0:T(128)} %pad_maximum_fusion.shares, bf16[3,512,640]{2,1,0:T(8,128)(2,1)} %clean.13, bf16[3,512,640]{2,1,0:T(8,128)(2,1)} %noise.13), custom_call_target="tpu_custom_call" | custom-call | flops 3932160 | bytes 2621440 | tf_op jit(solution)/shard_map/pallas_call | solution.py:86
  23.1 1.4 collective-permute-done
  24.5 0.7 add.176
  25.2 1.0 collective-permute-start.1
  26.2 20.3 %collective-permute-done.1 = f32[8,512]{1,0:T(8,128)S(1)} collective-permute-done((f32[8,512]{1,0:T(8,128)S(1)}, f32[8,512]{1,0:T(8,128)S(1)}, u32[]{:S(2)}, u32[]{:S(2)}) %collective-permute-start.1) | collective-permute-done | bytes 16416 | tf_op jit(solution)/shard_map/ppermute | solution.py:344
  46.6 4.6 %collective-permute-done.2 = f32[8,512]{1,0:T(8,128)S(1)} collective-permute-done((f32[8,512]{1,0:T(8,128)S(1)}, f32[8,512]{1,0:T(8,128)S(1)}, u32[]{:S(2)}, u32[]{:S(2)}) %collective-permute-start.2) | collective-permute-done | bytes 16416 | tf_op jit(solution)/shard_map/ppermute | solution.py:344
  51.2 1.3 fusion.1
  54.4 1.9 collective-permute-start.10
  56.3 1.2 collective-permute-start.9
  57.5 14.7 %collective-permute-done.10 = bf16[512,256]{1,0:T(8,128)(2,1)S(1)} collective-permute-done((bf16[512,256]{1,0:T(8,128)(2,1)S(1)}, bf16[512,256]{1,0:T(8,128)(2,1)S(1)}, u32[]{:S(2)}, u32[]{:S(2)}) %collective-permute-start.10) | collective-permute-done | bytes 262176 | tf_op jit(solution)/shard_map/ppermute | solution.py:39
  72.2 1.9 collective-permute-start.11
  74.8 1.3 collective-permute-start.16
  76.2 11.6 %collective-permute-start.17 = (bf16[512,256]{1,0:T(8,128)(2,1)S(1)}, bf16[512,256]{1,0:T(8,128)(2,1)S(1)}, u32[]{:S(2)}, u32[]{:S(2)}) collective-permute-start(bf16[512,256]{1,0:T(8,128)(2,1)S(1)} %collective-permute-done.10), channel_id=1, source_target_pairs={{8,0},{16,8},{24,16},{40,32},{48,40},{56,48},{72,64},{80,72},{88,8... | collective-permute-start | bytes 786440 | tf_op jit(solution)/shard_map/ppermute | solution.py:51
  89.0 3.7 %collective-permute-done.11 = bf16[512,384]{1,0:T(8,128)(2,1)} collective-permute-done((bf16[512,384]{1,0:T(8,128)(2,1)S(1)}, bf16[512,384]{1,0:T(8,128)(2,1)}, u32[]{:S(2)}, u32[]{:S(2)}) %collective-permute-start.11) | collective-permute-done | bytes 393248 | tf_op jit(solution)/shard_map/ppermute | solution.py:39
  93.4 1.3 collective-permute-start.13
  94.7 5.7 %collective-permute-start.14 = (bf16[512,384]{1,0:T(8,128)(2,1)}, bf16[512,384]{1,0:T(8,128)(2,1)}, u32[]{:S(2)}, u32[]{:S(2)}) collective-permute-start(bf16[512,384]{1,0:T(8,128)(2,1)} %collective-permute-done.11), channel_id=1, source_target_pairs={{8,0},{16,8},{24,16},{40,32},{48,40},{56,48},{72,64},{80,72},{88,8... | collective-permute-start | bytes 1179656 | tf_op jit(solution)/shard_map/ppermute | solution.py:51
  101.7 0.7 copy-done.30
  102.4 11.9 %shard_map.78 = (bf16[512,640]{1,0:T(8,128)(2,1)}, f32[512,640]{1,0:T(8,128)}, f32[512,640]{1,0:T(8,128)}, f32[512,640]{1,0:T(8,128)}, bf16[2,512,256]{2,1,0:T(8...) custom-call(s32[9]{0:T(128)} %add_convert_fusion.3.flags, ...), custom_call_target="tpu_custom_call" | custom-call | flops 3221225472 | bytes 8388608 | tf_op jit(solution)/shard_map/pallas_call | solution.py:237
  114.4 2.1 collective-permute-start.19
  116.5 0.7 copy-done.12
  117.2 2.4 collective-permute-start.20
  119.6 11.9 %shard_map.79 = (bf16[512,640]{1,0:T(8,128)(2,1)}, f32[512,640]{1,0:T(8,128)}, f32[512,640]{1,0:T(8,128)}, f32[512,640]{1,0:T(8,128)}, bf16[2,528,256]{2,1,0:T(8...) custom-call(s32[9]{0:T(128)} %add_convert_fusion.3.flags, ...), custom_call_target="tpu_custom_call", output_to_operand_aliasing={{0}: (17, {}), {1}: (18, {}), {2}: (19, {}), {3}: (20, {})} | custom-call | flops 3221225472 | bytes 8388608 | tf_op jit(solution)/shard_map/pallas_call | solution.py:237
  131.6 6.9 %shard_map.80 = (bf16[512,640]{1,0:T(8,128)(2,1)}, f32[512,640]{1,0:T(8,128)}, f32[512,640]{1,0:T(8,128)}, f32[512,640]{1,0:T(8,128)}, bf16[2,512,128]{2,1,0:T(8...) custom-call(s32[9]{0:T(128)} %add_convert_fusion.3.flags, ...), custom_call_target="tpu_custom_call", output_to_operand_aliasing={{0}: (17, {}), {1}: (18, {}), {2}: (19, {}), {3}: (20, {})} | custom-call | flops 1610612736 | bytes 4194304 | tf_op jit(solution)/shard_map/pallas_call | solution.py:237
  138.5 0.7 add_add_fusion
  139.3 1.8 collective-permute-done.20.in_3
  141.1 1.2 collective-permute-done.21
  142.5 3.5 %collective-permute-done.22 = f32[8,512]{1,0:T(8,128)S(1)} collective-permute-done((f32[8,512]{1,0:T(8,128)S(1)}, f32[8,512]{1,0:T(8,128)S(1)}, u32[]{:S(2)}, u32[]{:S(2)}) %collective-permute-start.22) | collective-permute-done | bytes 16416 | tf_op jit(solution)/shard_map/ppermute | solution.py:344
  146.1 4.6 %collective-permute-done.23 = f32[8,512]{1,0:T(8,128)S(1)} collective-permute-done((f32[8,512]{1,0:T(8,128)S(1)}, f32[8,512]{1,0:T(8,128)S(1)}, u32[]{:S(2)}, u32[]{:S(2)}) %collective-permute-start.23) | collective-permute-done | bytes 16416 | tf_op jit(solution)/shard_map/ppermute | solution.py:344
  152.1 1.7 collective-permute-start.25
  153.8 2.6 %collective-permute-start.24 = (bf16[2,528,256]{2,1,0:T(8,128)(2,1)}, bf16[2,528,256]{2,1,0:T(8,128)(2,1)S(1)}, u32[]{:S(2)}, u32[]{:S(2)}) collective-permute-start(bf16[2,528,256]{2,1,0:T(8,128)(2,1)} %get-tuple-element.60), channel_id=1, source_target_pairs={{0,24},{8,0},{16,8},{24,16},{32,56},{40,32},{48,40},{56,48},{64,88... | collective-permute-start | bytes 1622024 | tf_op jit(solution)/shard_map/ppermute | solution.py:51
  156.7 6.2 %collective-permute-start.28 = (bf16[2,512,256]{2,1,0:T(8,128)(2,1)S(1)}, bf16[2,512,256]{2,1,0:T(8,128)(2,1)S(1)}, u32[]{:S(2)}, u32[]{:S(2)}) collective-permute-start(bf16[2,512,256]{2,1,0:T(8,128)(2,1)S(1)} %add_convert_fusion.1), channel_id=1, source_target_pairs={{40,8},{48,16},{56,24},{72,40},{80,48},{88,56},{104,72},{112,80},{... | collective-permute-start | bytes 1572872 | tf_op jit(solution)/shard_map/ppermute | solution.py:39
  162.9 22.1 %collective-permute-done.28.crossed = bf16[2,512,256]{2,1,0:T(8,128)(2,1)S(1)} collective-permute-done((bf16[2,512,256]{2,1,0:T(8,128)(2,1)S(1)}, bf16[2,512,256]{2,1,0:T(8,128)(2,1)S(1)}, u32[]{:S(2)}, u32[]{:S(2)}) %collective-permute-start.28) | collective-permute-done | bytes 524320 | tf_op jit(solution)/shard_map/ppermute | solution.py:39
  185.1 1.1 collective-permute-start.30
  186.3 1.0 collective-permute-start.31
  187.6 6.6 %collective-permute-start.27 = (bf16[2,528,256]{2,1,0:T(8,128)(2,1)S(1)}, bf16[2,528,256]{2,1,0:T(8,128)(2,1)S(1)}, u32[]{:S(2)}, u32[]{:S(2)}) collective-permute-start(bf16[2,528,256]{2,1,0:T(8,128)(2,1)S(1)} %add_convert_fusion), channel_id=1, source_target_pairs={{40,8},{48,16},{56,24},{72,40},{80,48},{88,56},{104,72},{112,80},{... | collective-permute-start | bytes 1622024 | tf_op jit(solution)/shard_map/ppermute | solution.py:39
  194.2 3.3 %collective-permute-done.29.in_1 = bf16[2,512,128]{2,1,0:T(8,128)(2,1)S(1)} collective-permute-done((bf16[2,512,128]{2,1,0:T(8,128)(2,1)S(1)}, bf16[2,512,128]{2,1,0:T(8,128)(2,1)S(1)}, u32[]{:S(2)}, u32[]{:S(2)}) %collective-permute-start.29) | collective-permute-done | bytes 262176 | tf_op jit(solution)/shard_map/ppermute | solution.py:51
  197.5 1.8 collective-permute-done.31.in_3
  199.5 5.9 %collective-permute-start.32 = (bf16[2,512,128]{2,1,0:T(8,128)(2,1)S(1)}, bf16[2,512,128]{2,1,0:T(8,128)(2,1)S(1)}, u32[]{:S(2)}, u32[]{:S(2)}) collective-permute-start(bf16[2,512,128]{2,1,0:T(8,128)(2,1)S(1)} %add_convert_fusion.2), channel_id=1, source_target_pairs={{40,8},{48,16},{56,24},{72,40},{80,48},{88,56},{104,72},{112,80},{... | collective-permute-start | bytes 786440 | tf_op jit(solution)/shard_map/ppermute | solution.py:39
  205.5 16.5 %collective-permute-done.27.crossed = bf16[2,528,256]{2,1,0:T(8,128)(2,1)S(1)} collective-permute-done((bf16[2,528,256]{2,1,0:T(8,128)(2,1)S(1)}, bf16[2,528,256]{2,1,0:T(8,128)(2,1)S(1)}, u32[]{:S(2)}, u32[]{:S(2)}) %collective-permute-start.27) | collective-permute-done | bytes 540704 | tf_op jit(solution)/shard_map/ppermute | solution.py:39
  222.0 0.8 copy-done.16
  223.5 4.2 %shard_map.81.refs_0_ = f32[3,512,640]{2,1,0:T(8,128)} custom-call(s32[9]{0:T(128)} %add_convert_fusion.3.flags, f32[2]{0:T(128)} %pad_maximum_fusion.shares, f32[8,512]{1,0:T(8,128)} %concatenate.12.rows_ref, f32[1,640]{1,0:T(1,128)} %broadcast_in_dim.31.gain_q, f32[1,640]{1,0:T(1,128)} %broadcast_in_dim.32.gain_k, bf16[3,512,640]{2,1,0:T(8,128)(2,1)} %clean.13, ...), custom_call_target="tpu_custom_call" | custom-call | flops 3932160 | bytes 6291456 | tf_op jit(solution)/shard_map/pallas_call | solution.py:320
  227.6 4.0 %shard_map.82.refs_0_ = f32[3,512,640]{2,1,0:T(8,128)} custom-call(s32[9]{0:T(128)} %add_convert_fusion.3.flags, f32[2]{0:T(128)} %pad_maximum_fusion.shares, f32[8,512]{1,0:T(8,128)} %concatenate.12.rows_ref, f32[1,640]{1,0:T(1,128)} %broadcast_in_dim.31.gain_q, f32[1,640]{1,0:T(1,128)} %broadcast_in_dim.32.gain_k, ...), custom_call_target="tpu_custom_call", output_to_operand_aliasing={{}: (14, {})} | custom-call | flops 3932160 | bytes 6291456 | tf_op jit(solution)/shard_map/pallas_call | solution.py:320
  232.3 3.2 %shard_map.83 = f32[3,512,640]{2,1,0:T(8,128)} custom-call(s32[9]{0:T(128)} %add_convert_fusion.3.flags, f32[2]{0:T(128)} %pad_maximum_fusion.shares, f32[8,512]{1,0:T(8,128)} %concatenate.12.rows_ref, f32[1,640]{1,0:T(1,128)} %broadcast_in_dim.31.gain_q, f32[1,640]{1,0:T(1,128)} %broadcast_in_dim.32.gain_k, ...), custom_call_target="tpu_custom_call", output_to_operand_aliasing={{}: (14, {})} | custom-call | flops 1966080 | bytes 3145728 | tf_op jit(solution)/shard_map/pallas_call | solution.py:320
  (124 shorter events, 10.3 us)
Async XLA Ops:
  1.8 50.8 %collective-permute-start.3 = (bf16[512,640]{1,0:T(8,128)(2,1)S(1)}, bf16[512,640]{1,0:T(8,128)(2,1)S(1)}, u32[]{:S(2)}, u32[]{:S(2)}) collective-permute-start(bf16[512,640]{1,0:T(8,128)(2,1)S(1)} %slice_bitcast_fusion), channel_id=1, source_target_pairs={{0,8},{8,16},{16,24},{32,40},{40,48},{48,56},{64,72},{72,80},{80,8... | collective-permute-start | bytes 1966088 | tf_op jit(solution)/shard_map/ppermute | solution.py:51
  5.2 47.4 %collective-permute-start.4 = (bf16[512,640]{1,0:T(8,128)(2,1)S(1)}, bf16[512,640]{1,0:T(8,128)(2,1)S(1)}, u32[]{:S(2)}, u32[]{:S(2)}) collective-permute-start(bf16[512,640]{1,0:T(8,128)(2,1)S(1)} %slice_bitcast_fusion), channel_id=1, source_target_pairs={{0,16},{8,24},{32,48},{40,56},{64,80},{72,88},{96,112},{104,120},{... | collective-permute-start | bytes 1966088 | tf_op jit(solution)/shard_map/ppermute | solution.py:51
  7.2 45.4 %collective-permute-start.5 = (bf16[512,640]{1,0:T(8,128)(2,1)S(1)}, bf16[512,640]{1,0:T(8,128)(2,1)S(1)}, u32[]{:S(2)}, u32[]{:S(2)}) collective-permute-start(bf16[512,640]{1,0:T(8,128)(2,1)S(1)} %slice_bitcast_fusion), channel_id=1, source_target_pairs={{0,24},{32,56},{64,88},{96,120},{128,152},{160,184},{192,216},{224... | collective-permute-start | bytes 1966088 | tf_op jit(solution)/shard_map/ppermute | solution.py:51
  7.9 44.7 %collective-permute-start.6 = (bf16[512,640]{1,0:T(8,128)(2,1)S(1)}, bf16[512,640]{1,0:T(8,128)(2,1)S(1)}, u32[]{:S(2)}, u32[]{:S(2)}) collective-permute-start(bf16[512,640]{1,0:T(8,128)(2,1)S(1)} %slice_bitcast_fusion), channel_id=1, source_target_pairs={{8,40},{16,48},{24,56},{40,72},{48,80},{56,88},{72,104},{80,112},{... | collective-permute-start | bytes 1966088 | tf_op jit(solution)/shard_map/ppermute | solution.py:39
  18.3 32.9 %copy-start.21 = (f32[640]{0:T(1024)S(1)}, f32[640]{0:T(1024)}, u32[]{:S(2)}) copy-start(f32[640]{0:T(1024)} %param.10) | copy-start | bytes 7684
  23.1 1.4 collective-permute-start
  25.2 21.3 %collective-permute-start.1 = (f32[8,512]{1,0:T(8,128)S(1)}, f32[8,512]{1,0:T(8,128)S(1)}, u32[]{:S(2)}, u32[]{:S(2)}) collective-permute-start(f32[8,512]{1,0:T(8,128)S(1)} %add.176), channel_id=1, source_target_pairs={{0,2},{1,3},{2,0},{3,1},{4,6},{5,7},{6,4},{7,5},{8,10},{9,11},{10,... | collective-permute-start | bytes 49160 | tf_op jit(solution)/shard_map/ppermute | solution.py:344
  46.5 4.6 %collective-permute-start.2 = (f32[8,512]{1,0:T(8,128)S(1)}, f32[8,512]{1,0:T(8,128)S(1)}, u32[]{:S(2)}, u32[]{:S(2)}) collective-permute-start(f32[8,512]{1,0:T(8,128)S(1)} %add.177), channel_id=1, source_target_pairs={{0,4},{1,5},{2,6},{3,7},{4,0},{5,1},{6,2},{7,3},{8,12},{9,13},{10,... | collective-permute-start | bytes 49160 | tf_op jit(solution)/shard_map/ppermute | solution.py:344
  53.8 34.6 %copy-start.24 = (f32[640]{0:T(1024)S(1)}, f32[640]{0:T(1024)}, u32[]{:S(2)}) copy-start(f32[640]{0:T(1024)} %param.9) | copy-start | bytes 7684
  53.8 21.0 %collective-permute-start.7 = (bf16[512,640]{1,0:T(8,128)(2,1)S(1)}, bf16[512,640]{1,0:T(8,128)(2,1)S(1)}, u32[]{:S(2)}, u32[]{:S(2)}) collective-permute-start(bf16[512,640]{1,0:T(8,128)(2,1)S(1)} %get-tuple-element.74), channel_id=1, source_target_pairs={{0,8},{8,16},{16,24},{24,0},{32,40},{40,48},{48,56},{56,32},{64,72... | collective-permute-start | bytes 1966088 | tf_op jit(solution)/shard_map/ppermute | solution.py:51
  54.4 21.8 %collective-permute-start.8 = (bf16[512,640]{1,0:T(8,128)(2,1)S(1)}, bf16[512,640]{1,0:T(8,128)(2,1)S(1)}, u32[]{:S(2)}, u32[]{:S(2)}) collective-permute-start(bf16[512,640]{1,0:T(8,128)(2,1)S(1)} %get-tuple-element.73), channel_id=1, source_target_pairs={{0,16},{8,24},{16,0},{24,8},{32,48},{40,56},{48,32},{56,40},{64,80... | collective-permute-start | bytes 1966088 | tf_op jit(solution)/shard_map/ppermute | solution.py:51
  54.4 17.8 %collective-permute-start.10 = (bf16[512,256]{1,0:T(8,128)(2,1)S(1)}, bf16[512,256]{1,0:T(8,128)(2,1)S(1)}, u32[]{:S(2)}, u32[]{:S(2)}) collective-permute-start(bf16[512,256]{1,0:T(8,128)(2,1)S(1)} %slice.110), channel_id=1, source_target_pairs={{8,40},{16,48},{24,56},{40,72},{48,80},{56,88},{72,104},{80,112},{... | collective-permute-start | bytes 786440 | tf_op jit(solution)/shard_map/ppermute | solution.py:39
  56.3 32.7 %collective-permute-start.9 = (bf16[512,640]{1,0:T(8,128)(2,1)S(1)}, bf16[512,640]{1,0:T(8,128)(2,1)S(1)}, u32[]{:S(2)}, u32[]{:S(2)}) collective-permute-start(bf16[512,640]{1,0:T(8,128)(2,1)S(1)} %get-tuple-element.72), channel_id=1, source_target_pairs={{0,24},{8,0},{16,8},{24,16},{32,56},{40,32},{48,40},{56,48},{64,88... | collective-permute-start | bytes 1966088 | tf_op jit(solution)/shard_map/ppermute | solution.py:51
  72.2 20.5 %collective-permute-start.11 = (bf16[512,384]{1,0:T(8,128)(2,1)S(1)}, bf16[512,384]{1,0:T(8,128)(2,1)}, u32[]{:S(2)}, u32[]{:S(2)}) collective-permute-start(bf16[512,384]{1,0:T(8,128)(2,1)S(1)} %slice.109), channel_id=1, source_target_pairs={{8,40},{16,48},{24,56},{40,72},{48,80},{56,88},{72,104},{80,112},{... | collective-permute-start | bytes 1179656 | tf_op jit(solution)/shard_map/ppermute | solution.py:39
  74.1 20.6 %collective-permute-start.15 = (bf16[512,256]{1,0:T(8,128)(2,1)S(1)}, bf16[512,256]{1,0:T(8,128)(2,1)S(1)}, u32[]{:S(2)}, u32[]{:S(2)}) collective-permute-start(bf16[512,256]{1,0:T(8,128)(2,1)S(1)} %collective-permute-done.10), channel_id=1, source_target_pairs={{24,0},{56,32},{88,64},{120,96},{152,128},{184,160},{216,192},{248... | collective-permute-start | bytes 786440 | tf_op jit(solution)/shard_map/ppermute | solution.py:51
  74.8 26.2 %copy-start.3 = (bf16[512,640]{1,0:T(8,128)(2,1)}, bf16[512,640]{1,0:T(8,128)(2,1)S(1)}, u32[]{:S(2)}) copy-start(bf16[512,640]{1,0:T(8,128)(2,1)S(1)} %collective-permute-done.7.both_1) | copy-start | bytes 1966084
  74.8 26.1 %collective-permute-start.16 = (bf16[512,256]{1,0:T(8,128)(2,1)S(1)}, bf16[512,256]{1,0:T(8,128)(2,1)S(1)}, u32[]{:S(2)}, u32[]{:S(2)}) collective-permute-start(bf16[512,256]{1,0:T(8,128)(2,1)S(1)} %collective-permute-done.10), channel_id=1, source_target_pairs={{16,0},{24,8},{48,32},{56,40},{80,64},{88,72},{112,96},{120,104},{... | collective-permute-start | bytes 786440 | tf_op jit(solution)/shard_map/ppermute | solution.py:51
  76.1 24.9 %copy-start.4 = (bf16[512,640]{1,0:T(8,128)(2,1)}, bf16[512,640]{1,0:T(8,128)(2,1)S(1)}, u32[]{:S(2)}) copy-start(bf16[512,640]{1,0:T(8,128)(2,1)S(1)} %collective-permute-done.8.both_2) | copy-start | bytes 1966084
  76.2 24.8 %collective-permute-start.17 = (bf16[512,256]{1,0:T(8,128)(2,1)S(1)}, bf16[512,256]{1,0:T(8,128)(2,1)S(1)}, u32[]{:S(2)}, u32[]{:S(2)}) collective-permute-start(bf16[512,256]{1,0:T(8,128)(2,1)S(1)} %collective-permute-done.10), channel_id=1, source_target_pairs={{8,0},{16,8},{24,16},{40,32},{48,40},{56,48},{72,64},{80,72},{88,8... | collective-permute-start | bytes 786440 | tf_op jit(solution)/shard_map/ppermute | solution.py:51
  92.7 23.8 %collective-permute-start.12 = (bf16[512,384]{1,0:T(8,128)(2,1)}, bf16[512,384]{1,0:T(8,128)(2,1)S(1)}, u32[]{:S(2)}, u32[]{:S(2)}) collective-permute-start(bf16[512,384]{1,0:T(8,128)(2,1)} %collective-permute-done.11), channel_id=1, source_target_pairs={{24,0},{56,32},{88,64},{120,96},{152,128},{184,160},{216,192},{248... | collective-permute-start | bytes 1179656 | tf_op jit(solution)/shard_map/ppermute | solution.py:51
  93.4 26.2 %collective-permute-start.13 = (bf16[512,384]{1,0:T(8,128)(2,1)}, bf16[512,384]{1,0:T(8,128)(2,1)}, u32[]{:S(2)}, u32[]{:S(2)}) collective-permute-start(bf16[512,384]{1,0:T(8,128)(2,1)} %collective-permute-done.11), channel_id=1, source_target_pairs={{16,0},{24,8},{48,32},{56,40},{80,64},{88,72},{112,96},{120,104},{... | collective-permute-start | bytes 1179656 | tf_op jit(solution)/shard_map/ppermute | solution.py:51
  94.7 24.9 %collective-permute-start.14 = (bf16[512,384]{1,0:T(8,128)(2,1)}, bf16[512,384]{1,0:T(8,128)(2,1)}, u32[]{:S(2)}, u32[]{:S(2)}) collective-permute-start(bf16[512,384]{1,0:T(8,128)(2,1)} %collective-permute-done.11), channel_id=1, source_target_pairs={{8,0},{16,8},{24,16},{40,32},{48,40},{56,48},{72,64},{80,72},{88,8... | collective-permute-start | bytes 1179656 | tf_op jit(solution)/shard_map/ppermute | solution.py:51
  114.3 25.0 %collective-permute-start.18 = (bf16[2,512,256]{2,1,0:T(8,128)(2,1)}, bf16[2,512,256]{2,1,0:T(8,128)(2,1)S(1)}, u32[]{:S(2)}, u32[]{:S(2)}) collective-permute-start(bf16[2,512,256]{2,1,0:T(8,128)(2,1)} %get-tuple-element.53), channel_id=1, source_target_pairs={{0,24},{8,0},{16,8},{24,16},{32,56},{40,32},{48,40},{56,48},{64,88... | collective-permute-start | bytes 1572872 | tf_op jit(solution)/shard_map/ppermute | solution.py:51
  114.4 24.9 %collective-permute-start.19 = (bf16[2,512,256]{2,1,0:T(8,128)(2,1)}, bf16[2,512,256]{2,1,0:T(8,128)(2,1)S(1)}, u32[]{:S(2)}, u32[]{:S(2)}) collective-permute-start(bf16[2,512,256]{2,1,0:T(8,128)(2,1)} %get-tuple-element.54), channel_id=1, source_target_pairs={{0,16},{8,24},{16,0},{24,8},{32,48},{40,56},{48,32},{56,40},{64,80... | collective-permute-start | bytes 1572872 | tf_op jit(solution)/shard_map/ppermute | solution.py:51
  117.2 23.9 %collective-permute-start.20 = (bf16[2,512,256]{2,1,0:T(8,128)(2,1)}, bf16[2,512,256]{2,1,0:T(8,128)(2,1)S(1)}, u32[]{:S(2)}, u32[]{:S(2)}) collective-permute-start(bf16[2,512,256]{2,1,0:T(8,128)(2,1)} %get-tuple-element.55), channel_id=1, source_target_pairs={{0,8},{8,16},{16,24},{24,0},{32,40},{40,48},{48,56},{56,32},{64,72... | collective-permute-start | bytes 1572872 | tf_op jit(solution)/shard_map/ppermute | solution.py:51
  139.3 48.3 %copy-start.9 = (bf16[2,512,256]{2,1,0:T(8,128)(2,1)}, bf16[2,512,256]{2,1,0:T(8,128)(2,1)S(1)}, u32[]{:S(2)}) copy-start(bf16[2,512,256]{2,1,0:T(8,128)(2,1)S(1)} %collective-permute-done.18.in_1) | copy-start | bytes 1572868
  139.3 48.3 %copy-start.10 = (bf16[2,512,256]{2,1,0:T(8,128)(2,1)}, bf16[2,512,256]{2,1,0:T(8,128)(2,1)S(1)}, u32[]{:S(2)}) copy-start(bf16[2,512,256]{2,1,0:T(8,128)(2,1)S(1)} %collective-permute-done.19.in_2) | copy-start | bytes 1572868
  141.1 46.4 %copy-start.11 = (bf16[2,512,256]{2,1,0:T(8,128)(2,1)}, bf16[2,512,256]{2,1,0:T(8,128)(2,1)S(1)}, u32[]{:S(2)}) copy-start(bf16[2,512,256]{2,1,0:T(8,128)(2,1)S(1)} %collective-permute-done.20.in_3) | copy-start | bytes 1572868
  141.1 1.2 collective-permute-start.21
  142.3 3.7 %collective-permute-start.22 = (f32[8,512]{1,0:T(8,128)S(1)}, f32[8,512]{1,0:T(8,128)S(1)}, u32[]{:S(2)}, u32[]{:S(2)}) collective-permute-start(f32[8,512]{1,0:T(8,128)S(1)} %add.186), channel_id=1, source_target_pairs={{0,2},{1,3},{2,0},{3,1},{4,6},{5,7},{6,4},{7,5},{8,10},{9,11},{10,... | collective-permute-start | bytes 49160 | tf_op jit(solution)/shard_map/ppermute | solution.py:344
  146.1 4.6 %collective-permute-start.23 = (f32[8,512]{1,0:T(8,128)S(1)}, f32[8,512]{1,0:T(8,128)S(1)}, u32[]{:S(2)}, u32[]{:S(2)}) collective-permute-start(f32[8,512]{1,0:T(8,128)S(1)} %add.187), channel_id=1, source_target_pairs={{0,4},{1,5},{2,6},{3,7},{4,0},{5,1},{6,2},{7,3},{8,12},{9,13},{10,... | collective-permute-start | bytes 49160 | tf_op jit(solution)/shard_map/ppermute | solution.py:344
  150.8 34.2 %copy-start.27 = (bf16[2,512,128]{2,1,0:T(8,128)(2,1)S(1)}, bf16[2,512,128]{2,1,0:T(8,128)(2,1)}, u32[]{:S(2)}) copy-start(bf16[2,512,128]{2,1,0:T(8,128)(2,1)} %get-tuple-element.69) | copy-start | bytes 786436
  150.8 34.3 %copy-start.26 = (bf16[2,512,128]{2,1,0:T(8,128)(2,1)S(1)}, bf16[2,512,128]{2,1,0:T(8,128)(2,1)}, u32[]{:S(2)}) copy-start(bf16[2,512,128]{2,1,0:T(8,128)(2,1)} %get-tuple-element.70) | copy-start | bytes 786436
  150.8 35.5 %copy-start.25 = (bf16[2,512,128]{2,1,0:T(8,128)(2,1)S(1)}, bf16[2,512,128]{2,1,0:T(8,128)(2,1)}, u32[]{:S(2)}) copy-start(bf16[2,512,128]{2,1,0:T(8,128)(2,1)} %get-tuple-element.71) | copy-start | bytes 786436
  151.4 34.8 %collective-permute-start.26 = (bf16[2,528,256]{2,1,0:T(8,128)(2,1)}, bf16[2,528,256]{2,1,0:T(8,128)(2,1)S(1)}, u32[]{:S(2)}, u32[]{:S(2)}) collective-permute-start(bf16[2,528,256]{2,1,0:T(8,128)(2,1)} %get-tuple-element.62), channel_id=1, source_target_pairs={{0,8},{8,16},{16,24},{24,0},{32,40},{40,48},{48,56},{56,32},{64,72... | collective-permute-start | bytes 1622024 | tf_op jit(solution)/shard_map/ppermute | solution.py:51
  152.1 35.1 %collective-permute-start.25 = (bf16[2,528,256]{2,1,0:T(8,128)(2,1)}, bf16[2,528,256]{2,1,0:T(8,128)(2,1)S(1)}, u32[]{:S(2)}, u32[]{:S(2)}) collective-permute-start(bf16[2,528,256]{2,1,0:T(8,128)(2,1)} %get-tuple-element.61), channel_id=1, source_target_pairs={{0,16},{8,24},{16,0},{24,8},{32,48},{40,56},{48,32},{56,40},{64,80... | collective-permute-start | bytes 1622024 | tf_op jit(solution)/shard_map/ppermute | solution.py:51
  153.8 33.5 %collective-permute-start.24 = (bf16[2,528,256]{2,1,0:T(8,128)(2,1)}, bf16[2,528,256]{2,1,0:T(8,128)(2,1)S(1)}, u32[]{:S(2)}, u32[]{:S(2)}) collective-permute-start(bf16[2,528,256]{2,1,0:T(8,128)(2,1)} %get-tuple-element.60), channel_id=1, source_target_pairs={{0,24},{8,0},{16,8},{24,16},{32,56},{40,32},{48,40},{56,48},{64,88... | collective-permute-start | bytes 1622024 | tf_op jit(solution)/shard_map/ppermute | solution.py:51
  156.7 28.3 %collective-permute-start.28 = (bf16[2,512,256]{2,1,0:T(8,128)(2,1)S(1)}, bf16[2,512,256]{2,1,0:T(8,128)(2,1)S(1)}, u32[]{:S(2)}, u32[]{:S(2)}) collective-permute-start(bf16[2,512,256]{2,1,0:T(8,128)(2,1)S(1)} %add_convert_fusion.1), channel_id=1, source_target_pairs={{40,8},{48,16},{56,24},{72,40},{80,48},{88,56},{104,72},{112,80},{... | collective-permute-start | bytes 1572872 | tf_op jit(solution)/shard_map/ppermute | solution.py:39
  185.0 37.8 %copy-start.20 = (f32[8,512]{1,0:T(8,128)S(1)}, f32[8,512]{1,0:T(8,128)}, u32[]{:S(2)}) copy-start(f32[8,512]{1,0:T(8,128)} %copy-done.19) | copy-start | bytes 49156
  185.0 37.8 %slice-start = ((f32[8,512]{1,0:T(8,128)}), f32[3,512]{1,0:T(4,128)S(1)}, s32[]{:S(2)}) async-start(f32[8,512]{1,0:T(8,128)} %copy-done.19), calls=%async_computation | async-start | bytes 16384 | tf_op jit(solution)/shard_map/slice | solution.py:442
  185.0 12.5 %collective-permute-start.29 = (bf16[2,512,128]{2,1,0:T(8,128)(2,1)S(1)}, bf16[2,512,128]{2,1,0:T(8,128)(2,1)S(1)}, u32[]{:S(2)}, u32[]{:S(2)}) collective-permute-start(bf16[2,512,128]{2,1,0:T(8,128)(2,1)S(1)} %copy-done.27), channel_id=1, source_target_pairs={{0,24},{8,0},{16,8},{24,16},{32,56},{40,32},{48,40},{56,48},{64,88... | collective-permute-start | bytes 786440 | tf_op jit(solution)/shard_map/ppermute | solution.py:51
  185.1 12.4 %collective-permute-start.30 = (bf16[2,512,128]{2,1,0:T(8,128)(2,1)S(1)}, bf16[2,512,128]{2,1,0:T(8,128)(2,1)S(1)}, u32[]{:S(2)}, u32[]{:S(2)}) collective-permute-start(bf16[2,512,128]{2,1,0:T(8,128)(2,1)S(1)} %copy-done.26), channel_id=1, source_target_pairs={{0,16},{8,24},{16,0},{24,8},{32,48},{40,56},{48,32},{56,40},{64,80... | collective-permute-start | bytes 786440 | tf_op jit(solution)/shard_map/ppermute | solution.py:51
  186.3 13.2 %copy-start.6 = (bf16[2,528,256]{2,1,0:T(8,128)(2,1)}, bf16[2,528,256]{2,1,0:T(8,128)(2,1)S(1)}, u32[]{:S(2)}) copy-start(bf16[2,528,256]{2,1,0:T(8,128)(2,1)S(1)} %collective-permute-done.26.in_3) | copy-start | bytes 1622020
  186.3 13.1 %collective-permute-start.31 = (bf16[2,512,128]{2,1,0:T(8,128)(2,1)S(1)}, bf16[2,512,128]{2,1,0:T(8,128)(2,1)S(1)}, u32[]{:S(2)}, u32[]{:S(2)}) collective-permute-start(bf16[2,512,128]{2,1,0:T(8,128)(2,1)S(1)} %copy-done.25), channel_id=1, source_target_pairs={{0,8},{8,16},{16,24},{24,0},{32,40},{40,48},{48,56},{56,32},{64,72... | collective-permute-start | bytes 786440 | tf_op jit(solution)/shard_map/ppermute | solution.py:51
  187.6 34.4 %collective-permute-start.27 = (bf16[2,528,256]{2,1,0:T(8,128)(2,1)S(1)}, bf16[2,528,256]{2,1,0:T(8,128)(2,1)S(1)}, u32[]{:S(2)}, u32[]{:S(2)}) collective-permute-start(bf16[2,528,256]{2,1,0:T(8,128)(2,1)S(1)} %add_convert_fusion), channel_id=1, source_target_pairs={{40,8},{48,16},{56,24},{72,40},{80,48},{88,56},{104,72},{112,80},{... | collective-permute-start | bytes 1622024 | tf_op jit(solution)/shard_map/ppermute | solution.py:39
  197.5 30.1 %copy-start.13 = (bf16[2,512,128]{2,1,0:T(8,128)(2,1)}, bf16[2,512,128]{2,1,0:T(8,128)(2,1)S(1)}, u32[]{:S(2)}) copy-start(bf16[2,512,128]{2,1,0:T(8,128)(2,1)S(1)} %collective-permute-done.29.in_1) | copy-start | bytes 786436
  199.3 22.6 %copy-start.15 = (bf16[2,512,128]{2,1,0:T(8,128)(2,1)}, bf16[2,512,128]{2,1,0:T(8,128)(2,1)S(1)}, u32[]{:S(2)}) copy-start(bf16[2,512,128]{2,1,0:T(8,128)(2,1)S(1)} %collective-permute-done.31.in_3) | copy-start | bytes 786436
  199.5 32.1 %collective-permute-start.32 = (bf16[2,512,128]{2,1,0:T(8,128)(2,1)S(1)}, bf16[2,512,128]{2,1,0:T(8,128)(2,1)S(1)}, u32[]{:S(2)}, u32[]{:S(2)}) collective-permute-start(bf16[2,512,128]{2,1,0:T(8,128)(2,1)S(1)} %add_convert_fusion.2), channel_id=1, source_target_pairs={{40,8},{48,16},{56,24},{72,40},{80,48},{88,56},{104,72},{112,80},{... | collective-permute-start | bytes 786440 | tf_op jit(solution)/shard_map/ppermute | solution.py:39
  (17 other events, 75.4 us)
